TPU v7x, 512 devices: a whole 4x4x16 slice. The times are simulated.
512 devices in a mesh: grid: 64 (over z, y), scen: 8 (over x, core).
Axes of the slice: x: 4, y: 4, z: 16, core: 2. Of those that a mesh axis runs over, the one named last changes fastest.
Arguments:
- volt_init: float32 [2, 16384, 1024], P(None, 'grid', 'scen'), may hold values from 0.9 to 1.1
- line_dual: float32 [4, 16384, 1024], P(None, 'grid', 'scen'), may hold values from -1 to 1
- conductance: float32 [16384], P('grid'), may hold values from 0.2 to 2
- susceptance: float32 [16384], P('grid'), may hold values from -6 to -1
- endpoint_owner: int32 [32768, 1], P('grid'), may hold values from 0 to 63; in each aligned block of 512 rows (0 to 511, 512 to 1023, ...) at most 16 rows name the same one
- endpoint_bus: int32 [32768], P('grid'), may hold values from 0 to 255
- line_count: int32 [64], P('grid'), may hold values from 0 to 256, as said below
- bus_region: int32 [16384], P('grid'), may hold values from 0 to 15
- vm_set: float32 [16384], P('grid'), may hold values from 0.85 to 1.15
- stiffness: float32 [16384], P('grid'), may hold values from 0.2 to 2
- load: float32 [16384, 1024], P('grid', 'scen'), may hold values from -6 to 6
- price_init: float32 [16384, 1024], P('grid', 'scen'), may hold values from -3 to 3
- na_dual_init: float32 [16384, 1024], P('grid', 'scen'), may hold values from -2 to 2
- commit_init: float32 [16384], P('grid'), may hold values from 0 to 2
- cost_quad: float32 [16384], P('grid'), may hold values from 0.1 to 1
- cost_lin: float32 [16384], P('grid'), may hold values from -1 to 1
- pmax: float32 [16384], P('grid'), may hold values from 0.5 to 4
Outputs:
- volt: float32 [2, 16384, 1024], P(None, 'grid', 'scen')
- dual: float32 [4, 16384, 1024], P(None, 'grid', 'scen')
- dispatch: float32 [16384, 1024], P('grid', 'scen')
- price: float32 [16384, 1024], P('grid', 'scen')
- commit: float32 [16384], P('grid')
Inputs may be any that keep to these rules, and one draw needn't show every extreme that they name: `endpoint_owner`: in each aligned block of 512 rows (one device's line ends) no owner is named more than 16 times, a bound that some block reaches. `line_count`: device i and device i + 32 have 256 live lines or fewer together; some device has exactly 256; a device's live lines are its first slots.
All inputs are finite; a program needn't handle non-finite values.
Results may differ from a plain program's by a relative error of at most 0.0003.
Values sent between devices are 32-bit elements; how exact they have to be, the bound alone decides.
No kernel may reach another device: no remote copies, remote signals or barrier semaphores. Data moves between devices by JAX's collectives and lax.ppermute only.
A program may use at most 64 MiB of HBM per device.

v0:
```python
import jax
import jax.numpy as jnp
from jax import lax
from jax.sharding import PartitionSpec as P

NEWTON = 3
ITERS = 2
REGIONS = 16


penalty_line = 1.0
region_gain = 10.0


def cholesky_solve(hess, grad):
    lower = {}
    for row in range(4):
        for column in range(row + 1):
            total = hess[row][column]
            for inner in range(column):
                total = total - lower[row, inner] * lower[column, inner]
            if row == column:
                lower[row, row] = jnp.sqrt(total)
            else:
                lower[row, column] = total / lower[column, column]
    forward = []
    for row in range(4):
        total = grad[row]
        for inner in range(row):
            total = total - lower[row, inner] * forward[inner]
        forward.append(total / lower[row, row])
    answer = [None] * 4
    for row in range(3, -1, -1):
        total = forward[row]
        for inner in range(row + 1, 4):
            total = total - lower[inner, row] * answer[inner]
        answer[row] = total / lower[row, row]
    return answer


def branch_newton(center, cond, susc):
    state = list(center)
    for sweep in range(NEWTON):
        from_mag, from_ang, to_mag, to_ang = state
        cos_f = jnp.cos(from_ang)
        sin_f = jnp.sin(from_ang)
        cos_t = jnp.cos(to_ang)
        sin_t = jnp.sin(to_ang)
        real_gap = from_mag * cos_f - to_mag * cos_t
        imag_gap = from_mag * sin_f - to_mag * sin_t
        first = [cos_f, -from_mag * sin_f, -cos_t, to_mag * sin_t]
        second = [sin_f, from_mag * cos_f, -sin_t, -to_mag * cos_t]
        twice = 2.0 * cond
        grad = [
            twice * (first[row] * real_gap + second[row] * imag_gap)
            + penalty_line * (state[row] - center[row])
            for row in range(4)
        ]
        hess = [
            [
                twice * (first[row] * first[column] + second[row] * second[column])
                + (penalty_line if row == column else 0.0)
                for column in range(4)
            ]
            for row in range(4)
        ]
        update = cholesky_solve(hess, grad)
        state = [state[row] - update[row] for row in range(4)]
    from_mag, from_ang, to_mag, to_ang = state
    angle_gap = from_ang - to_ang
    product = from_mag * to_mag
    cos_d = jnp.cos(angle_gap)
    sin_d = jnp.sin(angle_gap)
    flow_from = cond * from_mag * from_mag - product * (cond * cos_d + susc * sin_d)
    flow_to = cond * to_mag * to_mag - product * (cond * cos_d - susc * sin_d)
    return (state, flow_from, flow_to)


def on_device(
    volt_init,
    line_dual,
    conductance,
    susceptance,
    endpoint_owner,
    endpoint_bus,
    line_count,
    bus_region,
    vm_set,
    stiffness,
    load,
    price_init,
    na_dual_init,
    commit_init,
    cost_quad,
    cost_lin,
    pmax,
):
    ngrid = lax.axis_size("grid")
    nscen = lax.axis_size("scen")
    lines = conductance.shape[0]
    ends_count = 2 * lines
    capacity = 2 * ends_count // ngrid
    buses = vm_set.shape[0]
    scen_dev = load.shape[1]
    owner = endpoint_owner[:, 0]
    owner_hits = (owner[:, None] == jnp.arange(ngrid, dtype=jnp.int32)[None, :]).astype(jnp.int32)
    earlier = jnp.cumsum(owner_hits, axis=0) - owner_hits
    rank = jnp.sum(earlier * owner_hits, axis=1)
    slot = owner * capacity + rank
    live = (jnp.arange(lines) < line_count[0]).astype(jnp.float32)
    live_int = live.astype(jnp.int32)
    request = jnp.zeros((ngrid * capacity,), jnp.int32).at[slot].set(endpoint_bus)
    request_live = (
        jnp.zeros((ngrid * capacity,), jnp.int32)
        .at[slot]
        .set(jnp.concatenate([live_int, live_int]))
    )
    asked, asked_live = (
        lax.all_to_all(request, "grid", split_axis=0, concat_axis=0, tiled=True),
        lax.all_to_all(request_live, "grid", split_axis=0, concat_axis=0, tiled=True),
    )
    degree = jnp.zeros((buses,), jnp.float32).at[asked].add(asked_live.astype(jnp.float32))
    cond = conductance[:, None]
    susc = susceptance[:, None]
    live_col = live[:, None]
    member = (bus_region[:, None] == jnp.arange(REGIONS, dtype=jnp.int32)[None, :]).astype(
        jnp.float32
    )
    volt = volt_init
    dual = line_dual
    previous = jnp.zeros_like(line_dual)
    price = price_init
    nadual = na_dual_init
    commit = commit_init
    dispatch = jnp.zeros_like(load)
    for turn in range(ITERS):
        looked = volt[:, asked, :]
        arrived = lax.all_to_all(looked, "grid", split_axis=1, concat_axis=1, tiled=True)
        at_ends = arrived[:, slot, :]
        near = jnp.stack(
            [at_ends[0, :lines], at_ends[1, :lines], at_ends[0, lines:], at_ends[1, lines:]]
        )
        if turn > 0:
            dual = jnp.where(live_col[None] > 0, dual + previous - near, dual)
        center = near - dual
        state, flow_from, flow_to = branch_newton([center[row] for row in range(4)], cond, susc)
        solved = jnp.stack(state)
        from_terms = jnp.stack(
            [
                live_col * (solved[0] + dual[0]),
                live_col * (solved[1] + dual[1]),
                live_col * flow_from,
            ]
        )
        to_terms = jnp.stack(
            [live_col * (solved[2] + dual[2]), live_col * (solved[3] + dual[3]), live_col * flow_to]
        )
        terms = jnp.concatenate([from_terms, to_terms], axis=1)
        outgoing = (
            jnp.zeros((3, ngrid * capacity, terms.shape[2]), jnp.float32).at[:, slot, :].set(terms)
        )
        previous, outgoing = (solved, outgoing)
        received = lax.all_to_all(outgoing, "grid", split_axis=1, concat_axis=1, tiled=True)
        summed = jnp.zeros((3, buses, received.shape[2]), jnp.float32).at[:, asked, :].add(received)
        weight = stiffness[:, None]
        target = jnp.stack([jnp.broadcast_to(vm_set[:, None], (buses, scen_dev)), volt[1]])
        volt = (penalty_line * summed[0:2] + weight * target) / (
            penalty_line * degree[:, None] + weight
        )
        net = summed[2]
        dispatch = (load + net - price - cost_lin[:, None] + (commit[:, None] - nadual)) / (
            2.0 * cost_quad[:, None] + 2.0
        )
        dispatch = jnp.clip(dispatch, 0.0, pmax[:, None])
        mismatch = dispatch - load - net
        regional_part = jnp.einsum("br,bs->rs", member, mismatch, precision=lax.Precision.HIGHEST)
        regional = lax.psum(regional_part, "grid")
        adder = jnp.dot(member, regional, precision=lax.Precision.HIGHEST) * (
            region_gain * REGIONS / (buses * ngrid)
        )
        scenario_total = lax.psum(jnp.sum(dispatch + nadual, axis=1), "scen")
        commit = scenario_total / (scen_dev * nscen)
        nadual = nadual + dispatch - commit[:, None]
        price = price + mismatch + adder
    return (volt, dual, dispatch, price, commit)


def solution(mesh):
    in_specs = (
        P(None, "grid", "scen"),
        P(None, "grid", "scen"),
        P("grid"),
        P("grid"),
        P("grid", None),
        P("grid"),
        P("grid"),
        P("grid"),
        P("grid"),
        P("grid"),
        P("grid", "scen"),
        P("grid", "scen"),
        P("grid", "scen"),
        P("grid"),
        P("grid"),
        P("grid"),
        P("grid"),
    )
    out_specs = (
        P(None, "grid", "scen"),
        P(None, "grid", "scen"),
        P("grid", "scen"),
        P("grid", "scen"),
        P("grid"),
    )
    return jax.shard_map(
        on_device, mesh=mesh, in_specs=in_specs, out_specs=out_specs, check_vma=False
    )
```

profile of v0, /device:TPU:6, one launch (start us, length us, event | category | flops | bytes accessed | tf_op | source)
XLA Modules:
  0.0 886.9 jit_solution(7220294062523722070)
XLA Ops:
  0.6 0.7 fusion.51
  1.4 1.2 reduce-window.6
  2.9 0.8 fusion.21
  4.4 2.6 scatter_custom_fusion
  7.0 33.2 %all_to_all.41 = s32[64,16,1]{1,2,0:T(1,128)S(1)} all-to-all(s32[64,16,1]{1,2,0:T(1,128)S(1)} %bitcast.94), channel_id=1, replica_groups=mesh['grid'=64,'scen'=8] {'grid'}, dimensions={0} | all-to-all | bytes 8192 | tf_op jit(solution)/shard_map/all_to_all | solution.py:119
  40.7 0.7 reduce.9
  41.6 3.3 gather_fusion
  44.9 1.8 copy.121
  46.7 4.7 all-to-all-start.1
  52.1 2.4 scatter_custom_fusion.3
  55.8 49.7 %all-to-all-done.1 = f32[2,1024,128]{2,0,1:T(2,128)S(1)} async-done(((f32[2,1024,128]{2,0,1:T(2,128)}), f32[2,1024,128]{2,0,1:T(2,128)S(1)}, u32[]{:S(2)}, u32[]{:S(2)}) %all-to-all-start.1) | async-done | bytes 1048608 | tf_op jit(solution)/shard_map/all_to_all | solution.py:138
  105.5 6.1 all-to-all-start.3
  111.6 2.1 gather_fusion.1
  113.9 1.0 multiply_subtract_fusion.11
  114.9 2.3 fusion.78
  118.5 2.5 fusion.76
  121.7 1.7 add_multiply_fusion.3
  125.3 1.6 broadcast.2380.clone
  126.9 47.4 %scatter_fusion = f32[3,1024,128]{2,0,1:T(4,128)} fusion(f32[3,1024,128]{2,0,1:T(4,128)} %broadcast.2380.clone, s32[512]{0:T(512)S(1)} %bitcast.102, f32[512,3,128]{2,1,0:T(4,128)S(1)} %copy.123), kind=kCustom, calls=%fused_computation.5 | custom fusion | bytes 2361344 | tf_op jit(solution)/shard_map/scatter | solution.py:160
  175.0 15.3 %all-to-all-start.2 = ((f32[3,1024,128]{2,0,1:T(4,128)}), f32[3,1024,128]{2,0,1:T(4,128)S(1)}, u32[]{:S(2)}, u32[]{:S(2)}) async-start(f32[3,1024,128]{2,0,1:T(4,128)} %scatter_fusion), calls=%async_computation.2 | async-start | bytes 4194304 | tf_op jit(solution)/shard_map/all_to_all | solution.py:163
  190.3 0.8 convert_reduce_fusion
  191.3 7.6 scatter_fusion.2
  198.9 90.2 %all-to-all-done.2 = f32[3,1024,128]{2,0,1:T(4,128)S(1)} async-done(((f32[3,1024,128]{2,0,1:T(4,128)}), f32[3,1024,128]{2,0,1:T(4,128)S(1)}, u32[]{:S(2)}, u32[]{:S(2)}) %all-to-all-start.2) | async-done | bytes 1572896 | tf_op jit(solution)/shard_map/all_to_all | solution.py:163
  289.2 33.0 %scatter_fusion.1 = f32[3,256,128]{2,0,1:T(4,128)S(1)} fusion(f32[3,256,128]{2,0,1:T(4,128)S(1)} %broadcast.2372.clone, s32[1024]{0:T(1024)S(1)} %bitcast.97, f32[1024,3,128]{2,1,0:T(4,128)S(1)} %bitcast.89), kind=kCustom, calls=%fused_computation.6 | custom fusion | flops 393216 | bytes 4722688 | tf_op jit(solution)/shard_map/scatter-add | solution.py:164
  322.2 1.0 stack_broadcast_in_dim.2
  323.8 2.1 fusion.7
  325.9 4.0 gather_fusion.2
  330.0 71.6 %all_to_all.42 = f32[2,1024,128]{2,0,1:T(2,128)} all-to-all(f32[2,1024,128]{2,0,1:T(2,128)S(1)} %bitcast.91), channel_id=1, replica_groups=mesh['grid'=64,'scen'=8] {'grid'}, dimensions={1} | all-to-all | bytes 2097152 | tf_op jit(solution)/shard_map/all_to_all | solution.py:138
  401.6 2.7 gather_fusion.3
  404.7 1.0 multiply_subtract_fusion.5
  405.7 2.3 fusion.72
  409.3 2.5 fusion.70
  412.5 1.7 fusion.25
  415.5 1.6 broadcast.2380
  417.1 47.4 %scatter_fusion.3 = f32[3,1024,128]{2,0,1:T(4,128)} fusion(f32[3,1024,128]{2,0,1:T(4,128)} %broadcast.2380, s32[512]{0:T(512)S(1)} %bitcast.103, f32[512,3,128]{2,1,0:T(4,128)S(1)} %copy.127), kind=kCustom, calls=%fused_computation.9 | custom fusion | bytes 2361344 | tf_op jit(solution)/shard_map/scatter | solution.py:160
  464.5 6.2 all-to-all-start.5
  471.0 0.8 copy.133
  472.8 1.0 fusion.68
  473.9 10.6 %psum.29 = f32[256]{0:T(256)S(1)} all-reduce(f32[256]{0:T(256)S(1)} %get-tuple-element.32), channel_id=1, replica_groups=mesh['grid'=64,'scen'=8] {'scen'}, use_global_device_ids=true, to_apply=%region_12.13 | all-reduce | flops 256 | bytes 2048 | tf_op jit(solution)/shard_map/psum | solution.py:181
  484.7 209.9 %psum.28 = f32[16,128]{1,0:T(8,128)S(1)} all-reduce(f32[16,128]{1,0:T(8,128)S(1)} %fusion.54), channel_id=1, replica_groups=mesh['grid'=64,'scen'=8] {'grid'}, use_global_device_ids=true, to_apply=%region_10.11 | all-reduce | flops 2048 | bytes 16384 | tf_op jit(solution)/shard_map/psum | solution.py:177
  695.2 33.0 %scatter_fusion.4 = f32[3,256,128]{2,0,1:T(4,128)S(1)} fusion(f32[3,256,128]{2,0,1:T(4,128)S(1)} %broadcast.2372, s32[1024]{0:T(1024)S(1)} %bitcast.98, f32[1024,3,128]{2,1,0:T(4,128)S(1)} %bitcast.88), kind=kCustom, calls=%fused_computation.10 | custom fusion | flops 393216 | bytes 4722688 | tf_op jit(solution)/shard_map/scatter-add | solution.py:164
  728.5 1.1 add_reduce_fusion
  729.6 0.9 fusion.52
  730.6 0.8 copy.140
  731.4 141.9 %psum.30 = f32[16,128]{1,0:T(8,128)S(1)} all-reduce(f32[16,128]{1,0:T(8,128)S(1)} %fusion.52), channel_id=1, replica_groups=mesh['grid'=64,'scen'=8] {'grid'}, use_global_device_ids=true, to_apply=%region_13.14 | all-reduce | flops 2048 | bytes 16384 | tf_op jit(solution)/shard_map/psum | solution.py:177
  873.6 0.8 copy.141
  874.3 10.0 %psum.31 = f32[256]{0:T(256)S(1)} all-reduce(f32[256]{0:T(256)S(1)} %get-tuple-element.30), channel_id=1, replica_groups=mesh['grid'=64,'scen'=8] {'scen'}, use_global_device_ids=true, to_apply=%region_15.16 | all-reduce | flops 256 | bytes 2048 | tf_op jit(solution)/shard_map/psum | solution.py:181
  884.9 1.1 fusion.10
  (114 shorter events, 16.0 us)
Async XLA Ops:
  0.6 40.9 %copy-start = (f32[2,256,128]{2,1,0:T(8,128)S(1)}, f32[2,256,128]{2,1,0:T(8,128)}, u32[]{:S(2)}) copy-start(f32[2,256,128]{2,1,0:T(8,128)} %param.17) | copy-start | bytes 786436
  4.4 122.6 %copy-start.14 = (s32[512,1]{0,1:T(1,128)}, s32[512,1]{0,1:T(1,128)S(1)}, u32[]{:S(2)}) copy-start(s32[512,1]{0,1:T(1,128)S(1)} %compare_select_fusion.1) | copy-start | bytes 6148
  41.6 3.3 copy-start.13
  44.9 10.9 %copy-start.20 = (f32[256]{0:T(256)S(1)}, f32[256]{0:T(256)}, u32[]{:S(2)}) copy-start(f32[256]{0:T(256)} %param.19) | copy-start | bytes 3076
  46.7 58.8 %all-to-all-start.1 = ((f32[2,1024,128]{2,0,1:T(2,128)}), f32[2,1024,128]{2,0,1:T(2,128)S(1)}, u32[]{:S(2)}, u32[]{:S(2)}) async-start(f32[2,1024,128]{2,0,1:T(2,128)} %copy.121), calls=%async_computation.1 | async-start | bytes 2097152 | tf_op jit(solution)/shard_map/all_to_all | solution.py:138
  51.4 62.4 %copy-start.1 = (f32[4,256,128]{2,1,0:T(8,128)S(1)}, f32[4,256,128]{2,1,0:T(8,128)}, u32[]{:S(2)}) copy-start(f32[4,256,128]{2,1,0:T(8,128)} %param.18) | copy-start | bytes 1572868
  55.8 58.1 %copy-start.18 = (s32[1024]{0:T(1024)}, s32[1024]{0:T(1024)S(1)}, u32[]{:S(2)}) copy-start(s32[1024]{0:T(1024)S(1)} %pad_clamp_fusion) | copy-start | bytes 12292
  105.5 68.9 %all-to-all-start.3 = ((s32[64,16,1]{1,2,0:T(1,128)}), s32[64,16,1]{1,2,0:T(1,128)S(1)}, u32[]{:S(2)}, u32[]{:S(2)}) async-start(s32[64,16,1]{1,2,0:T(1,128)} %bitcast.13), calls=%async_computation.3 | async-start | bytes 65536 | tf_op jit(solution)/shard_map/all_to_all | solution.py:120
  121.0 2.5 copy-start.25
  124.0 0.7 copy-start.5
  124.0 0.7 copy-start.7
  174.4 15.9 %copy-start.22 = (f32[256]{0:T(256)S(1)}, f32[256]{0:T(256)}, u32[]{:S(2)}) copy-start(f32[256]{0:T(256)} %param.26) | copy-start | bytes 3076
  174.4 0.6 copy-start.12
  175.0 114.1 %all-to-all-start.2 = ((f32[3,1024,128]{2,0,1:T(4,128)}), f32[3,1024,128]{2,0,1:T(4,128)S(1)}, u32[]{:S(2)}, u32[]{:S(2)}) async-start(f32[3,1024,128]{2,0,1:T(4,128)} %scatter_fusion), calls=%async_computation.2 | async-start | bytes 4194304 | tf_op jit(solution)/shard_map/all_to_all | solution.py:163
  289.1 34.7 %slice-start = ((f32[2,256,128]{2,1,0:T(8,128)}), f32[1,256,128]{2,1,0:T(8,128)S(1)}, s32[]{:S(2)}) async-start(f32[2,256,128]{2,1,0:T(8,128)} %param.17), calls=%async_computation.6 | async-start | bytes 262144 | tf_op jit(solution)/shard_map/slice | solution.py:166
  323.2 0.7 copy-start.3
  325.9 75.7 %copy-start.19 = (s32[1024]{0:T(1024)S(1)}, s32[1024]{0:T(1024)}, u32[]{:S(2)}) copy-start(s32[1024]{0:T(1024)} %copy-done.18) | copy-start | bytes 12292
  401.6 2.9 copy-start.6
  401.6 2.9 copy-start.8
  401.6 2.9 copy-start.27
  404.7 9.5 %copy-start.2 = (f32[4,256,128]{2,1,0:T(8,128)}, f32[4,256,128]{2,1,0:T(8,128)S(1)}, u32[]{:S(2)}) copy-start(f32[4,256,128]{2,1,0:T(8,128)S(1)} %get-tuple-element.64) | copy-start | bytes 1572868
  411.8 2.4 copy-start.21
  411.8 2.4 copy-start.26
  414.9 2.2 copy-start.15
  464.5 6.2 copy-start.9
  464.5 6.4 copy-start.10
  464.5 6.5 copy-start.11
  464.5 230.6 %all-to-all-start.5 = ((f32[3,1024,128]{2,0,1:T(4,128)}), f32[3,1024,128]{2,0,1:T(4,128)S(1)}, u32[]{:S(2)}, u32[]{:S(2)}) async-start(f32[3,1024,128]{2,0,1:T(4,128)} %scatter_fusion.3), calls=%async_computation.5 | async-start | bytes 4194304 | tf_op jit(solution)/shard_map/all_to_all | solution.py:163
  470.8 13.7 %copy-start.16 = (s32[256]{0:T(256)S(1)}, s32[256]{0:T(256)}, u32[]{:S(2)}) copy-start(s32[256]{0:T(256)} %param.24) | copy-start | bytes 3076
  472.5 12.0 %copy-start.24 = (f32[256]{0:T(256)}, f32[256]{0:T(256)S(1)}, u32[]{:S(2)}) copy-start(f32[256]{0:T(256)S(1)} %multiply_add_fusion) | copy-start | bytes 3076
  728.2 145.0 %copy-start.17 = (s32[256]{0:T(256)S(1)}, s32[256]{0:T(256)}, u32[]{:S(2)}) copy-start(s32[256]{0:T(256)} %param.24) | copy-start | bytes 3076
  728.3 156.6 %copy-start.4 = (f32[1,256,128]{2,0,1:T(1,128)S(1)}, f32[1,256,128]{2,0,1:T(1,128)}, u32[]{:S(2)}) copy-start(f32[1,256,128]{2,0,1:T(1,128)} %copy-done.3) | copy-start | bytes 393220
  728.3 156.6 %copy-start.23 = (f32[256]{0:T(256)S(1)}, f32[256]{0:T(256)}, u32[]{:S(2)}) copy-start(f32[256]{0:T(256)} %param.26) | copy-start | bytes 3076
where the time goes:
time: 898 us; the launch traced here: 887 us
  blocking collectives  477 us (53%)
  waiting for transfers between devices  140 us (16%)
  local copies, waits for them, and re-layouts  128 us (14%)
  other arithmetic  105 us (12%)
  starting transfers between devices  32.3 us (4%)
    psum x2, blocking collectives, on_device(): regional = lax.psum(regional_part, 'grid')  352 us
    scatter x2, local copies, waits for them, and re-layouts, on_device(): jnp.zeros((3, ngrid * capacity, terms.shape[2]), jnp.float32).at[:, slot, :]  94.9 us
    all_to_all x2, waiting for transfers between devices, on_device(): lax.all_to_all(outgoing, 'grid', split_axis=1, concat_axis=1, tiled=True)  90.2 us
    all_to_all x1, blocking collectives, on_device(): lax.all_to_all(looked, 'grid', split_axis=1, concat_axis=1, tiled=True)  71.6 us
    scatter-add x2, other arithmetic, on_device(): jnp.zeros((3, buses, received.shape[2]), jnp.float32).at[:, asked, :]  66 us
    all_to_all x1, waiting for transfers between devices, on_device(): lax.all_to_all(looked, 'grid', split_axis=1, concat_axis=1, tiled=True)  49.7 us
    all_to_all x1, blocking collectives, on_device(): lax.all_to_all(request, 'grid', split_axis=0, concat_axis=0, tiled=True)  33.2 us
    all_to_all x2, starting transfers between devices, on_device(): lax.all_to_all(outgoing, 'grid', split_axis=1, concat_axis=1, tiled=True)  21.5 us
  transfers between devices with their start and end apart: 4, of which 2 were waited for; matrix products, arithmetic and copies ran while one was open for 9% of the time, Pallas kernels for 0%

commit v1 on v0

v1 whole, which is shorter than its diff:
```python
import functools

import jax
import jax.numpy as jnp
from jax import lax
from jax.experimental import pallas as pl
from jax.experimental.pallas import tpu as pltpu
from jax.sharding import PartitionSpec as P

NEWTON = 3
REGIONS = 16
CAP = 16
LANES = 128
REGION_GAIN = 10.0
BLOCK = 32

F32 = jnp.float32
BF16 = jnp.bfloat16
SMEM = pltpu.SMEM
VMEM = pltpu.VMEM


def smem():
    return pl.BlockSpec(memory_space=SMEM)


def vmem():
    return pl.BlockSpec(memory_space=VMEM)


def pieces(x, count):
    parts = []
    for _ in range(count - 1):
        head = x.astype(BF16)
        parts.append(head)
        x = x - head.astype(F32)
    parts.append(x.astype(BF16))
    return parts


def picked(selector, x, count):
    total = None
    for part in pieces(x, count):
        term = jnp.dot(selector, part, preferred_element_type=F32)
        total = term if total is None else total + term
    return total


def dot_lanes(a, b):
    return lax.dot_general(a, b, (((1,), (1,)), ((), ())), preferred_element_type=F32)


def plan_kernel(count_ref, owner_ref, bus_ref, slot_ref, request_ref):
    ends = owner_ref.shape[1]
    owners = request_ref.shape[0]
    owner = owner_ref[...]
    end_id = lax.broadcasted_iota(jnp.int32, (1, ends), 1)
    live = lax.rem(end_id, ends // 2) < count_ref[0]
    code = jnp.where(live, bus_ref[...] + 1, 0).astype(F32)
    hits = lax.broadcasted_iota(jnp.int32, (owners, ends), 0) == owner
    hits = hits.astype(F32)
    before = lax.broadcasted_iota(jnp.int32, (ends, ends), 0) < lax.broadcasted_iota(
        jnp.int32, (ends, ends), 1
    )
    earlier = jnp.dot(hits.astype(BF16), before.astype(BF16), preferred_element_type=F32)
    rank = jnp.sum(hits * earlier, axis=0, keepdims=True).astype(jnp.int32)
    slot_ref[...] = owner * CAP + rank
    ranks = lax.broadcasted_iota(jnp.int32, (LANES, ends), 0) == rank
    table = dot_lanes((hits * code).astype(BF16), ranks.astype(BF16))
    request_ref[...] = table.astype(jnp.int32)


def send_rows(asked_ref, volt_ref, out_ref):
    def step(o, carry):
        for r in range(CAP):
            bus = jnp.maximum(asked_ref[o, r] - 1, 0)
            for c in range(2):
                out_ref[o, c * CAP + r : c * CAP + r + 1, :] = volt_ref[c, pl.ds(bus, 1), :]
        return carry

    lax.fori_loop(0, out_ref.shape[0], step, 0)


def first_send_kernel(asked_ref, volt_ref, out_ref):
    send_rows(asked_ref, volt_ref, out_ref)


def sin_cos(x):
    turns = jnp.floor(x * 0.636619772367581343 + 0.5)
    r = x - turns * 1.5703125
    r = r - turns * 4.83751296997070312e-04
    r = r - turns * 7.54978995489188216e-08
    n = turns.astype(jnp.int32)
    z = r * r
    s = ((-1.9515295891e-4 * z + 8.3321608736e-3) * z - 1.6666654611e-1) * z * r + r
    c = ((2.443315711809948e-5 * z - 1.388731625493765e-3) * z + 4.166664568298827e-2) * z * z
    c = c - 0.5 * z + 1.0
    odd = (n & 1) == 1
    sine = jnp.where(odd, c, s)
    cosine = jnp.where(odd, s, c)
    sine = jnp.where((n & 2) == 2, -sine, sine)
    cosine = jnp.where(((n + 1) & 2) == 2, -cosine, cosine)
    return sine, cosine


def branch_newton(center, cond, susc):
    k = 2.0 * cond
    vf, af, vt, at = center
    for step in range(NEWTON):
        s, c = sin_cos(af - at)
        w0 = vf - vt * c
        w1 = vt * s
        if step > 0:
            r0, r1, r2, r3 = vf - center[0], af - center[1], vt - center[2], at - center[3]
            r3 = vt * r3
            w0 = w0 - r0 + r2 * c + r3 * s
            w1 = w1 - r1 * vf - r2 * s + r3 * c
        ss, cc, tt = s * s, c * c, vt * vt
        m00 = 1.0 + k * (1.0 + cc + tt * ss)
        m11 = 1.0 + k * (vf * vf + ss + tt * cc)
        m01 = k * (s * c * (tt - 1.0))
        scale = k / (m00 * m11 - m01 * m01)
        z0 = (m11 * w0 - m01 * w1) * scale
        z1 = (m00 * w1 - m01 * w0) * scale
        new = (
            center[0] - z0,
            center[1] - vf * z1,
            center[2] + (c * z0 - s * z1),
            center[3] + vt * (s * z0 + c * z1),
        )
        vf, af, vt, at = new
    s, c = sin_cos(af - at)
    product = vf * vt
    flow_from = cond * vf * vf - product * (cond * c + susc * s)
    flow_to = cond * vt * vt - product * (cond * c - susc * s)
    return (vf, af, vt, at), flow_from, flow_to


def line_kernel(second, count_ref, slot_ref, arrived_ref, dual_ref, *refs):
    if second:
        previous_ref, param_ref, out_ref, dual_out_ref, near_ref, term_ref = refs
    else:
        param_ref, out_ref, state_ref, near_ref, term_ref = refs
    lines = dual_ref.shape[1]

    def step(block, carry):
        base = pl.multiple_of(block * BLOCK, BLOCK)
        rows = pl.ds(base, BLOCK)
        starts = []
        for end in range(2):
            for j in range(BLOCK):
                slot = slot_ref[end * lines + base + j]
                high = slot & -CAP
                starts.append((slot + high, slot + high + high))
        for end in range(2):
            for j in range(BLOCK):
                start = starts[end * BLOCK + j][0]
                for c in range(2):
                    near_ref[2 * end + c, j : j + 1, :] = arrived_ref[pl.ds(start + c * CAP, 1), :]
        near = [near_ref[i] for i in range(4)]
        dual = [dual_ref[i, rows, :] for i in range(4)]
        line_id = lax.broadcasted_iota(jnp.int32, (BLOCK, LANES), 0) + base
        live = line_id < count_ref[0]
        if second:
            dual = [
                jnp.where(live, dual[i] + previous_ref[i, rows, :] - near[i], dual[i])
                for i in range(4)
            ]
            for i in range(4):
                dual_out_ref[i, rows, :] = dual[i]
        center = [near[i] - dual[i] for i in range(4)]
        param = param_ref[rows, :]
        cond = jnp.broadcast_to(param[:, 0:1], (BLOCK, LANES))
        susc = jnp.broadcast_to(param[:, 1:2], (BLOCK, LANES))
        state, flow_from, flow_to = branch_newton(center, cond, susc)
        if not second:
            for i in range(4):
                state_ref[i, rows, :] = state[i]
        terms = [
            state[0] + dual[0], state[1] + dual[1], flow_from,
            state[2] + dual[2], state[3] + dual[3], flow_to,
        ]
        for i in range(6):
            term_ref[i] = jnp.where(live, terms[i], 0.0)
        for end in range(2):
            for j in range(BLOCK):
                start = starts[end * BLOCK + j][1]
                for c in range(3):
                    out_ref[pl.ds(start + c * CAP, 1), :] = term_ref[3 * end + c, j : j + 1, :]
        return carry

    out_ref[...] = jnp.zeros_like(out_ref)
    lax.fori_loop(0, lines // BLOCK, step, 0)


def column(param, index):
    return jnp.broadcast_to(param[:, index : index + 1], (param.shape[0], LANES))


def region_term(param, regional, buses_all):
    width = regional.shape[0]
    share = width // REGIONS
    ids = lax.broadcasted_iota(jnp.int32, (param.shape[0], width), 1)
    member = ids == param[:, 6:7].astype(jnp.int32) * share
    total = picked(member.astype(BF16), regional, 3)
    return total * (REGION_GAIN * REGIONS / buses_all)


def owner_kernel(second, buses_all, scen_all, asked_ref, row_ref, recv_ref, volt_ref, param_ref,
                 region_ref, load_ref, price_ref, nadual_ref, *refs):
    if second:
        (disp1_ref, mism1_ref, regional_ref, totals_ref,
         volt_out, disp_out, part_out, total_out, price_out) = refs
    else:
        volt_out, disp_out, mism_out, part_out, total_out, send_out = refs
    buses = volt_ref.shape[1]
    devices = recv_ref.shape[0]
    slots = devices * CAP
    ids = lax.broadcasted_iota(jnp.int32, (buses, slots), 0) + 1
    hits = (ids == row_ref[...]).astype(BF16)
    rows = [recv_ref[:, c * CAP : (c + 1) * CAP, :].reshape(slots, LANES) for c in range(3)]
    pair = picked(hits, jnp.concatenate(rows[:2], axis=1), 2)
    flows = pieces(rows[2], 2)
    ones = jnp.ones((slots, LANES), BF16)
    last = jnp.dot(hits, jnp.concatenate([flows[0], ones], axis=1), preferred_element_type=F32)
    net = last[:, :LANES] + jnp.dot(hits, flows[1], preferred_element_type=F32)
    degree = last[:, LANES:]
    param = param_ref[...]
    weight = column(param, 0)
    inverse = 1.0 / (degree + weight)
    volt_out[0] = (pair[:, :LANES] + weight * column(param, 1)) * inverse
    volt_out[1] = (pair[:, LANES:] + weight * volt_ref[1]) * inverse
    if not second:
        send_rows(asked_ref, volt_out, send_out)
    load, price, nadual = load_ref[...], price_ref[...], nadual_ref[...]
    if second:
        commit = jnp.sum(jnp.transpose(totals_ref[...]), axis=1, keepdims=True) / scen_all
        commit = jnp.broadcast_to(commit, (buses, LANES))
        nadual = nadual + disp1_ref[...] - commit
        price = price + mism1_ref[...] + region_term(param, regional_ref[...], buses_all)
    else:
        commit = column(param, 5)
    want = (load + net - price - column(param, 3) + (commit - nadual)) / (
        2.0 * column(param, 2) + 2.0
    )
    dispatch = jnp.clip(want, 0.0, column(param, 4))
    mismatch = dispatch - load - net
    disp_out[...] = dispatch
    if second:
        price_out[...] = price + mismatch
    else:
        mism_out[...] = mismatch
    width = part_out.shape[0]
    share = width // REGIONS
    region = lax.broadcasted_iota(jnp.int32, (width, buses), 0) // share == region_ref[...]
    part_out[...] = picked(region.astype(BF16), mismatch, 3)
    total = None
    ones = jnp.ones((total_out.shape[0], LANES), BF16)
    for piece in pieces(dispatch + nadual, 3):
        term = dot_lanes(ones, piece)
        total = term if total is None else total + term
    total_out[...] = total


def close_kernel(buses_all, param_ref, regional_ref, price_ref, out_ref):
    out_ref[...] = price_ref[...] + region_term(param_ref[...], regional_ref[...], buses_all)


def on_device(
    volt_init,
    line_dual,
    conductance,
    susceptance,
    endpoint_owner,
    endpoint_bus,
    line_count,
    bus_region,
    vm_set,
    stiffness,
    load,
    price_init,
    na_dual_init,
    commit_init,
    cost_quad,
    cost_lin,
    pmax,
):
    ngrid = lax.axis_size("grid")
    nscen = lax.axis_size("scen")
    lines = conductance.shape[0]
    ends = 2 * lines
    buses = vm_set.shape[0]
    scen = load.shape[1]
    buses_all = buses * ngrid
    shape = jax.ShapeDtypeStruct

    def exchange(x):
        return lax.all_to_all(x, "grid", split_axis=0, concat_axis=0, tiled=True)

    slot, request = pl.pallas_call(
        plan_kernel,
        out_shape=(shape((1, ends), jnp.int32), shape((ngrid, LANES), jnp.int32)),
        in_specs=[smem(), vmem(), vmem()],
        out_specs=(vmem(), vmem()),
        name="plan",
    )(line_count, endpoint_owner.reshape(1, ends), endpoint_bus.reshape(1, ends))
    slot = slot.reshape(ends)
    asked = exchange(request)
    asked_row = asked[:, :CAP].reshape(1, ngrid * CAP)

    line_param = jnp.stack([conductance, susceptance], axis=1)
    bus_param = jnp.stack(
        [stiffness, vm_set, cost_quad, cost_lin, pmax, commit_init, bus_region.astype(F32),
         jnp.zeros_like(pmax)],
        axis=1,
    )
    region_row = bus_region.reshape(1, buses)
    send_shape = shape((ngrid, 2 * CAP, LANES), F32)
    bus_shape = shape((buses, LANES), F32)

    sent = pl.pallas_call(
        first_send_kernel,
        out_shape=send_shape,
        in_specs=[smem(), vmem()],
        out_specs=vmem(),
        name="first_send",
    )(asked, volt_init)

    def line_call(second, arrived, previous):
        outs = [shape((ngrid * 3 * CAP, LANES), F32), shape((4, lines, LANES), F32)]
        args = [line_count, slot, arrived.reshape(ngrid * 2 * CAP, LANES), line_dual]
        if second:
            args.append(previous)
        args.append(line_param)
        out, other = pl.pallas_call(
            functools.partial(line_kernel, second),
            out_shape=outs,
            in_specs=[smem(), smem()] + [vmem()] * (len(args) - 2),
            out_specs=[vmem(), vmem()],
            scratch_shapes=[VMEM((4, BLOCK, LANES), F32), VMEM((6, BLOCK, LANES), F32)],
            name="lines2" if second else "lines1",
        )(*args)
        return out.reshape(ngrid, 3 * CAP, LANES), other

    def owner_call(second, received, volt, extra):
        outs = [shape((2, buses, LANES), F32), bus_shape]
        if not second:
            outs.append(bus_shape)
        outs += [shape((ngrid, LANES), F32), shape((nscen, buses), F32)]
        outs.append(bus_shape if second else send_shape)
        args = [asked, asked_row, received, volt, bus_param, region_row, load, price_init,
                na_dual_init] + list(extra)
        return pl.pallas_call(
            functools.partial(owner_kernel, second, buses_all, scen * nscen),
            out_shape=outs,
            in_specs=[smem()] + [vmem()] * (len(args) - 1),
            out_specs=[vmem()] * len(outs),
            name="owner2" if second else "owner1",
        )(*args)

    def regional_sum(part):
        own = jnp.sum(exchange(part), axis=0, keepdims=True)
        return exchange(jnp.broadcast_to(own, (ngrid, LANES)))

    def scenario_parts(total):
        return lax.all_to_all(total, "scen", split_axis=0, concat_axis=0, tiled=True)

    out, state = line_call(False, exchange(sent), None)
    volt, disp1, mism1, part, total, sent = owner_call(False, exchange(out), volt_init, ())
    regional = regional_sum(part)
    totals = scenario_parts(total)
    out, dual = line_call(True, exchange(sent), state)
    volt, dispatch, part, total, price = owner_call(
        True, exchange(out), volt, (disp1, mism1, regional, totals)
    )
    regional = regional_sum(part)
    commit = jnp.sum(scenario_parts(total), axis=0) / (scen * nscen)
    price = pl.pallas_call(
        functools.partial(close_kernel, buses_all),
        out_shape=bus_shape,
        in_specs=[vmem()] * 3,
        out_specs=vmem(),
        name="close",
    )(bus_param, regional, price)
    return (volt, dual, dispatch, price, commit)


def solution(mesh):
    in_specs = (
        P(None, "grid", "scen"),
        P(None, "grid", "scen"),
        P("grid"),
        P("grid"),
        P("grid", None),
        P("grid"),
        P("grid"),
        P("grid"),
        P("grid"),
        P("grid"),
        P("grid", "scen"),
        P("grid", "scen"),
        P("grid", "scen"),
        P("grid"),
        P("grid"),
        P("grid"),
        P("grid"),
    )
    out_specs = (
        P(None, "grid", "scen"),
        P(None, "grid", "scen"),
        P("grid", "scen"),
        P("grid", "scen"),
        P("grid"),
    )
    return jax.shard_map(
        on_device, mesh=mesh, in_specs=in_specs, out_specs=out_specs, check_vma=False
    )
```

time: 898 us -> 448 us (0.50); the launches traced: 887 us -> 446 us
  blocking collectives: 477 us -> 69.1 us
  waiting for transfers between devices: 140 us -> 295 us
  local copies, waits for them, and re-layouts: 128 us -> 10.2 us
  other arithmetic: 105 us -> 0.77 us
  Pallas kernels: 0 us -> 30.5 us
    psum x4 -> x0, blocking collectives: 372 us -> none  [the longest x2 352 us: on_device(): regional = lax.psum(regional_part, 'grid')]
    all_to_all x4 -> x7, waiting for transfers between devices: 140 us -> 295 us  [exchange(): return lax.all_to_all(x, 'grid', split_axis=0, concat_axis=0, tiled=True)]
    scatter x4 -> x0, local copies, waits for them, and re-layouts: 99.9 us -> none  [the longest x2 94.9 us: on_device(): jnp.zeros((3, ngrid * capacity, terms.shape[2]), jnp.float32).at[:, slot, :]]
    scatter-add x3 -> x0, other arithmetic: 73.6 us -> none  [the longest x2 66 us: on_device(): jnp.zeros((3, buses, received.shape[2]), jnp.float32).at[:, asked, :]]
    all_to_all x2 -> x4, blocking collectives: 105 us -> 69.1 us  [the longest x2 53.6 us: exchange(): return lax.all_to_all(x, 'grid', split_axis=0, concat_axis=0, tiled=True)]
    pallas_call x0 -> x7, Pallas kernels: none -> 30.5 us  [the longest x2 13.2 us: line_call(): pl.pallas_call(functools.partial(line_kernel, second), out_shape=outs, in...]
    gather x7 -> x0, local copies, waits for them, and re-layouts: 14 us -> none  [the longest x3 9.14 us: on_device(): looked = volt[:, asked, :]]
    cos x8 -> x0, other arithmetic: 11.8 us -> none  [the longest x4 9.56 us: branch_newton(): cos_f = jnp.cos(from_ang)]
  transfers between devices with their start and end apart: 4 -> 7, of which waited for: 2 -> 7; matrix products, arithmetic and copies ran while one was open for 9% -> 1% of each run, Pallas kernels for 0% -> 1%
where the time goes in v1:
time: 448 us; the launch traced here: 446 us
  waiting for transfers between devices  295 us (66%)
  blocking collectives  69.1 us (15%)
  starting transfers between devices  38.7 us (9%)
  Pallas kernels  30.5 us (7%)
  local copies, waits for them, and re-layouts  10.2 us (2%)
    all_to_all x7, waiting for transfers between devices, exchange(): return lax.all_to_all(x, 'grid', split_axis=0, concat_axis=0, tiled=True)  295 us
    all_to_all x2, blocking collectives, exchange(): return lax.all_to_all(x, 'grid', split_axis=0, concat_axis=0, tiled=True)  53.6 us
    all_to_all x7, starting transfers between devices, exchange(): return lax.all_to_all(x, 'grid', split_axis=0, concat_axis=0, tiled=True)  38.7 us
    all_to_all x2, blocking collectives, scenario_parts(): lax.all_to_all(total, 'scen', split_axis=0, concat_axis=0, tiled=True)  15.5 us
    pallas_call x2, Pallas kernels, line_call(): pl.pallas_call(functools.partial(line_kernel, second), out_shape=outs, in...  13.2 us
    pallas_call x2, Pallas kernels, owner_call(): pl.pallas_call(functools.partial(owner_kernel, second, buses_all, scen *...  9.25 us
  transfers between devices with their start and end apart: 7, of which 7 were waited for; matrix products, arithmetic and copies ran while one was open for 1% of the time, Pallas kernels for 1%

profile of v1, /device:TPU:6, one launch (start us, length us, event | category | flops | bytes accessed | tf_op | source)
XLA Modules:
  0.0 446.1 jit_solution(14341420428654461336)
XLA Ops:
  1.3 1.7 plan.1
  3.0 33.3 %all_to_all.85 = s32[64,1,128]{2,1,0:T(1,128)} all-to-all(s32[64,1,128]{2,1,0:T(1,128)} %bitcast.48), channel_id=1, replica_groups=mesh['grid'=64,'scen'=8] {'grid'}, dimensions={0} | all-to-all | bytes 65536 | tf_op jit(solution)/shard_map/all_to_all | solution.py:298
  36.3 4.4 first_send.1
  40.6 4.7 %all-to-all-start.1 = ((f32[64,32,128]{2,1,0:T(8,128)}), f32[64,32,128]{2,1,0:T(8,128)S(1)}, u32[]{:S(2)}, u32[]{:S(2)}) async-start(f32[64,32,128]{2,1,0:T(8,128)} %first_send.1), calls=%async_computation.1 | async-start | bytes 2097152 | tf_op jit(solution)/shard_map/all_to_all | solution.py:298
  45.3 0.0 copy-done.14
  45.3 0.0 copy-done.15
  45.3 0.8 copy.32.refs_0_.refs_1_
  46.1 53.5 %all-to-all-done.1 = f32[64,32,128]{2,1,0:T(8,128)S(1)} async-done(((f32[64,32,128]{2,1,0:T(8,128)}), f32[64,32,128]{2,1,0:T(8,128)S(1)}, u32[]{:S(2)}, u32[]{:S(2)}) %all-to-all-start.1) | async-done | bytes 1048608 | tf_op jit(solution)/shard_map/all_to_all | solution.py:298
  99.6 1.0 copy-done.3
  100.6 6.6 %lines1.1 = (f32[3072,128]{1,0:T(8,128)}, f32[4,256,128]{2,1,0:T(8,128)}) custom-call(s32[1]{0:T(128)S(6)} %copy.44.count_ref, s32[512]{0:T(512)} %bitcast.53, f32[2048,128]{1,0:T(8,128)} %bitcast.36, f32[4,256,128]{2,1,0:T(8,128)} %dual_ref.3, f32[256,2]{1,0:T(8,128)} %copy.32.refs_0_.refs_1_), custom_call_target="tpu_custom_call" | custom-call | tf_op jit(solution)/shard_map/lines1/pallas_call | solution.py:335
  107.2 0.0 copy-start.10
  107.2 0.0 copy-start.11
  107.2 0.0 copy-start.12
  107.2 0.0 copy-start.13
  107.2 6.0 %all-to-all-start.2 = ((f32[64,48,128]{2,1,0:T(8,128)}), f32[64,48,128]{2,1,0:T(8,128)S(1)}, u32[]{:S(2)}, u32[]{:S(2)}) async-start(f32[64,48,128]{2,1,0:T(8,128)} %bitcast.38), calls=%async_computation.2 | async-start | bytes 3145728 | tf_op jit(solution)/shard_map/all_to_all | solution.py:298
  113.4 0.8 copy.33.param_ref
  114.2 0.7 reshape.61.row_ref
  114.8 75.2 %all-to-all-done.2.recv_ref = f32[64,48,128]{2,1,0:T(8,128)S(1)} async-done(((f32[64,48,128]{2,1,0:T(8,128)}), f32[64,48,128]{2,1,0:T(8,128)S(1)}, u32[]{:S(2)}, u32[]{:S(2)}) %all-to-all-start.2) | async-done | bytes 1572896 | tf_op jit(solution)/shard_map/all_to_all | solution.py:298
  190.1 1.2 copy-done
  191.3 5.8 %owner1.1 = (f32[2,256,128]{2,1,0:T(8,128)}, f32[256,128]{1,0:T(8,128)}, f32[256,128]{1,0:T(8,128)}, f32[64,128]{1,0:T(8,128)}, f32[8,256]{1,0:T(8,128)}, /*index=5*/f32[64,32,128]{2,1,0:T(8,128)}) custom-call(s32[64,128]{1,0:T(8,128)} %bitcast.40, s32[1,1024]{1,0:T(1,128)} %reshape.61.row_ref, f32[64,48,128]{2,1,0:T(8,128)} %copy-done, ...), custom_call_target="tpu_custom_call" | custom-call | tf_op jit(solution)/shard_map/owner1/pallas_call | solution.py:353
  197.0 0.7 copy.36
  197.8 7.8 %all_to_all.86 = f32[8,1,256]{2,1,0:T(1,128)S(1)} all-to-all(f32[8,1,256]{2,1,0:T(1,128)S(1)} %copy.36), channel_id=1, replica_groups=mesh['grid'=64,'scen'=8] {'scen'}, dimensions={0} | all-to-all | bytes 16384 | tf_op jit(solution)/shard_map/all_to_all | solution.py:366
  205.6 20.4 %all_to_all.87 = f32[64,1,128]{2,1,0:T(1,128)S(1)} all-to-all(f32[64,1,128]{2,1,0:T(1,128)} %bitcast.47), channel_id=1, replica_groups=mesh['grid'=64,'scen'=8] {'grid'}, dimensions={0} | all-to-all | bytes 65536 | tf_op jit(solution)/shard_map/all_to_all | solution.py:298
  226.0 4.7 %all-to-all-start.3 = ((f32[64,32,128]{2,1,0:T(8,128)}), f32[64,32,128]{2,1,0:T(8,128)S(1)}, u32[]{:S(2)}, u32[]{:S(2)}) async-start(f32[64,32,128]{2,1,0:T(8,128)} %get-tuple-element.25), calls=%async_computation.3 | async-start | bytes 2097152 | tf_op jit(solution)/shard_map/all_to_all | solution.py:298
  230.6 0.1 reduce_sum.27
  230.7 54.0 %all-to-all-done.3 = f32[64,32,128]{2,1,0:T(8,128)S(1)} async-done(((f32[64,32,128]{2,1,0:T(8,128)}), f32[64,32,128]{2,1,0:T(8,128)S(1)}, u32[]{:S(2)}, u32[]{:S(2)}) %all-to-all-start.3) | async-done | bytes 1048608 | tf_op jit(solution)/shard_map/all_to_all | solution.py:298
  284.7 0.7 broadcast_in_dim.4
  285.4 5.8 %all-to-all-start.6 = ((f32[64,1,128]{2,1,0:T(1,128)}), f32[64,1,128]{2,1,0:T(1,128)S(1)}, u32[]{:S(2)}, u32[]{:S(2)}) async-start(f32[64,1,128]{2,1,0:T(1,128)} %broadcast_in_dim.4), calls=%async_computation.6 | async-start | bytes 65536 | tf_op jit(solution)/shard_map/all_to_all | solution.py:298
  291.3 0.0 copy-done.2
  291.3 6.6 %lines2.1 = (f32[3072,128]{1,0:T(8,128)}, f32[4,256,128]{2,1,0:T(8,128)}) custom-call(s32[1]{0:T(128)S(6)} %copy.44.count_ref, s32[512]{0:T(512)} %bitcast.54, f32[2048,128]{1,0:T(8,128)} %bitcast.35, f32[4,256,128]{2,1,0:T(8,128)} %dual_ref.3, f32[4,256,128]{2,1,0:T(8,128)} %get-tuple-element.26.refs_0_, f32[256,2]{1,0:T(8,128)} %copy.32.refs_0_.refs_1_), custom_call_target="tpu_custom_call" | custom-call | tf_op jit(solution)/shard_map/lines2/pallas_call | solution.py:335
  297.9 8.0 %all-to-all-done.6 = f32[64,1,128]{2,1,0:T(1,128)S(1)} async-done(((f32[64,1,128]{2,1,0:T(1,128)}), f32[64,1,128]{2,1,0:T(1,128)S(1)}, u32[]{:S(2)}, u32[]{:S(2)}) %all-to-all-start.6) | async-done | bytes 32800 | tf_op jit(solution)/shard_map/all_to_all | solution.py:298
  305.9 0.6 copy-done.5
  306.5 7.1 %all-to-all-start.4 = ((f32[64,48,128]{2,1,0:T(8,128)}), f32[64,48,128]{2,1,0:T(8,128)S(1)}, u32[]{:S(2)}, u32[]{:S(2)}) async-start(f32[64,48,128]{2,1,0:T(8,128)} %bitcast.37), calls=%async_computation.4 | async-start | bytes 3145728 | tf_op jit(solution)/shard_map/all_to_all | solution.py:298
  313.6 0.6 copy.43
  314.2 75.7 %all-to-all-done.4.recv_ref = f32[64,48,128]{2,1,0:T(8,128)S(1)} async-done(((f32[64,48,128]{2,1,0:T(8,128)}), f32[64,48,128]{2,1,0:T(8,128)S(1)}, u32[]{:S(2)}, u32[]{:S(2)}) %all-to-all-start.4) | async-done | bytes 1572896 | tf_op jit(solution)/shard_map/all_to_all | solution.py:298
  389.9 1.2 copy-done.1
  391.1 3.5 owner2.1
  394.6 0.7 copy.40
  395.3 7.7 %all_to_all.88 = f32[8,1,256]{2,1,0:T(1,128)S(1)} all-to-all(f32[8,1,256]{2,1,0:T(1,128)S(1)} %copy.40), channel_id=1, replica_groups=mesh['grid'=64,'scen'=8] {'scen'}, dimensions={0} | all-to-all | bytes 16384 | tf_op jit(solution)/shard_map/all_to_all | solution.py:366
  403.0 5.8 %all-to-all-start.8 = ((f32[64,1,128]{2,1,0:T(1,128)}), f32[64,1,128]{2,1,0:T(1,128)S(1)}, u32[]{:S(2)}, u32[]{:S(2)}) async-start(f32[64,1,128]{2,1,0:T(1,128)} %bitcast.46), calls=%async_computation.8 | async-start | bytes 65536 | tf_op jit(solution)/shard_map/all_to_all | solution.py:298
  408.9 14.7 %all-to-all-done.8 = f32[64,1,128]{2,1,0:T(1,128)S(1)} async-done(((f32[64,1,128]{2,1,0:T(1,128)}), f32[64,1,128]{2,1,0:T(1,128)S(1)}, u32[]{:S(2)}, u32[]{:S(2)}) %all-to-all-start.8) | async-done | bytes 32800 | tf_op jit(solution)/shard_map/all_to_all | solution.py:298
  423.6 0.1 reduce_sum.28
  423.7 0.6 broadcast_in_dim.5
  424.3 4.6 %all-to-all-start.9 = ((f32[64,1,128]{2,1,0:T(1,128)}), f32[64,1,128]{2,1,0:T(1,128)S(1)}, u32[]{:S(2)}, u32[]{:S(2)}) async-start(f32[64,1,128]{2,1,0:T(1,128)} %broadcast_in_dim.5), calls=%async_computation.9 | async-start | bytes 65536 | tf_op jit(solution)/shard_map/all_to_all | solution.py:298
  428.9 0.6 broadcast_multiply_fusion
  429.5 14.1 %all-to-all-done.9 = f32[64,1,128]{2,1,0:T(1,128)S(1)} async-done(((f32[64,1,128]{2,1,0:T(1,128)}), f32[64,1,128]{2,1,0:T(1,128)S(1)}, u32[]{:S(2)}, u32[]{:S(2)}) %all-to-all-start.9) | async-done | bytes 32800 | tf_op jit(solution)/shard_map/all_to_all | solution.py:298
  443.6 0.6 copy-done.6
  444.2 1.9 close.1
  (25 shorter events, 0.1 us)
Async XLA Ops:
  36.3 9.0 %copy-start.14 = (f32[256]{0:T(256)S(1)}, f32[256]{0:T(256)}, u32[]{:S(2)}) copy-start(f32[256]{0:T(256)} %param.20) | copy-start | bytes 3076
  36.3 9.0 %copy-start.15 = (f32[256]{0:T(256)S(1)}, f32[256]{0:T(256)}, u32[]{:S(2)}) copy-start(f32[256]{0:T(256)} %param.19) | copy-start | bytes 3076
  40.6 59.0 %all-to-all-start.1 = ((f32[64,32,128]{2,1,0:T(8,128)}), f32[64,32,128]{2,1,0:T(8,128)S(1)}, u32[]{:S(2)}, u32[]{:S(2)}) async-start(f32[64,32,128]{2,1,0:T(8,128)} %first_send.1), calls=%async_computation.1 | async-start | bytes 2097152 | tf_op jit(solution)/shard_map/all_to_all | solution.py:298
  99.6 1.0 copy-start.3
  107.2 6.1 %copy-start.7 = (s32[256]{0:T(256)S(1)}, s32[256]{0:T(256)}, u32[]{:S(2)}) copy-start(s32[256]{0:T(256)} %param.24) | copy-start | bytes 3076
  107.2 6.1 %copy-start.8 = (f32[256]{0:T(256)S(1)}, f32[256]{0:T(256)}, u32[]{:S(2)}) copy-start(f32[256]{0:T(256)} %param.26) | copy-start | bytes 3076
  107.2 6.1 %copy-start.9 = (f32[256]{0:T(256)S(1)}, f32[256]{0:T(256)}, u32[]{:S(2)}) copy-start(f32[256]{0:T(256)} %param.25) | copy-start | bytes 3076
  107.2 6.1 %copy-start.10 = (f32[256]{0:T(256)S(1)}, f32[256]{0:T(256)}, u32[]{:S(2)}) copy-start(f32[256]{0:T(256)} %param.31) | copy-start | bytes 3076
  107.2 6.1 %copy-start.11 = (f32[256]{0:T(256)S(1)}, f32[256]{0:T(256)}, u32[]{:S(2)}) copy-start(f32[256]{0:T(256)} %param.32) | copy-start | bytes 3076
  107.2 6.1 %copy-start.12 = (f32[256]{0:T(256)S(1)}, f32[256]{0:T(256)}, u32[]{:S(2)}) copy-start(f32[256]{0:T(256)} %param.33) | copy-start | bytes 3076
  107.2 6.1 %copy-start.13 = (f32[256]{0:T(256)S(1)}, f32[256]{0:T(256)}, u32[]{:S(2)}) copy-start(f32[256]{0:T(256)} %param.30) | copy-start | bytes 3076
  107.2 6.9 %copy-start.4 = (s32[64,1,128]{2,1,0:T(1,128)S(1)}, s32[64,1,128]{2,1,0:T(1,128)}, u32[]{:S(2)}) copy-start(s32[64,1,128]{2,1,0:T(1,128)} %all_to_all.85) | copy-start | bytes 98308
  107.2 82.8 %all-to-all-start.2 = ((f32[64,48,128]{2,1,0:T(8,128)}), f32[64,48,128]{2,1,0:T(8,128)S(1)}, u32[]{:S(2)}, u32[]{:S(2)}) async-start(f32[64,48,128]{2,1,0:T(8,128)} %bitcast.38), calls=%async_computation.2 | async-start | bytes 3145728 | tf_op jit(solution)/shard_map/all_to_all | solution.py:298
  190.1 1.2 copy-start
  226.0 58.8 %all-to-all-start.3 = ((f32[64,32,128]{2,1,0:T(8,128)}), f32[64,32,128]{2,1,0:T(8,128)S(1)}, u32[]{:S(2)}, u32[]{:S(2)}) async-start(f32[64,32,128]{2,1,0:T(8,128)} %get-tuple-element.25), calls=%async_computation.3 | async-start | bytes 2097152 | tf_op jit(solution)/shard_map/all_to_all | solution.py:298
  284.7 6.5 %copy-start.2 = (f32[64,32,128]{2,1,0:T(8,128)}, f32[64,32,128]{2,1,0:T(8,128)S(1)}, u32[]{:S(2)}) copy-start(f32[64,32,128]{2,1,0:T(8,128)S(1)} %all-to-all-done.3) | copy-start | bytes 3145732
  285.4 20.5 %all-to-all-start.6 = ((f32[64,1,128]{2,1,0:T(1,128)}), f32[64,1,128]{2,1,0:T(1,128)S(1)}, u32[]{:S(2)}, u32[]{:S(2)}) async-start(f32[64,1,128]{2,1,0:T(1,128)} %broadcast_in_dim.4), calls=%async_computation.6 | async-start | bytes 65536 | tf_op jit(solution)/shard_map/all_to_all | solution.py:298
  305.9 0.6 copy-start.5
  306.5 83.4 %all-to-all-start.4 = ((f32[64,48,128]{2,1,0:T(8,128)}), f32[64,48,128]{2,1,0:T(8,128)S(1)}, u32[]{:S(2)}, u32[]{:S(2)}) async-start(f32[64,48,128]{2,1,0:T(8,128)} %bitcast.37), calls=%async_computation.4 | async-start | bytes 3145728 | tf_op jit(solution)/shard_map/all_to_all | solution.py:298
  389.9 1.2 copy-start.1
  403.0 20.6 %all-to-all-start.8 = ((f32[64,1,128]{2,1,0:T(1,128)}), f32[64,1,128]{2,1,0:T(1,128)S(1)}, u32[]{:S(2)}, u32[]{:S(2)}) async-start(f32[64,1,128]{2,1,0:T(1,128)} %bitcast.46), calls=%async_computation.8 | async-start | bytes 65536 | tf_op jit(solution)/shard_map/all_to_all | solution.py:298
  424.3 19.3 %all-to-all-start.9 = ((f32[64,1,128]{2,1,0:T(1,128)}), f32[64,1,128]{2,1,0:T(1,128)S(1)}, u32[]{:S(2)}, u32[]{:S(2)}) async-start(f32[64,1,128]{2,1,0:T(1,128)} %broadcast_in_dim.5), calls=%async_computation.9 | async-start | bytes 65536 | tf_op jit(solution)/shard_map/all_to_all | solution.py:298
  443.6 0.6 copy-start.6

commit v2 on v1

--- a/solution.py
+++ b/solution.py
@@ -13,6 +13,8 @@
 LANES = 128
 REGION_GAIN = 10.0
 BLOCK = 32
+NEAR = 4
+GRANT = 16 * 2**20
 
 F32 = jnp.float32
 BF16 = jnp.bfloat16
@@ -198,10 +200,8 @@
 
 
 def region_term(param, regional, buses_all):
-    width = regional.shape[0]
-    share = width // REGIONS
-    ids = lax.broadcasted_iota(jnp.int32, (param.shape[0], width), 1)
-    member = ids == param[:, 6:7].astype(jnp.int32) * share
+    ids = lax.broadcasted_iota(jnp.int32, (param.shape[0], REGIONS), 1)
+    member = ids == param[:, 6:7].astype(jnp.int32)
     total = picked(member.astype(BF16), regional, 3)
     return total * (REGION_GAIN * REGIONS / buses_all)
 
@@ -234,7 +234,7 @@
         send_rows(asked_ref, volt_out, send_out)
     load, price, nadual = load_ref[...], price_ref[...], nadual_ref[...]
     if second:
-        commit = jnp.sum(jnp.transpose(totals_ref[...]), axis=1, keepdims=True) / scen_all
+        commit = jnp.transpose(totals_ref[...])[:, 0:1] / scen_all
         commit = jnp.broadcast_to(commit, (buses, LANES))
         nadual = nadual + disp1_ref[...] - commit
         price = price + mism1_ref[...] + region_term(param, regional_ref[...], buses_all)
@@ -250,10 +250,10 @@
         price_out[...] = price + mismatch
     else:
         mism_out[...] = mismatch
-    width = part_out.shape[0]
-    share = width // REGIONS
-    region = lax.broadcasted_iota(jnp.int32, (width, buses), 0) // share == region_ref[...]
-    part_out[...] = picked(region.astype(BF16), mismatch, 3)
+    region = lax.broadcasted_iota(jnp.int32, (REGIONS, buses), 0) == region_ref[...]
+    part = picked(region.astype(BF16), mismatch, 3)
+    for copy in range(part_out.shape[0] // REGIONS):
+        part_out[copy * REGIONS : (copy + 1) * REGIONS, :] = part
     total = None
     ones = jnp.ones((total_out.shape[0], LANES), BF16)
     for piece in pieces(dispatch + nadual, 3):
@@ -263,7 +263,10 @@
 
 
 def close_kernel(buses_all, param_ref, regional_ref, price_ref, out_ref):
-    out_ref[...] = price_ref[...] + region_term(param_ref[...], regional_ref[...], buses_all)
+    regional = regional_ref[0:REGIONS, :]
+    for part in range(1, regional_ref.shape[0] // REGIONS):
+        regional = regional + regional_ref[part * REGIONS : (part + 1) * REGIONS, :]
+    out_ref[...] = price_ref[...] + region_term(param_ref[...], regional, buses_all)
 
 
 def on_device(
@@ -302,6 +305,7 @@
         out_shape=(shape((1, ends), jnp.int32), shape((ngrid, LANES), jnp.int32)),
         in_specs=[smem(), vmem(), vmem()],
         out_specs=(vmem(), vmem()),
+        compiler_params=pltpu.CompilerParams(vmem_limit_bytes=GRANT),
         name="plan",
     )(line_count, endpoint_owner.reshape(1, ends), endpoint_bus.reshape(1, ends))
     slot = slot.reshape(ends)
@@ -323,6 +327,7 @@
         out_shape=send_shape,
         in_specs=[smem(), vmem()],
         out_specs=vmem(),
+        compiler_params=pltpu.CompilerParams(vmem_limit_bytes=GRANT),
         name="first_send",
     )(asked, volt_init)
 
@@ -338,6 +343,7 @@
             in_specs=[smem(), smem()] + [vmem()] * (len(args) - 2),
             out_specs=[vmem(), vmem()],
             scratch_shapes=[VMEM((4, BLOCK, LANES), F32), VMEM((6, BLOCK, LANES), F32)],
+            compiler_params=pltpu.CompilerParams(vmem_limit_bytes=GRANT),
             name="lines2" if second else "lines1",
         )(*args)
         return out.reshape(ngrid, 3 * CAP, LANES), other
@@ -346,7 +352,8 @@
         outs = [shape((2, buses, LANES), F32), bus_shape]
         if not second:
             outs.append(bus_shape)
-        outs += [shape((ngrid, LANES), F32), shape((nscen, buses), F32)]
+        copies = NEAR if second else 1
+        outs += [shape((copies * REGIONS, LANES), F32), shape((8, buses), F32)]
         outs.append(bus_shape if second else send_shape)
         args = [asked, asked_row, received, volt, bus_param, region_row, load, price_init,
                 na_dual_init] + list(extra)
@@ -355,33 +362,41 @@
             out_shape=outs,
             in_specs=[smem()] + [vmem()] * (len(args) - 1),
             out_specs=[vmem()] * len(outs),
+            compiler_params=pltpu.CompilerParams(vmem_limit_bytes=GRANT),
             name="owner2" if second else "owner1",
         )(*args)
 
-    def regional_sum(part):
-        own = jnp.sum(exchange(part), axis=0, keepdims=True)
-        return exchange(jnp.broadcast_to(own, (ngrid, LANES)))
-
-    def scenario_parts(total):
-        return lax.all_to_all(total, "scen", split_axis=0, concat_axis=0, tiled=True)
+    def doubling_sum(x, axis, size):
+        step = 1
+        while step < size:
+            x = x + lax.ppermute(x, axis, [(i, i ^ step) for i in range(size)])
+            step *= 2
+        return x
 
     out, state = line_call(False, exchange(sent), None)
     volt, disp1, mism1, part, total, sent = owner_call(False, exchange(out), volt_init, ())
-    regional = regional_sum(part)
-    totals = scenario_parts(total)
-    out, dual = line_call(True, exchange(sent), state)
+    arrived = exchange(sent)
+    totals = doubling_sum(total, "scen", nscen)
+    regional = doubling_sum(part, "grid", ngrid)
+    out, dual = line_call(True, arrived, state)
     volt, dispatch, part, total, price = owner_call(
         True, exchange(out), volt, (disp1, mism1, regional, totals)
     )
-    regional = regional_sum(part)
-    commit = jnp.sum(scenario_parts(total), axis=0) / (scen * nscen)
+    commit = doubling_sum(total, "scen", nscen)[0] / (scen * nscen)
+    near = [[i * NEAR + j for j in range(NEAR)] for i in range(ngrid // NEAR)]
+    far = [[i * NEAR + j for i in range(ngrid // NEAR)] for j in range(NEAR)]
+    part = lax.all_to_all(part, "grid", 0, 0, axis_index_groups=near, tiled=True)
+    part = jnp.sum(part.reshape(NEAR, REGIONS, LANES), axis=0)
+    part = jnp.broadcast_to(part[None], (ngrid // NEAR, REGIONS, LANES))
+    parts = lax.all_to_all(part, "grid", 0, 0, axis_index_groups=far, tiled=True)
     price = pl.pallas_call(
         functools.partial(close_kernel, buses_all),
         out_shape=bus_shape,
         in_specs=[vmem()] * 3,
         out_specs=vmem(),
+        compiler_params=pltpu.CompilerParams(vmem_limit_bytes=GRANT),
         name="close",
-    )(bus_param, regional, price)
+    )(bus_param, parts.reshape(ngrid // NEAR * REGIONS, LANES), price)
     return (volt, dual, dispatch, price, commit)
 
 

time: 448 us -> 406 us (0.906)
  waiting for transfers between devices: 295 us -> 193 us
  starting transfers between devices: 38.7 us -> 78.4 us
  blocking collectives: 69.1 us -> 103 us
  Pallas kernels: 30.5 us -> 22.2 us
    all_to_all x7 -> x3, waiting for transfers between devices: 295 us -> 130 us  [exchange(): return lax.all_to_all(x, 'grid', split_axis=0, concat_axis=0, tiled=True)]
    ppermute x0 -> x12, waiting for transfers between devices: none -> 62.3 us  [doubling_sum(): x = x + lax.ppermute(x, axis, [(i, i ^ step) for i in range(size)])]
    ppermute x0 -> x12, starting transfers between devices: none -> 50.7 us  [doubling_sum(): x = x + lax.ppermute(x, axis, [(i, i ^ step) for i in range(size)])]
    all_to_all x2, blocking collectives: 53.6 us -> 93.4 us  [exchange(): return lax.all_to_all(x, 'grid', split_axis=0, concat_axis=0, tiled=True)]
    all_to_all x7 -> x3, starting transfers between devices: 38.7 us -> 16.6 us  [exchange(): return lax.all_to_all(x, 'grid', split_axis=0, concat_axis=0, tiled=True)]
    all_to_all x0 -> x1, starting transfers between devices: none -> 11.1 us  [on_device(): lax.all_to_all(part, 'grid', 0, 0, axis_index_groups=far, tiled=True)]
    all_to_all x2 -> x1, blocking collectives: 15.5 us -> 9.48 us  [on_device(): lax.all_to_all(part, 'grid', 0, 0, axis_index_groups=near, tiled=True)]
  transfers between devices with their start and end apart: 7 -> 16, of which waited for: 7 -> 9; matrix products, arithmetic and copies ran while one was open for 1% -> 0% of each run, Pallas kernels for 1% -> 0%
where the time goes in v2:
time: 406 us; the launch traced here: 405 us
  waiting for transfers between devices  193 us (48%)
  blocking collectives  103 us (25%)
  starting transfers between devices  78.4 us (19%)
  Pallas kernels  22.2 us (5%)
  local copies, waits for them, and re-layouts  6.07 us (1%)
    all_to_all x3, waiting for transfers between devices, exchange(): return lax.all_to_all(x, 'grid', split_axis=0, concat_axis=0, tiled=True)  130 us
    all_to_all x2, blocking collectives, exchange(): return lax.all_to_all(x, 'grid', split_axis=0, concat_axis=0, tiled=True)  93.4 us
    ppermute x12, waiting for transfers between devices, doubling_sum(): x = x + lax.ppermute(x, axis, [(i, i ^ step) for i in range(size)])  62.3 us
    ppermute x12, starting transfers between devices, doubling_sum(): x = x + lax.ppermute(x, axis, [(i, i ^ step) for i in range(size)])  50.7 us
    all_to_all x3, starting transfers between devices, exchange(): return lax.all_to_all(x, 'grid', split_axis=0, concat_axis=0, tiled=True)  16.6 us
    all_to_all x1, starting transfers between devices, on_device(): lax.all_to_all(part, 'grid', 0, 0, axis_index_groups=far, tiled=True)  11.1 us
    pallas_call x2, Pallas kernels, line_call(): pl.pallas_call(functools.partial(line_kernel, second), out_shape=outs, in...  9.89 us
    all_to_all x1, blocking collectives, on_device(): lax.all_to_all(part, 'grid', 0, 0, axis_index_groups=near, tiled=True)  9.48 us
  transfers between devices with their start and end apart: 16, of which 9 were waited for; matrix products, arithmetic and copies ran while one was open for 0% of the time, Pallas kernels for 0%

profile of v2, /device:TPU:6, one launch (start us, length us, event | category | flops | bytes accessed | tf_op | source)
XLA Modules:
  0.0 404.6 jit_solution(14968152970385579409)
XLA Ops:
  1.3 0.7 copy-done.12
  2.0 0.7 copy-done.13
  2.6 0.4 plan.1
  3.1 33.2 %all_to_all.45 = s32[64,1,128]{2,1,0:T(1,128)S(1)} all-to-all(s32[64,1,128]{2,1,0:T(1,128)S(1)} %bitcast.34), channel_id=1, replica_groups=mesh['grid'=64,'scen'=8] {'grid'}, dimensions={0} | all-to-all | bytes 65536 | tf_op jit(solution)/shard_map/all_to_all | solution.py:301
  36.2 0.9 copy-done.2
  37.2 4.1 %first_send.1 = f32[64,32,128]{2,1,0:T(8,128)} custom-call(s32[64,128]{1,0:T(8,128)S(1)} %bitcast.28, f32[2,256,128]{2,1,0:T(8,128)S(1)} %copy-done.2), custom_call_target="tpu_custom_call" | custom-call | tf_op jit(solution)/shard_map/first_send/pallas_call | solution.py:325
  41.3 4.7 %all-to-all-start.1 = ((f32[64,32,128]{2,1,0:T(8,128)}), f32[64,32,128]{2,1,0:T(8,128)S(1)}, u32[]{:S(2)}, u32[]{:S(2)}) async-start(f32[64,32,128]{2,1,0:T(8,128)} %first_send.1), calls=%async_computation.1 | async-start | bytes 2097152 | tf_op jit(solution)/shard_map/all_to_all | solution.py:301
  46.0 0.1 copy.32.refs_0_.refs_1_
  46.1 54.0 %all-to-all-done.1 = f32[64,32,128]{2,1,0:T(8,128)S(1)} async-done(((f32[64,32,128]{2,1,0:T(8,128)}), f32[64,32,128]{2,1,0:T(8,128)S(1)}, u32[]{:S(2)}, u32[]{:S(2)}) %all-to-all-start.1) | async-done | bytes 1048608 | tf_op jit(solution)/shard_map/all_to_all | solution.py:301
  100.1 4.3 %lines1.1 = (f32[3072,128]{1,0:T(8,128)S(1)}, f32[4,256,128]{2,1,0:T(8,128)S(1)}) custom-call(s32[1]{0:T(128)S(6)} %copy.37.count_ref, s32[512]{0:T(512)S(1)} %bitcast.37, f32[2048,128]{1,0:T(8,128)S(1)} %bitcast.25, f32[4,256,128]{2,1,0:T(8,128)S(1)} %copy-done, f32[256,2]{1,0:T(8,128)S(1)} %copy.32.refs_0_.refs_1_), custom_call_target="tpu_custom_call" | custom-call | tf_op jit(solution)/shard_map/lines1/pallas_call | solution.py:340
  104.3 1.2 copy-done.1
  105.5 0.8 copy-done.7
  106.3 0.0 copy-start.17
  106.3 0.0 copy-start.18
  106.4 6.0 %all-to-all-start.2 = ((f32[64,48,128]{2,1,0:T(8,128)}), f32[64,48,128]{2,1,0:T(8,128)S(1)}, u32[]{:S(2)}, u32[]{:S(2)}) async-start(f32[64,48,128]{2,1,0:T(8,128)} %bitcast.27), calls=%async_computation.2 | async-start | bytes 3145728 | tf_op jit(solution)/shard_map/all_to_all | solution.py:301
  112.5 0.1 copy.33.param_ref
  112.6 0.1 reshape.51.row_ref
  112.7 76.5 %all-to-all-done.2.recv_ref = f32[64,48,128]{2,1,0:T(8,128)S(1)} async-done(((f32[64,48,128]{2,1,0:T(8,128)}), f32[64,48,128]{2,1,0:T(8,128)S(1)}, u32[]{:S(2)}, u32[]{:S(2)}) %all-to-all-start.2) | async-done | bytes 1572896 | tf_op jit(solution)/shard_map/all_to_all | solution.py:301
  189.2 4.3 %owner1.1 = (f32[2,256,128]{2,1,0:T(8,128)S(1)}, f32[256,128]{1,0:T(8,128)S(1)}, f32[256,128]{1,0:T(8,128)S(1)}, f32[16,128]{1,0:T(8,128)S(1)}, f32[8,256]{1,0:T(8,128)S(1)}, /*index=5*/f32[64,32,128]{2,1,0:T(8,128)S(1)}) custom-call(s32[64,128]{1,0:T(8,128)S(1)} %bitcast.30, s32[1,1024]{1,0:T(1,128)S(1)} %reshape.51.row_ref, ...), custom_call_target="tpu_custom_call" | custom-call | tf_op jit(solution)/shard_map/owner1/pallas_call | solution.py:360
  193.5 0.7 copy-done.9
  194.2 60.2 %all_to_all.46 = f32[64,32,128]{2,1,0:T(8,128)S(1)} all-to-all(f32[64,32,128]{2,1,0:T(8,128)S(1)} %get-tuple-element.25), channel_id=1, replica_groups=mesh['grid'=64,'scen'=8] {'grid'}, dimensions={0} | all-to-all | bytes 2097152 | tf_op jit(solution)/shard_map/all_to_all | solution.py:301
  254.4 5.6 %lines2.1 = (f32[3072,128]{1,0:T(8,128)}, f32[4,256,128]{2,1,0:T(8,128)}) custom-call(s32[1]{0:T(128)S(6)} %copy.37.count_ref, s32[512]{0:T(512)S(1)} %bitcast.38, f32[2048,128]{1,0:T(8,128)S(1)} %bitcast.26, f32[4,256,128]{2,1,0:T(8,128)S(1)} %copy-done, f32[4,256,128]{2,1,0:T(8,128)S(1)} %copy-done.8, f32[256,2]{1,0:T(8,128)S(1)} %copy.32.refs_0_.refs_1_), custom_call_target="tpu_custom_call" | custom-call | tf_op jit(solution)/shard_map/lines2/pallas_call | solution.py:340
  260.1 6.0 %all-to-all-start.4 = ((f32[64,48,128]{2,1,0:T(8,128)}), f32[64,48,128]{2,1,0:T(8,128)S(1)}, u32[]{:S(2)}, u32[]{:S(2)}) async-start(f32[64,48,128]{2,1,0:T(8,128)} %bitcast.19), calls=%async_computation.4 | async-start | bytes 3145728 | tf_op jit(solution)/shard_map/all_to_all | solution.py:301
  266.0 3.5 collective-permute-start
  269.5 2.1 collective-permute-done
  271.6 5.1 %collective-permute-start.1 = (f32[16,128]{1,0:T(8,128)S(1)}, f32[16,128]{1,0:T(8,128)S(1)}, u32[]{:S(2)}, u32[]{:S(2)}) collective-permute-start(f32[16,128]{1,0:T(8,128)S(1)} %add.36), channel_id=1, source_target_pairs={{0,16},{8,24},{16,0},{24,8},{32,48},{40,56},{48,32},{56,40},{64,80... | collective-permute-start | bytes 24584 | tf_op jit(solution)/shard_map/ppermute | solution.py:372
  276.7 1.9 collective-permute-done.1
  278.6 3.5 collective-permute-start.2
  282.1 1.9 collective-permute-start.6
  284.0 48.0 %collective-permute-done.2 = f32[16,128]{1,0:T(8,128)S(1)} collective-permute-done((f32[16,128]{1,0:T(8,128)S(1)}, f32[16,128]{1,0:T(8,128)S(1)}, u32[]{:S(2)}, u32[]{:S(2)}) %collective-permute-start.2) | collective-permute-done | bytes 8224 | tf_op jit(solution)/shard_map/ppermute | solution.py:372
  332.1 4.2 %collective-permute-start.3 = (f32[16,128]{1,0:T(8,128)S(1)}, f32[16,128]{1,0:T(8,128)S(1)}, u32[]{:S(2)}, u32[]{:S(2)}) collective-permute-start(f32[16,128]{1,0:T(8,128)S(1)} %add.38), channel_id=1, source_target_pairs={{0,64},{8,72},{16,80},{24,88},{32,96},{40,104},{48,112},{56,120},{... | collective-permute-start | bytes 24584 | tf_op jit(solution)/shard_map/ppermute | solution.py:372
  336.2 2.7 collective-permute-start.7
  339.0 7.2 %collective-permute-start.4 = (f32[16,128]{1,0:T(8,128)S(1)}, f32[16,128]{1,0:T(8,128)S(1)}, u32[]{:S(2)}, u32[]{:S(2)}) collective-permute-start(f32[16,128]{1,0:T(8,128)S(1)} %add.39), channel_id=1, source_target_pairs={{0,128},{8,136},{16,144},{24,152},{32,160},{40,168},{48,176},{56,1... | collective-permute-start | bytes 24584 | tf_op jit(solution)/shard_map/ppermute | solution.py:372
  346.3 3.0 collective-permute-start.8
  349.3 11.6 %collective-permute-start.5 = (f32[16,128]{1,0:T(8,128)S(1)}, f32[16,128]{1,0:T(8,128)S(1)}, u32[]{:S(2)}, u32[]{:S(2)}) collective-permute-start(f32[16,128]{1,0:T(8,128)S(1)} %add.40), channel_id=1, source_target_pairs={{0,256},{8,264},{16,272},{24,280},{32,288},{40,296},{48,304},{56,3... | collective-permute-start | bytes 24584 | tf_op jit(solution)/shard_map/ppermute | solution.py:372
  361.0 2.6 collective-permute-done.5
  363.6 2.7 owner2.1
  366.3 9.5 %all_to_all.47 = f32[4,16,128]{2,1,0:T(8,128)S(1)} all-to-all(f32[4,16,128]{2,1,0:T(8,128)S(1)} %bitcast.33), channel_id=1, replica_groups={{0,8,16,24},{32,40,48,56},{64,72,80,88},{96,104,112,120},{128,136,144,1..., dimensions={0} | all-to-all | bytes 65536 | tf_op jit(solution)/shard_map/all_to_all | solution.py:388
  375.8 0.7 broadcast_in_dim.2
  376.4 11.1 %all-to-all-start.6 = ((f32[16,16,128]{2,1,0:T(8,128)}), f32[16,16,128]{2,1,0:T(8,128)S(1)}, u32[]{:S(2)}, u32[]{:S(2)}) async-start(f32[16,16,128]{2,1,0:T(8,128)} %broadcast_in_dim.2), calls=%async_computation.6 | async-start | bytes 262144 | tf_op jit(solution)/shard_map/all_to_all | solution.py:391
  387.5 1.9 collective-permute-start.9
  389.5 1.1 collective-permute-done.9
  390.6 2.7 collective-permute-start.10
  393.3 2.8 collective-permute-done.10
  396.1 3.3 collective-permute-start.11
  399.4 3.7 collective-permute-done.11
  403.2 0.6 fusion
  403.7 0.9 close.1
  (59 shorter events, 0.2 us)
Async XLA Ops:
  1.3 0.7 copy-start.12
  2.0 0.7 copy-start.13
  36.2 1.0 copy-start.2
  37.2 8.7 %copy-start.20 = (f32[256]{0:T(256)S(1)}, f32[256]{0:T(256)}, u32[]{:S(2)}) copy-start(f32[256]{0:T(256)} %param.20) | copy-start | bytes 3076
  37.2 8.8 %copy-start.21 = (f32[256]{0:T(256)S(1)}, f32[256]{0:T(256)}, u32[]{:S(2)}) copy-start(f32[256]{0:T(256)} %param.19) | copy-start | bytes 3076
  37.2 62.9 %copy-start = (f32[4,256,128]{2,1,0:T(8,128)S(1)}, f32[4,256,128]{2,1,0:T(8,128)}, u32[]{:S(2)}) copy-start(f32[4,256,128]{2,1,0:T(8,128)} %dual_ref.3) | copy-start | bytes 1572868
  41.3 58.8 %all-to-all-start.1 = ((f32[64,32,128]{2,1,0:T(8,128)}), f32[64,32,128]{2,1,0:T(8,128)S(1)}, u32[]{:S(2)}, u32[]{:S(2)}) async-start(f32[64,32,128]{2,1,0:T(8,128)} %first_send.1), calls=%async_computation.1 | async-start | bytes 2097152 | tf_op jit(solution)/shard_map/all_to_all | solution.py:301
  104.3 1.2 copy-start.1
  105.5 0.8 copy-start.7
  106.3 6.1 %copy-start.11 = (s32[256]{0:T(256)S(1)}, s32[256]{0:T(256)}, u32[]{:S(2)}) copy-start(s32[256]{0:T(256)} %param.24) | copy-start | bytes 3076
  106.3 6.1 %copy-start.14 = (f32[256]{0:T(256)S(1)}, f32[256]{0:T(256)}, u32[]{:S(2)}) copy-start(f32[256]{0:T(256)} %param.26) | copy-start | bytes 3076
  106.3 6.1 %copy-start.15 = (f32[256]{0:T(256)S(1)}, f32[256]{0:T(256)}, u32[]{:S(2)}) copy-start(f32[256]{0:T(256)} %param.25) | copy-start | bytes 3076
  106.3 6.1 %copy-start.16 = (f32[256]{0:T(256)S(1)}, f32[256]{0:T(256)}, u32[]{:S(2)}) copy-start(f32[256]{0:T(256)} %param.31) | copy-start | bytes 3076
  106.3 6.1 %copy-start.17 = (f32[256]{0:T(256)S(1)}, f32[256]{0:T(256)}, u32[]{:S(2)}) copy-start(f32[256]{0:T(256)} %param.32) | copy-start | bytes 3076
  106.3 6.1 %copy-start.18 = (f32[256]{0:T(256)S(1)}, f32[256]{0:T(256)}, u32[]{:S(2)}) copy-start(f32[256]{0:T(256)} %param.33) | copy-start | bytes 3076
  106.3 6.1 %copy-start.19 = (f32[256]{0:T(256)S(1)}, f32[256]{0:T(256)}, u32[]{:S(2)}) copy-start(f32[256]{0:T(256)} %param.30) | copy-start | bytes 3076
  106.3 82.9 %copy-start.3 = (f32[2,256,128]{2,1,0:T(8,128)S(1)}, f32[2,256,128]{2,1,0:T(8,128)}, u32[]{:S(2)}) copy-start(f32[2,256,128]{2,1,0:T(8,128)} %volt_ref.3) | copy-start | bytes 786436
  106.3 82.9 %copy-start.4 = (f32[256,128]{1,0:T(8,128)S(1)}, f32[256,128]{1,0:T(8,128)}, u32[]{:S(2)}) copy-start(f32[256,128]{1,0:T(8,128)} %load_ref.3) | copy-start | bytes 393220
  106.4 82.9 %copy-start.5 = (f32[256,128]{1,0:T(8,128)S(1)}, f32[256,128]{1,0:T(8,128)}, u32[]{:S(2)}) copy-start(f32[256,128]{1,0:T(8,128)} %price_ref.3) | copy-start | bytes 393220
  106.4 82.9 %copy-start.6 = (f32[256,128]{1,0:T(8,128)S(1)}, f32[256,128]{1,0:T(8,128)}, u32[]{:S(2)}) copy-start(f32[256,128]{1,0:T(8,128)} %nadual_ref.3) | copy-start | bytes 393220
  106.4 82.8 %all-to-all-start.2 = ((f32[64,48,128]{2,1,0:T(8,128)}), f32[64,48,128]{2,1,0:T(8,128)S(1)}, u32[]{:S(2)}, u32[]{:S(2)}) async-start(f32[64,48,128]{2,1,0:T(8,128)} %bitcast.27), calls=%async_computation.2 | async-start | bytes 3145728 | tf_op jit(solution)/shard_map/all_to_all | solution.py:301
  193.5 0.7 copy-start.9
  194.2 60.2 %copy-start.8 = (f32[4,256,128]{2,1,0:T(8,128)S(1)}, f32[4,256,128]{2,1,0:T(8,128)}, u32[]{:S(2)}) copy-start(f32[4,256,128]{2,1,0:T(8,128)} %copy-done.7) | copy-start | bytes 1572868
  260.1 103.5 %copy-start.10 = (f32[256,128]{1,0:T(8,128)S(1)}, f32[256,128]{1,0:T(8,128)}, u32[]{:S(2)}) copy-start(f32[256,128]{1,0:T(8,128)} %copy-done.9) | copy-start | bytes 393220
  260.1 103.5 %all-to-all-start.4 = ((f32[64,48,128]{2,1,0:T(8,128)}), f32[64,48,128]{2,1,0:T(8,128)S(1)}, u32[]{:S(2)}, u32[]{:S(2)}) async-start(f32[64,48,128]{2,1,0:T(8,128)} %bitcast.19), calls=%async_computation.4 | async-start | bytes 3145728 | tf_op jit(solution)/shard_map/all_to_all | solution.py:301
  266.0 5.5 %collective-permute-start = (f32[16,128]{1,0:T(8,128)S(1)}, f32[16,128]{1,0:T(8,128)S(1)}, u32[]{:S(2)}, u32[]{:S(2)}) collective-permute-start(f32[16,128]{1,0:T(8,128)S(1)} %get-tuple-element.31), channel_id=1, source_target_pairs={{0,8},{8,0},{16,24},{24,16},{32,40},{40,32},{48,56},{56,48},{64,72... | collective-permute-start | bytes 24584 | tf_op jit(solution)/shard_map/ppermute | solution.py:372
  271.6 7.1 %collective-permute-start.1 = (f32[16,128]{1,0:T(8,128)S(1)}, f32[16,128]{1,0:T(8,128)S(1)}, u32[]{:S(2)}, u32[]{:S(2)}) collective-permute-start(f32[16,128]{1,0:T(8,128)S(1)} %add.36), channel_id=1, source_target_pairs={{0,16},{8,24},{16,0},{24,8},{32,48},{40,56},{48,32},{56,40},{64,80... | collective-permute-start | bytes 24584 | tf_op jit(solution)/shard_map/ppermute | solution.py:372
  278.6 53.4 %collective-permute-start.2 = (f32[16,128]{1,0:T(8,128)S(1)}, f32[16,128]{1,0:T(8,128)S(1)}, u32[]{:S(2)}, u32[]{:S(2)}) collective-permute-start(f32[16,128]{1,0:T(8,128)S(1)} %add.37), channel_id=1, source_target_pairs={{0,32},{8,40},{16,48},{24,56},{32,0},{40,8},{48,16},{56,24},{64,96... | collective-permute-start | bytes 24584 | tf_op jit(solution)/shard_map/ppermute | solution.py:372
  282.1 54.1 %collective-permute-start.6 = (f32[8,256]{1,0:T(8,128)S(1)}, f32[8,256]{1,0:T(8,128)S(1)}, u32[]{:S(2)}, u32[]{:S(2)}) collective-permute-start(f32[8,256]{1,0:T(8,128)S(1)} %get-tuple-element.32), channel_id=1, source_target_pairs={{0,1},{1,0},{2,3},{3,2},{4,5},{5,4},{6,7},{7,6},{8,9},{9,8},{10,11... | collective-permute-start | bytes 24584 | tf_op jit(solution)/shard_map/ppermute | solution.py:372
  332.1 6.9 %collective-permute-start.3 = (f32[16,128]{1,0:T(8,128)S(1)}, f32[16,128]{1,0:T(8,128)S(1)}, u32[]{:S(2)}, u32[]{:S(2)}) collective-permute-start(f32[16,128]{1,0:T(8,128)S(1)} %add.38), channel_id=1, source_target_pairs={{0,64},{8,72},{16,80},{24,88},{32,96},{40,104},{48,112},{56,120},{... | collective-permute-start | bytes 24584 | tf_op jit(solution)/shard_map/ppermute | solution.py:372
  336.2 10.0 %collective-permute-start.7 = (f32[8,256]{1,0:T(8,128)S(1)}, f32[8,256]{1,0:T(8,128)S(1)}, u32[]{:S(2)}, u32[]{:S(2)}) collective-permute-start(f32[8,256]{1,0:T(8,128)S(1)} %add.42), channel_id=1, source_target_pairs={{0,2},{1,3},{2,0},{3,1},{4,6},{5,7},{6,4},{7,5},{8,10},{9,11},{10,... | collective-permute-start | bytes 24584 | tf_op jit(solution)/shard_map/ppermute | solution.py:372
  339.0 10.3 %collective-permute-start.4 = (f32[16,128]{1,0:T(8,128)S(1)}, f32[16,128]{1,0:T(8,128)S(1)}, u32[]{:S(2)}, u32[]{:S(2)}) collective-permute-start(f32[16,128]{1,0:T(8,128)S(1)} %add.39), channel_id=1, source_target_pairs={{0,128},{8,136},{16,144},{24,152},{32,160},{40,168},{48,176},{56,1... | collective-permute-start | bytes 24584 | tf_op jit(solution)/shard_map/ppermute | solution.py:372
  346.3 14.7 %collective-permute-start.8 = (f32[8,256]{1,0:T(8,128)S(1)}, f32[8,256]{1,0:T(8,128)S(1)}, u32[]{:S(2)}, u32[]{:S(2)}) collective-permute-start(f32[8,256]{1,0:T(8,128)S(1)} %add.43), channel_id=1, source_target_pairs={{0,4},{1,5},{2,6},{3,7},{4,0},{5,1},{6,2},{7,3},{8,12},{9,13},{10,... | collective-permute-start | bytes 24584 | tf_op jit(solution)/shard_map/ppermute | solution.py:372
  349.3 14.3 %collective-permute-start.5 = (f32[16,128]{1,0:T(8,128)S(1)}, f32[16,128]{1,0:T(8,128)S(1)}, u32[]{:S(2)}, u32[]{:S(2)}) collective-permute-start(f32[16,128]{1,0:T(8,128)S(1)} %add.40), channel_id=1, source_target_pairs={{0,256},{8,264},{16,272},{24,280},{32,288},{40,296},{48,304},{56,3... | collective-permute-start | bytes 24584 | tf_op jit(solution)/shard_map/ppermute | solution.py:372
  376.4 27.3 %all-to-all-start.6 = ((f32[16,16,128]{2,1,0:T(8,128)}), f32[16,16,128]{2,1,0:T(8,128)S(1)}, u32[]{:S(2)}, u32[]{:S(2)}) async-start(f32[16,16,128]{2,1,0:T(8,128)} %broadcast_in_dim.2), calls=%async_computation.6 | async-start | bytes 262144 | tf_op jit(solution)/shard_map/all_to_all | solution.py:391
  387.5 3.1 collective-permute-start.9
  390.6 5.5 %collective-permute-start.10 = (f32[8,256]{1,0:T(8,128)S(1)}, f32[8,256]{1,0:T(8,128)S(1)}, u32[]{:S(2)}, u32[]{:S(2)}) collective-permute-start(f32[8,256]{1,0:T(8,128)S(1)} %add.45), channel_id=1, source_target_pairs={{0,2},{1,3},{2,0},{3,1},{4,6},{5,7},{6,4},{7,5},{8,10},{9,11},{10,... | collective-permute-start | bytes 24584 | tf_op jit(solution)/shard_map/ppermute | solution.py:372
  396.1 7.0 %collective-permute-start.11 = (f32[8,256]{1,0:T(8,128)S(1)}, f32[8,256]{1,0:T(8,128)S(1)}, u32[]{:S(2)}, u32[]{:S(2)}) collective-permute-start(f32[8,256]{1,0:T(8,128)S(1)} %add.46), channel_id=1, source_target_pairs={{0,4},{1,5},{2,6},{3,7},{4,0},{5,1},{6,2},{7,3},{8,12},{9,13},{10,... | collective-permute-start | bytes 24584 | tf_op jit(solution)/shard_map/ppermute | solution.py:372

commit v3 on v2

--- a/solution.py
+++ b/solution.py
@@ -366,18 +366,30 @@
             name="owner2" if second else "owner1",
         )(*args)
 
+    def near_sum(x, axis, size, step, count):
+        parts = [
+            lax.ppermute(x, axis, [(i, i ^ (k * step)) for i in range(size)])
+            for k in range(1, count)
+        ]
+        return sum(parts, x)
+
     def doubling_sum(x, axis, size):
         step = 1
         while step < size:
-            x = x + lax.ppermute(x, axis, [(i, i ^ step) for i in range(size)])
+            x = near_sum(x, axis, size, step, 2)
             step *= 2
         return x
 
     out, state = line_call(False, exchange(sent), None)
     volt, disp1, mism1, part, total, sent = owner_call(False, exchange(out), volt_init, ())
     arrived = exchange(sent)
+    for step in range(1, NEAR):
+        if step & (step - 1) == 0:
+            part = near_sum(part, "grid", ngrid, step, 2)
+    part = near_sum(part, "grid", ngrid, NEAR, NEAR)
+    arrived, part = lax.optimization_barrier((arrived, part))
     totals = doubling_sum(total, "scen", nscen)
-    regional = doubling_sum(part, "grid", ngrid)
+    regional = near_sum(part, "grid", ngrid, NEAR * NEAR, ngrid // (NEAR * NEAR))
     out, dual = line_call(True, arrived, state)
     volt, dispatch, part, total, price = owner_call(
         True, exchange(out), volt, (disp1, mism1, regional, totals)

time: 406 us -> 379 us (0.933)
  blocking collectives: 103 us -> 42.7 us
  waiting for transfers between devices: 193 us -> 227 us
    all_to_all x2 -> x1, blocking collectives: 93.4 us -> 33.2 us  [exchange(): return lax.all_to_all(x, 'grid', split_axis=0, concat_axis=0, tiled=True)]
    ppermute x12 -> x14, waiting for transfers between devices: 62.3 us -> 87.7 us  [near_sum(): lax.ppermute(x, axis, [(i, i ^ k * step) for i in range(size)])]
    all_to_all x3 -> x4, waiting for transfers between devices: 130 us -> 139 us  [exchange(): return lax.all_to_all(x, 'grid', split_axis=0, concat_axis=0, tiled=True)]
    all_to_all x1, starting transfers between devices: 11.1 us -> 3.51 us  [on_device(): lax.all_to_all(part, 'grid', 0, 0, axis_index_groups=far, tiled=True)]
    all_to_all x3 -> x4, starting transfers between devices: 16.6 us -> 22.8 us  [exchange(): return lax.all_to_all(x, 'grid', split_axis=0, concat_axis=0, tiled=True)]
    ppermute x12 -> x14, starting transfers between devices: 50.7 us -> 51.5 us  [near_sum(): lax.ppermute(x, axis, [(i, i ^ k * step) for i in range(size)])]
  transfers between devices with their start and end apart: 16 -> 19, of which waited for: 9 -> 13; matrix products, arithmetic and copies ran while one was open for 0% -> 0% of each run, Pallas kernels for 0% -> 0%
where the time goes in v3:
time: 379 us; the launch traced here: 378 us
  waiting for transfers between devices  227 us (60%)
  starting transfers between devices  77.8 us (21%)
  blocking collectives  42.7 us (11%)
  Pallas kernels  22.8 us (6%)
  local copies, waits for them, and re-layouts  6.04 us (2%)
    all_to_all x4, waiting for transfers between devices, exchange(): return lax.all_to_all(x, 'grid', split_axis=0, concat_axis=0, tiled=True)  139 us
    ppermute x14, waiting for transfers between devices, near_sum(): lax.ppermute(x, axis, [(i, i ^ k * step) for i in range(size)])  87.7 us
    ppermute x14, starting transfers between devices, near_sum(): lax.ppermute(x, axis, [(i, i ^ k * step) for i in range(size)])  51.5 us
    all_to_all x1, blocking collectives, exchange(): return lax.all_to_all(x, 'grid', split_axis=0, concat_axis=0, tiled=True)  33.2 us
    all_to_all x4, starting transfers between devices, exchange(): return lax.all_to_all(x, 'grid', split_axis=0, concat_axis=0, tiled=True)  22.8 us
    pallas_call x2, Pallas kernels, line_call(): pl.pallas_call(functools.partial(line_kernel, second), out_shape=outs, in...  9.89 us
    all_to_all x1, blocking collectives, on_device(): lax.all_to_all(part, 'grid', 0, 0, axis_index_groups=near, tiled=True)  9.49 us
  transfers between devices with their start and end apart: 19, of which 13 were waited for; matrix products, arithmetic and copies ran while one was open for 0% of the time, Pallas kernels for 0%

profile of v3, /device:TPU:6, one launch (start us, length us, event | category | flops | bytes accessed | tf_op | source)
XLA Modules:
  0.0 378.2 jit_solution(7364698780382760619)
XLA Ops:
  1.3 0.7 copy-done.12
  2.0 0.7 copy-done.13
  3.1 33.2 %all_to_all.45 = s32[64,1,128]{2,1,0:T(1,128)S(1)} all-to-all(s32[64,1,128]{2,1,0:T(1,128)S(1)} %bitcast.34), channel_id=1, replica_groups=mesh['grid'=64,'scen'=8] {'grid'}, dimensions={0} | all-to-all | bytes 65536 | tf_op jit(solution)/shard_map/all_to_all | solution.py:301
  36.2 0.9 copy-done.2
  37.2 4.1 %first_send.1 = f32[64,32,128]{2,1,0:T(8,128)} custom-call(s32[64,128]{1,0:T(8,128)S(1)} %bitcast.28, f32[2,256,128]{2,1,0:T(8,128)S(1)} %copy-done.2), custom_call_target="tpu_custom_call" | custom-call | tf_op jit(solution)/shard_map/first_send/pallas_call | solution.py:325
  41.3 4.7 %all-to-all-start.1 = ((f32[64,32,128]{2,1,0:T(8,128)}), f32[64,32,128]{2,1,0:T(8,128)S(1)}, u32[]{:S(2)}, u32[]{:S(2)}) async-start(f32[64,32,128]{2,1,0:T(8,128)} %first_send.1), calls=%async_computation.1 | async-start | bytes 2097152 | tf_op jit(solution)/shard_map/all_to_all | solution.py:301
  46.1 54.0 %all-to-all-done.1 = f32[64,32,128]{2,1,0:T(8,128)S(1)} async-done(((f32[64,32,128]{2,1,0:T(8,128)}), f32[64,32,128]{2,1,0:T(8,128)S(1)}, u32[]{:S(2)}, u32[]{:S(2)}) %all-to-all-start.1) | async-done | bytes 1048608 | tf_op jit(solution)/shard_map/all_to_all | solution.py:301
  100.1 4.3 %lines1.1 = (f32[3072,128]{1,0:T(8,128)S(1)}, f32[4,256,128]{2,1,0:T(8,128)S(1)}) custom-call(s32[1]{0:T(128)S(6)} %copy.37.count_ref, s32[512]{0:T(512)S(1)} %bitcast.37, f32[2048,128]{1,0:T(8,128)S(1)} %bitcast.26, f32[4,256,128]{2,1,0:T(8,128)S(1)} %copy-done, f32[256,2]{1,0:T(8,128)S(1)} %copy.32.refs_0_.refs_1_), custom_call_target="tpu_custom_call" | custom-call | tf_op jit(solution)/shard_map/lines1/pallas_call | solution.py:340
  104.3 1.2 copy-done.1
  105.5 0.8 copy-done.7
  106.4 6.0 %all-to-all-start.2 = ((f32[64,48,128]{2,1,0:T(8,128)}), f32[64,48,128]{2,1,0:T(8,128)S(1)}, u32[]{:S(2)}, u32[]{:S(2)}) async-start(f32[64,48,128]{2,1,0:T(8,128)} %bitcast.27), calls=%async_computation.2 | async-start | bytes 3145728 | tf_op jit(solution)/shard_map/all_to_all | solution.py:301
  112.7 76.5 %all-to-all-done.2.recv_ref = f32[64,48,128]{2,1,0:T(8,128)S(1)} async-done(((f32[64,48,128]{2,1,0:T(8,128)}), f32[64,48,128]{2,1,0:T(8,128)S(1)}, u32[]{:S(2)}, u32[]{:S(2)}) %all-to-all-start.2) | async-done | bytes 1572896 | tf_op jit(solution)/shard_map/all_to_all | solution.py:301
  189.3 4.8 %owner1.1 = (f32[2,256,128]{2,1,0:T(8,128)S(1)}, f32[256,128]{1,0:T(8,128)S(1)}, f32[256,128]{1,0:T(8,128)S(1)}, f32[16,128]{1,0:T(8,128)S(1)}, f32[8,256]{1,0:T(8,128)S(1)}, /*index=5*/f32[64,32,128]{2,1,0:T(8,128)}) custom-call(s32[64,128]{1,0:T(8,128)S(1)} %bitcast.30, s32[1,1024]{1,0:T(1,128)S(1)} %reshape.51.row_ref, ...), custom_call_target="tpu_custom_call" | custom-call | tf_op jit(solution)/shard_map/owner1/pallas_call | solution.py:360
  194.1 0.7 copy-done.9
  194.8 6.0 %all-to-all-start.3 = ((f32[64,32,128]{2,1,0:T(8,128)}), f32[64,32,128]{2,1,0:T(8,128)S(1)}, u32[]{:S(2)}, u32[]{:S(2)}) async-start(f32[64,32,128]{2,1,0:T(8,128)} %get-tuple-element.27), calls=%async_computation.3 | async-start | bytes 2097152 | tf_op jit(solution)/shard_map/all_to_all | solution.py:301
  200.7 3.5 collective-permute-start
  204.2 2.1 collective-permute-done
  206.3 5.0 %collective-permute-start.1 = (f32[16,128]{1,0:T(8,128)S(1)}, f32[16,128]{1,0:T(8,128)S(1)}, u32[]{:S(2)}, u32[]{:S(2)}) collective-permute-start(f32[16,128]{1,0:T(8,128)S(1)} %add.42), channel_id=1, source_target_pairs={{0,16},{8,24},{16,0},{24,8},{32,48},{40,56},{48,32},{56,40},{64,80... | collective-permute-start | bytes 24584 | tf_op jit(solution)/shard_map/ppermute | solution.py:371
  211.3 2.1 collective-permute-done.1
  213.3 5.3 %collective-permute-start.4 = (f32[16,128]{1,0:T(8,128)S(1)}, f32[16,128]{1,0:T(8,128)S(1)}, u32[]{:S(2)}, u32[]{:S(2)}) collective-permute-start(f32[16,128]{1,0:T(8,128)S(1)} %add.43), channel_id=1, source_target_pairs={{0,96},{8,104},{16,112},{24,120},{32,64},{40,72},{48,80},{56,88},{... | collective-permute-start | bytes 24584 | tf_op jit(solution)/shard_map/ppermute | solution.py:371
  218.6 1.9 collective-permute-start.3
  220.5 2.9 collective-permute-start.2
  223.5 23.2 %collective-permute-done.4 = f32[16,128]{1,0:T(8,128)S(1)} collective-permute-done((f32[16,128]{1,0:T(8,128)S(1)}, f32[16,128]{1,0:T(8,128)S(1)}, u32[]{:S(2)}, u32[]{:S(2)}) %collective-permute-start.4) | collective-permute-done | bytes 8224 | tf_op jit(solution)/shard_map/ppermute | solution.py:371
  246.7 8.5 %all-to-all-done.3 = f32[64,32,128]{2,1,0:T(8,128)S(1)} async-done(((f32[64,32,128]{2,1,0:T(8,128)}), f32[64,32,128]{2,1,0:T(8,128)S(1)}, u32[]{:S(2)}, u32[]{:S(2)}) %all-to-all-start.3) | async-done | bytes 1048608 | tf_op jit(solution)/shard_map/all_to_all | solution.py:301
  255.2 5.6 %lines2.1 = (f32[3072,128]{1,0:T(8,128)}, f32[4,256,128]{2,1,0:T(8,128)}) custom-call(s32[1]{0:T(128)S(6)} %copy.37.count_ref, s32[512]{0:T(512)S(1)} %bitcast.38, f32[2048,128]{1,0:T(8,128)S(1)} %bitcast.25, f32[4,256,128]{2,1,0:T(8,128)S(1)} %copy-done, f32[4,256,128]{2,1,0:T(8,128)S(1)} %copy-done.8, f32[256,2]{1,0:T(8,128)S(1)} %copy.32.refs_0_.refs_1_), custom_call_target="tpu_custom_call" | custom-call | tf_op jit(solution)/shard_map/lines2/pallas_call | solution.py:340
  260.8 6.2 %all-to-all-start.4 = ((f32[64,48,128]{2,1,0:T(8,128)}), f32[64,48,128]{2,1,0:T(8,128)S(1)}, u32[]{:S(2)}, u32[]{:S(2)}) async-start(f32[64,48,128]{2,1,0:T(8,128)} %bitcast.19), calls=%async_computation.4 | async-start | bytes 3145728 | tf_op jit(solution)/shard_map/all_to_all | solution.py:301
  267.0 1.9 collective-permute-start.8
  269.0 1.1 collective-permute-done.8
  270.1 2.7 collective-permute-start.9
  272.8 2.8 collective-permute-done.9
  275.6 3.3 collective-permute-start.10
  278.9 7.6 %collective-permute-start.7 = (f32[16,128]{1,0:T(8,128)S(1)}, f32[16,128]{1,0:T(8,128)S(1)}, u32[]{:S(2)}, u32[]{:S(2)}) collective-permute-start(f32[16,128]{1,0:T(8,128)S(1)} %add_add_fusion.1), channel_id=1, source_target_pairs={{0,384},{8,392},{16,400},{24,408},{32,416},{40,424},{48,432},{56,4... | collective-permute-start | bytes 24584 | tf_op jit(solution)/shard_map/ppermute | solution.py:371
  286.5 7.1 %collective-permute-start.6 = (f32[16,128]{1,0:T(8,128)S(1)}, f32[16,128]{1,0:T(8,128)S(1)}, u32[]{:S(2)}, u32[]{:S(2)}) collective-permute-start(f32[16,128]{1,0:T(8,128)S(1)} %add_add_fusion.1), channel_id=1, source_target_pairs={{0,256},{8,264},{16,272},{24,280},{32,288},{40,296},{48,304},{56,3... | collective-permute-start | bytes 24584 | tf_op jit(solution)/shard_map/ppermute | solution.py:371
  293.6 2.4 collective-permute-start.5
  296.0 39.6 %collective-permute-done.7 = f32[16,128]{1,0:T(8,128)S(1)} collective-permute-done((f32[16,128]{1,0:T(8,128)S(1)}, f32[16,128]{1,0:T(8,128)S(1)}, u32[]{:S(2)}, u32[]{:S(2)}) %collective-permute-start.7) | collective-permute-done | bytes 8224 | tf_op jit(solution)/shard_map/ppermute | solution.py:371
  335.6 9.1 %collective-permute-done.6 = f32[16,128]{1,0:T(8,128)S(1)} collective-permute-done((f32[16,128]{1,0:T(8,128)S(1)}, f32[16,128]{1,0:T(8,128)S(1)}, u32[]{:S(2)}, u32[]{:S(2)}) %collective-permute-start.6) | collective-permute-done | bytes 8224 | tf_op jit(solution)/shard_map/ppermute | solution.py:371
  344.7 2.7 owner2.1
  347.4 9.5 %all_to_all.46 = f32[4,16,128]{2,1,0:T(8,128)S(1)} all-to-all(f32[4,16,128]{2,1,0:T(8,128)S(1)} %bitcast.33), channel_id=1, replica_groups={{0,8,16,24},{32,40,48,56},{64,72,80,88},{96,104,112,120},{128,136,144,1..., dimensions={0} | all-to-all | bytes 65536 | tf_op jit(solution)/shard_map/all_to_all | solution.py:400
  356.9 0.7 broadcast_in_dim.2
  357.5 3.5 all-to-all-start.6
  361.1 1.9 collective-permute-start.11
  363.0 1.1 collective-permute-done.11
  364.1 2.7 collective-permute-start.12
  366.9 2.8 collective-permute-done.12
  369.7 3.3 collective-permute-start.13
  373.0 3.7 collective-permute-done.13
  376.7 0.6 fusion
  377.3 0.9 close.1
  (62 shorter events, 0.9 us)
Async XLA Ops:
  1.3 0.7 copy-start.12
  2.0 0.7 copy-start.13
  36.2 1.0 copy-start.2
  37.2 8.8 %copy-start.20 = (f32[256]{0:T(256)S(1)}, f32[256]{0:T(256)}, u32[]{:S(2)}) copy-start(f32[256]{0:T(256)} %param.20) | copy-start | bytes 3076
  37.2 8.8 %copy-start.21 = (f32[256]{0:T(256)S(1)}, f32[256]{0:T(256)}, u32[]{:S(2)}) copy-start(f32[256]{0:T(256)} %param.19) | copy-start | bytes 3076
  37.2 62.9 %copy-start = (f32[4,256,128]{2,1,0:T(8,128)S(1)}, f32[4,256,128]{2,1,0:T(8,128)}, u32[]{:S(2)}) copy-start(f32[4,256,128]{2,1,0:T(8,128)} %dual_ref.3) | copy-start | bytes 1572868
  41.3 58.8 %all-to-all-start.1 = ((f32[64,32,128]{2,1,0:T(8,128)}), f32[64,32,128]{2,1,0:T(8,128)S(1)}, u32[]{:S(2)}, u32[]{:S(2)}) async-start(f32[64,32,128]{2,1,0:T(8,128)} %first_send.1), calls=%async_computation.1 | async-start | bytes 2097152 | tf_op jit(solution)/shard_map/all_to_all | solution.py:301
  104.3 1.2 copy-start.1
  105.5 0.8 copy-start.7
  106.3 6.1 %copy-start.11 = (s32[256]{0:T(256)S(1)}, s32[256]{0:T(256)}, u32[]{:S(2)}) copy-start(s32[256]{0:T(256)} %param.24) | copy-start | bytes 3076
  106.3 6.1 %copy-start.14 = (f32[256]{0:T(256)S(1)}, f32[256]{0:T(256)}, u32[]{:S(2)}) copy-start(f32[256]{0:T(256)} %param.26) | copy-start | bytes 3076
  106.3 6.1 %copy-start.15 = (f32[256]{0:T(256)S(1)}, f32[256]{0:T(256)}, u32[]{:S(2)}) copy-start(f32[256]{0:T(256)} %param.25) | copy-start | bytes 3076
  106.3 6.1 %copy-start.16 = (f32[256]{0:T(256)S(1)}, f32[256]{0:T(256)}, u32[]{:S(2)}) copy-start(f32[256]{0:T(256)} %param.31) | copy-start | bytes 3076
  106.3 6.1 %copy-start.17 = (f32[256]{0:T(256)S(1)}, f32[256]{0:T(256)}, u32[]{:S(2)}) copy-start(f32[256]{0:T(256)} %param.32) | copy-start | bytes 3076
  106.3 6.1 %copy-start.18 = (f32[256]{0:T(256)S(1)}, f32[256]{0:T(256)}, u32[]{:S(2)}) copy-start(f32[256]{0:T(256)} %param.33) | copy-start | bytes 3076
  106.3 6.1 %copy-start.19 = (f32[256]{0:T(256)S(1)}, f32[256]{0:T(256)}, u32[]{:S(2)}) copy-start(f32[256]{0:T(256)} %param.30) | copy-start | bytes 3076
  106.4 82.9 %copy-start.3 = (f32[2,256,128]{2,1,0:T(8,128)S(1)}, f32[2,256,128]{2,1,0:T(8,128)}, u32[]{:S(2)}) copy-start(f32[2,256,128]{2,1,0:T(8,128)} %volt_ref.3) | copy-start | bytes 786436
  106.4 82.9 %copy-start.4 = (f32[256,128]{1,0:T(8,128)S(1)}, f32[256,128]{1,0:T(8,128)}, u32[]{:S(2)}) copy-start(f32[256,128]{1,0:T(8,128)} %load_ref.3) | copy-start | bytes 393220
  106.4 82.9 %copy-start.5 = (f32[256,128]{1,0:T(8,128)S(1)}, f32[256,128]{1,0:T(8,128)}, u32[]{:S(2)}) copy-start(f32[256,128]{1,0:T(8,128)} %price_ref.3) | copy-start | bytes 393220
  106.4 82.9 %copy-start.6 = (f32[256,128]{1,0:T(8,128)S(1)}, f32[256,128]{1,0:T(8,128)}, u32[]{:S(2)}) copy-start(f32[256,128]{1,0:T(8,128)} %nadual_ref.3) | copy-start | bytes 393220
  106.4 82.8 %all-to-all-start.2 = ((f32[64,48,128]{2,1,0:T(8,128)}), f32[64,48,128]{2,1,0:T(8,128)S(1)}, u32[]{:S(2)}, u32[]{:S(2)}) async-start(f32[64,48,128]{2,1,0:T(8,128)} %bitcast.27), calls=%async_computation.2 | async-start | bytes 3145728 | tf_op jit(solution)/shard_map/all_to_all | solution.py:301
  194.1 0.7 copy-start.9
  194.8 60.4 %copy-start.8 = (f32[4,256,128]{2,1,0:T(8,128)S(1)}, f32[4,256,128]{2,1,0:T(8,128)}, u32[]{:S(2)}) copy-start(f32[4,256,128]{2,1,0:T(8,128)} %copy-done.7) | copy-start | bytes 1572868
  194.8 60.4 %all-to-all-start.3 = ((f32[64,32,128]{2,1,0:T(8,128)}), f32[64,32,128]{2,1,0:T(8,128)S(1)}, u32[]{:S(2)}, u32[]{:S(2)}) async-start(f32[64,32,128]{2,1,0:T(8,128)} %get-tuple-element.27), calls=%async_computation.3 | async-start | bytes 2097152 | tf_op jit(solution)/shard_map/all_to_all | solution.py:301
  200.7 5.5 %collective-permute-start = (f32[16,128]{1,0:T(8,128)S(1)}, f32[16,128]{1,0:T(8,128)S(1)}, u32[]{:S(2)}, u32[]{:S(2)}) collective-permute-start(f32[16,128]{1,0:T(8,128)S(1)} %get-tuple-element.28), channel_id=1, source_target_pairs={{0,8},{8,0},{16,24},{24,16},{32,40},{40,32},{48,56},{56,48},{64,72... | collective-permute-start | bytes 24584 | tf_op jit(solution)/shard_map/ppermute | solution.py:371
  206.3 7.1 %collective-permute-start.1 = (f32[16,128]{1,0:T(8,128)S(1)}, f32[16,128]{1,0:T(8,128)S(1)}, u32[]{:S(2)}, u32[]{:S(2)}) collective-permute-start(f32[16,128]{1,0:T(8,128)S(1)} %add.42), channel_id=1, source_target_pairs={{0,16},{8,24},{16,0},{24,8},{32,48},{40,56},{48,32},{56,40},{64,80... | collective-permute-start | bytes 24584 | tf_op jit(solution)/shard_map/ppermute | solution.py:371
  213.3 33.4 %collective-permute-start.4 = (f32[16,128]{1,0:T(8,128)S(1)}, f32[16,128]{1,0:T(8,128)S(1)}, u32[]{:S(2)}, u32[]{:S(2)}) collective-permute-start(f32[16,128]{1,0:T(8,128)S(1)} %add.43), channel_id=1, source_target_pairs={{0,96},{8,104},{16,112},{24,120},{32,64},{40,72},{48,80},{56,88},{... | collective-permute-start | bytes 24584 | tf_op jit(solution)/shard_map/ppermute | solution.py:371
  218.6 28.1 %collective-permute-start.3 = (f32[16,128]{1,0:T(8,128)S(1)}, f32[16,128]{1,0:T(8,128)S(1)}, u32[]{:S(2)}, u32[]{:S(2)}) collective-permute-start(f32[16,128]{1,0:T(8,128)S(1)} %add.43), channel_id=1, source_target_pairs={{0,64},{8,72},{16,80},{24,88},{32,96},{40,104},{48,112},{56,120},{... | collective-permute-start | bytes 24584 | tf_op jit(solution)/shard_map/ppermute | solution.py:371
  220.5 26.2 %collective-permute-start.2 = (f32[16,128]{1,0:T(8,128)S(1)}, f32[16,128]{1,0:T(8,128)S(1)}, u32[]{:S(2)}, u32[]{:S(2)}) collective-permute-start(f32[16,128]{1,0:T(8,128)S(1)} %add.43), channel_id=1, source_target_pairs={{0,32},{8,40},{16,48},{24,56},{32,0},{40,8},{48,16},{56,24},{64,96... | collective-permute-start | bytes 24584 | tf_op jit(solution)/shard_map/ppermute | solution.py:371
  260.8 83.9 %copy-start.10 = (f32[256,128]{1,0:T(8,128)S(1)}, f32[256,128]{1,0:T(8,128)}, u32[]{:S(2)}) copy-start(f32[256,128]{1,0:T(8,128)} %copy-done.9) | copy-start | bytes 393220
  260.8 83.9 %all-to-all-start.4 = ((f32[64,48,128]{2,1,0:T(8,128)}), f32[64,48,128]{2,1,0:T(8,128)S(1)}, u32[]{:S(2)}, u32[]{:S(2)}) async-start(f32[64,48,128]{2,1,0:T(8,128)} %bitcast.19), calls=%async_computation.4 | async-start | bytes 3145728 | tf_op jit(solution)/shard_map/all_to_all | solution.py:301
  267.0 3.1 collective-permute-start.8
  270.1 5.5 %collective-permute-start.9 = (f32[8,256]{1,0:T(8,128)S(1)}, f32[8,256]{1,0:T(8,128)S(1)}, u32[]{:S(2)}, u32[]{:S(2)}) collective-permute-start(f32[8,256]{1,0:T(8,128)S(1)} %add.50), channel_id=1, source_target_pairs={{0,2},{1,3},{2,0},{3,1},{4,6},{5,7},{6,4},{7,5},{8,10},{9,11},{10,... | collective-permute-start | bytes 24584 | tf_op jit(solution)/shard_map/ppermute | solution.py:371
  275.6 20.4 %collective-permute-start.10 = (f32[8,256]{1,0:T(8,128)S(1)}, f32[8,256]{1,0:T(8,128)S(1)}, u32[]{:S(2)}, u32[]{:S(2)}) collective-permute-start(f32[8,256]{1,0:T(8,128)S(1)} %add.51), channel_id=1, source_target_pairs={{0,4},{1,5},{2,6},{3,7},{4,0},{5,1},{6,2},{7,3},{8,12},{9,13},{10,... | collective-permute-start | bytes 24584 | tf_op jit(solution)/shard_map/ppermute | solution.py:371
  278.9 56.6 %collective-permute-start.7 = (f32[16,128]{1,0:T(8,128)S(1)}, f32[16,128]{1,0:T(8,128)S(1)}, u32[]{:S(2)}, u32[]{:S(2)}) collective-permute-start(f32[16,128]{1,0:T(8,128)S(1)} %add_add_fusion.1), channel_id=1, source_target_pairs={{0,384},{8,392},{16,400},{24,408},{32,416},{40,424},{48,432},{56,4... | collective-permute-start | bytes 24584 | tf_op jit(solution)/shard_map/ppermute | solution.py:371
  286.5 58.1 %collective-permute-start.6 = (f32[16,128]{1,0:T(8,128)S(1)}, f32[16,128]{1,0:T(8,128)S(1)}, u32[]{:S(2)}, u32[]{:S(2)}) collective-permute-start(f32[16,128]{1,0:T(8,128)S(1)} %add_add_fusion.1), channel_id=1, source_target_pairs={{0,256},{8,264},{16,272},{24,280},{32,288},{40,296},{48,304},{56,3... | collective-permute-start | bytes 24584 | tf_op jit(solution)/shard_map/ppermute | solution.py:371
  293.6 51.0 %collective-permute-start.5 = (f32[16,128]{1,0:T(8,128)S(1)}, f32[16,128]{1,0:T(8,128)S(1)}, u32[]{:S(2)}, u32[]{:S(2)}) collective-permute-start(f32[16,128]{1,0:T(8,128)S(1)} %add_add_fusion.1), channel_id=1, source_target_pairs={{0,128},{8,136},{16,144},{24,152},{32,160},{40,168},{48,176},{56,1... | collective-permute-start | bytes 24584 | tf_op jit(solution)/shard_map/ppermute | solution.py:371
  357.5 19.7 %all-to-all-start.6 = ((f32[16,16,128]{2,1,0:T(8,128)}), f32[16,16,128]{2,1,0:T(8,128)S(1)}, u32[]{:S(2)}, u32[]{:S(2)}) async-start(f32[16,16,128]{2,1,0:T(8,128)} %broadcast_in_dim.2), calls=%async_computation.6 | async-start | bytes 262144 | tf_op jit(solution)/shard_map/all_to_all | solution.py:403
  361.1 3.1 collective-permute-start.11
  364.1 5.5 %collective-permute-start.12 = (f32[8,256]{1,0:T(8,128)S(1)}, f32[8,256]{1,0:T(8,128)S(1)}, u32[]{:S(2)}, u32[]{:S(2)}) collective-permute-start(f32[8,256]{1,0:T(8,128)S(1)} %add.53), channel_id=1, source_target_pairs={{0,2},{1,3},{2,0},{3,1},{4,6},{5,7},{6,4},{7,5},{8,10},{9,11},{10,... | collective-permute-start | bytes 24584 | tf_op jit(solution)/shard_map/ppermute | solution.py:371
  369.7 7.0 %collective-permute-start.13 = (f32[8,256]{1,0:T(8,128)S(1)}, f32[8,256]{1,0:T(8,128)S(1)}, u32[]{:S(2)}, u32[]{:S(2)}) collective-permute-start(f32[8,256]{1,0:T(8,128)S(1)} %add.54), channel_id=1, source_target_pairs={{0,4},{1,5},{2,6},{3,7},{4,0},{5,1},{6,2},{7,3},{8,12},{9,13},{10,... | collective-permute-start | bytes 24584 | tf_op jit(solution)/shard_map/ppermute | solution.py:371

commit v4 on v3

--- a/solution.py
+++ b/solution.py
@@ -12,7 +12,7 @@
 CAP = 16
 LANES = 128
 REGION_GAIN = 10.0
-BLOCK = 32
+BLOCK = 16
 NEAR = 4
 GRANT = 16 * 2**20
 
@@ -73,14 +73,16 @@
 
 
 def send_rows(asked_ref, volt_ref, out_ref):
+    buses = volt_ref.shape[1]
+
     def step(o, carry):
         for r in range(CAP):
-            bus = jnp.maximum(asked_ref[o, r] - 1, 0)
+            bus = (asked_ref[o, r] - 1) & (buses - 1)
             for c in range(2):
                 out_ref[o, c * CAP + r : c * CAP + r + 1, :] = volt_ref[c, pl.ds(bus, 1), :]
         return carry
 
-    lax.fori_loop(0, out_ref.shape[0], step, 0)
+    lax.fori_loop(0, out_ref.shape[0], step, 0, unroll=4)
 
 
 def first_send_kernel(asked_ref, volt_ref, out_ref):
@@ -140,25 +142,32 @@
 
 def line_kernel(second, count_ref, slot_ref, arrived_ref, dual_ref, *refs):
     if second:
-        previous_ref, param_ref, out_ref, dual_out_ref, near_ref, term_ref = refs
+        previous_ref, param_ref, out_ref, dual_out_ref, *scratch = refs
     else:
-        param_ref, out_ref, state_ref, near_ref, term_ref = refs
+        param_ref, out_ref, state_ref, *scratch = refs
+    near_refs, term_refs = scratch[:2], scratch[2:]
     lines = dual_ref.shape[1]
-
-    def step(block, carry):
+    blocks = lines // BLOCK
+
+    def gather(block, near_ref):
+        for end in range(2):
+            for j in range(BLOCK):
+                slot = slot_ref[end * lines + block * BLOCK + j]
+                start = slot + (slot & -CAP)
+                for c in range(2):
+                    near_ref[2 * end + c, j : j + 1, :] = arrived_ref[pl.ds(start + c * CAP, 1), :]
+
+    def scatter(block, term_ref):
+        for end in range(2):
+            for j in range(BLOCK):
+                slot = slot_ref[end * lines + block * BLOCK + j]
+                start = slot + 2 * (slot & -CAP)
+                for c in range(3):
+                    out_ref[pl.ds(start + c * CAP, 1), :] = term_ref[3 * end + c, j : j + 1, :]
+
+    def solve(block, near_ref, term_ref):
         base = pl.multiple_of(block * BLOCK, BLOCK)
         rows = pl.ds(base, BLOCK)
-        starts = []
-        for end in range(2):
-            for j in range(BLOCK):
-                slot = slot_ref[end * lines + base + j]
-                high = slot & -CAP
-                starts.append((slot + high, slot + high + high))
-        for end in range(2):
-            for j in range(BLOCK):
-                start = starts[end * BLOCK + j][0]
-                for c in range(2):
-                    near_ref[2 * end + c, j : j + 1, :] = arrived_ref[pl.ds(start + c * CAP, 1), :]
         near = [near_ref[i] for i in range(4)]
         dual = [dual_ref[i, rows, :] for i in range(4)]
         line_id = lax.broadcasted_iota(jnp.int32, (BLOCK, LANES), 0) + base
@@ -184,15 +193,22 @@
         ]
         for i in range(6):
             term_ref[i] = jnp.where(live, terms[i], 0.0)
-        for end in range(2):
-            for j in range(BLOCK):
-                start = starts[end * BLOCK + j][1]
-                for c in range(3):
-                    out_ref[pl.ds(start + c * CAP, 1), :] = term_ref[3 * end + c, j : j + 1, :]
+
+    def step(pair, carry):
+        block = 2 * pair
+        scatter(lax.rem(block + blocks - 1, blocks), term_refs[1])
+        gather(block + 1, near_refs[1])
+        solve(block, near_refs[0], term_refs[0])
+        gather(lax.rem(block + 2, blocks), near_refs[0])
+        scatter(block, term_refs[0])
+        solve(block + 1, near_refs[1], term_refs[1])
         return carry
 
     out_ref[...] = jnp.zeros_like(out_ref)
-    lax.fori_loop(0, lines // BLOCK, step, 0)
+    term_refs[1][...] = jnp.zeros_like(term_refs[1])
+    gather(0, near_refs[0])
+    lax.fori_loop(0, blocks // 2, step, 0)
+    scatter(blocks - 1, term_refs[1])
 
 
 def column(param, index):
@@ -206,32 +222,41 @@
     return total * (REGION_GAIN * REGIONS / buses_all)
 
 
-def owner_kernel(second, buses_all, scen_all, asked_ref, row_ref, recv_ref, volt_ref, param_ref,
-                 region_ref, load_ref, price_ref, nadual_ref, *refs):
-    if second:
-        (disp1_ref, mism1_ref, regional_ref, totals_ref,
-         volt_out, disp_out, part_out, total_out, price_out) = refs
-    else:
-        volt_out, disp_out, mism_out, part_out, total_out, send_out = refs
-    buses = volt_ref.shape[1]
-    devices = recv_ref.shape[0]
-    slots = devices * CAP
+def bus_hits(row_ref, buses):
+    slots = row_ref.shape[1]
     ids = lax.broadcasted_iota(jnp.int32, (buses, slots), 0) + 1
-    hits = (ids == row_ref[...]).astype(BF16)
-    rows = [recv_ref[:, c * CAP : (c + 1) * CAP, :].reshape(slots, LANES) for c in range(3)]
-    pair = picked(hits, jnp.concatenate(rows[:2], axis=1), 2)
-    flows = pieces(rows[2], 2)
-    ones = jnp.ones((slots, LANES), BF16)
-    last = jnp.dot(hits, jnp.concatenate([flows[0], ones], axis=1), preferred_element_type=F32)
-    net = last[:, :LANES] + jnp.dot(hits, flows[1], preferred_element_type=F32)
-    degree = last[:, LANES:]
+    return (ids == row_ref[...]).astype(BF16)
+
+
+def slot_rows(recv_ref, c):
+    return recv_ref[:, c * CAP : (c + 1) * CAP, :].reshape(recv_ref.shape[0] * CAP, LANES)
+
+
+def volt_kernel(send, asked_ref, row_ref, recv_ref, volt_ref, param_ref, volt_out, *refs):
+    hits = bus_hits(row_ref, volt_ref.shape[1])
+    rows = jnp.concatenate([slot_rows(recv_ref, 0), slot_rows(recv_ref, 1)], axis=1)
+    pair = picked(hits, rows, 2)
+    ones = jnp.ones((hits.shape[1], LANES), BF16)
+    degree = jnp.dot(hits, ones, preferred_element_type=F32)
     param = param_ref[...]
     weight = column(param, 0)
     inverse = 1.0 / (degree + weight)
     volt_out[0] = (pair[:, :LANES] + weight * column(param, 1)) * inverse
     volt_out[1] = (pair[:, LANES:] + weight * volt_ref[1]) * inverse
-    if not second:
-        send_rows(asked_ref, volt_out, send_out)
+    if send:
+        send_rows(asked_ref, volt_out, refs[0])
+
+
+def dispatch_kernel(second, buses_all, scen_all, row_ref, recv_ref, param_ref, region_ref,
+                    load_ref, price_ref, nadual_ref, *refs):
+    if second:
+        (disp1_ref, mism1_ref, regional_ref, totals_ref,
+         disp_out, part_out, total_out, price_out) = refs
+    else:
+        disp_out, mism_out, part_out, total_out = refs
+    buses = load_ref.shape[0]
+    net = picked(bus_hits(row_ref, buses), slot_rows(recv_ref, 2), 2)
+    param = param_ref[...]
     load, price, nadual = load_ref[...], price_ref[...], nadual_ref[...]
     if second:
         commit = jnp.transpose(totals_ref[...])[:, 0:1] / scen_all
@@ -342,28 +367,38 @@
             out_shape=outs,
             in_specs=[smem(), smem()] + [vmem()] * (len(args) - 2),
             out_specs=[vmem(), vmem()],
-            scratch_shapes=[VMEM((4, BLOCK, LANES), F32), VMEM((6, BLOCK, LANES), F32)],
+            scratch_shapes=[VMEM((4, BLOCK, LANES), F32)] * 2 + [VMEM((6, BLOCK, LANES), F32)] * 2,
             compiler_params=pltpu.CompilerParams(vmem_limit_bytes=GRANT),
             name="lines2" if second else "lines1",
         )(*args)
         return out.reshape(ngrid, 3 * CAP, LANES), other
 
-    def owner_call(second, received, volt, extra):
-        outs = [shape((2, buses, LANES), F32), bus_shape]
-        if not second:
-            outs.append(bus_shape)
+    def volt_call(send, received, volt):
+        outs = [shape((2, buses, LANES), F32)] + ([send_shape] if send else [])
+        return pl.pallas_call(
+            functools.partial(volt_kernel, send),
+            out_shape=outs,
+            in_specs=[smem()] + [vmem()] * 4,
+            out_specs=[vmem()] * len(outs),
+            compiler_params=pltpu.CompilerParams(vmem_limit_bytes=GRANT),
+            name="volt1" if send else "volt2",
+        )(asked, asked_row, received, volt, bus_param)
+
+    def dispatch_call(second, received, extra):
+        outs = [bus_shape] if second else [bus_shape] * 2
         copies = NEAR if second else 1
         outs += [shape((copies * REGIONS, LANES), F32), shape((8, buses), F32)]
-        outs.append(bus_shape if second else send_shape)
-        args = [asked, asked_row, received, volt, bus_param, region_row, load, price_init,
-                na_dual_init] + list(extra)
+        if second:
+            outs.append(bus_shape)
+        args = [asked_row, received, bus_param, region_row, load, price_init, na_dual_init]
+        args += list(extra)
         return pl.pallas_call(
-            functools.partial(owner_kernel, second, buses_all, scen * nscen),
+            functools.partial(dispatch_kernel, second, buses_all, scen * nscen),
             out_shape=outs,
-            in_specs=[smem()] + [vmem()] * (len(args) - 1),
+            in_specs=[vmem()] * len(args),
             out_specs=[vmem()] * len(outs),
             compiler_params=pltpu.CompilerParams(vmem_limit_bytes=GRANT),
-            name="owner2" if second else "owner1",
+            name="dispatch2" if second else "dispatch1",
         )(*args)
 
     def near_sum(x, axis, size, step, count):
@@ -373,16 +408,18 @@
         ]
         return sum(parts, x)
 
-    def doubling_sum(x, axis, size):
+    def doubling_sum(x, axis, count):
         step = 1
-        while step < size:
-            x = near_sum(x, axis, size, step, 2)
+        while step < count:
+            x = near_sum(x, axis, lax.axis_size(axis), step, 2)
             step *= 2
         return x
 
     out, state = line_call(False, exchange(sent), None)
-    volt, disp1, mism1, part, total, sent = owner_call(False, exchange(out), volt_init, ())
+    received = exchange(out)
+    volt, sent = volt_call(True, received, volt_init)
     arrived = exchange(sent)
+    disp1, mism1, part, total = dispatch_call(False, received, ())
     for step in range(1, NEAR):
         if step & (step - 1) == 0:
             part = near_sum(part, "grid", ngrid, step, 2)
@@ -391,16 +428,18 @@
     totals = doubling_sum(total, "scen", nscen)
     regional = near_sum(part, "grid", ngrid, NEAR * NEAR, ngrid // (NEAR * NEAR))
     out, dual = line_call(True, arrived, state)
-    volt, dispatch, part, total, price = owner_call(
-        True, exchange(out), volt, (disp1, mism1, regional, totals)
-    )
-    commit = doubling_sum(total, "scen", nscen)[0] / (scen * nscen)
+    received = exchange(out)
+    dispatch, part, total, price = dispatch_call(True, received, (disp1, mism1, regional, totals))
     near = [[i * NEAR + j for j in range(NEAR)] for i in range(ngrid // NEAR)]
     far = [[i * NEAR + j for i in range(ngrid // NEAR)] for j in range(NEAR)]
     part = lax.all_to_all(part, "grid", 0, 0, axis_index_groups=near, tiled=True)
+    total = doubling_sum(total, "scen", nscen // 2)
+    part, total = lax.optimization_barrier((part, total))
     part = jnp.sum(part.reshape(NEAR, REGIONS, LANES), axis=0)
     part = jnp.broadcast_to(part[None], (ngrid // NEAR, REGIONS, LANES))
     parts = lax.all_to_all(part, "grid", 0, 0, axis_index_groups=far, tiled=True)
+    commit = near_sum(total, "scen", nscen, nscen // 2, 2)[0] / (scen * nscen)
+    (volt,) = volt_call(False, received, volt)
     price = pl.pallas_call(
         functools.partial(close_kernel, buses_all),
         out_shape=bus_shape,

time: 379 us -> 379 us (level)
  blocking collectives: 42.7 us -> 33.2 us
  local copies, waits for them, and re-layouts: 6.04 us -> 13.4 us
  starting transfers between devices: 77.8 us -> 82 us
    all_to_all x1 -> x0, blocking collectives: 9.49 us -> none  [on_device(): lax.all_to_all(part, 'grid', 0, 0, axis_index_groups=near, tiled=True)]
    unnamed x44 -> x62, local copies, waits for them, and re-layouts: 5 us -> 12.3 us
    ppermute x14, waiting for transfers between devices: 87.7 us -> 80.4 us  [near_sum(): lax.ppermute(x, axis, [(i, i ^ k * step) for i in range(size)])]
    all_to_all x1, waiting for transfers between devices: 0.01 us -> 6.49 us  [on_device(): lax.all_to_all(part, 'grid', 0, 0, axis_index_groups=far, tiled=True)]
    all_to_all x0 -> x1, starting transfers between devices: none -> 4.25 us  [on_device(): lax.all_to_all(part, 'grid', 0, 0, axis_index_groups=near, tiled=True)]
    pallas_call x2 -> x4, Pallas kernels: 7.49 us -> 7.66 us  [the longest x2 5.53 us: volt_call(): pl.pallas_call(functools.partial(volt_kernel, send), out_shape=outs, in_s...]
  transfers between devices with their start and end apart: 19 -> 20, of which waited for: 13 -> 14; matrix products, arithmetic and copies ran while one was open for 0% -> 0% of each run, Pallas kernels for 0% -> 1%
where the time goes in v4:
time: 379 us; the launch traced here: 377 us
  waiting for transfers between devices  226 us (60%)
  starting transfers between devices  82 us (22%)
  blocking collectives  33.2 us (9%)
  Pallas kernels  20.3 us (5%)
  local copies, waits for them, and re-layouts  13.4 us (4%)
    all_to_all x4, waiting for transfers between devices, exchange(): return lax.all_to_all(x, 'grid', split_axis=0, concat_axis=0, tiled=True)  139 us
    ppermute x14, waiting for transfers between devices, near_sum(): lax.ppermute(x, axis, [(i, i ^ k * step) for i in range(size)])  80.4 us
    ppermute x14, starting transfers between devices, near_sum(): lax.ppermute(x, axis, [(i, i ^ k * step) for i in range(size)])  51.5 us
    all_to_all x1, blocking collectives, exchange(): return lax.all_to_all(x, 'grid', split_axis=0, concat_axis=0, tiled=True)  33.2 us
    all_to_all x4, starting transfers between devices, exchange(): return lax.all_to_all(x, 'grid', split_axis=0, concat_axis=0, tiled=True)  22.7 us
    unnamed x62, local copies, waits for them, and re-layouts  12.3 us
    pallas_call x2, Pallas kernels, line_call(): pl.pallas_call(functools.partial(line_kernel, second), out_shape=outs, in...  7.82 us
  transfers between devices with their start and end apart: 20, of which 14 were waited for; matrix products, arithmetic and copies ran while one was open for 0% of the time, Pallas kernels for 1%

profile of v4, /device:TPU:6, one launch (start us, length us, event | category | flops | bytes accessed | tf_op | source)
XLA Modules:
  0.0 377.1 jit_solution(8292537729837572800)
XLA Ops:
  3.1 33.2 %all_to_all.48 = s32[64,1,128]{2,1,0:T(1,128)S(1)} all-to-all(s32[64,1,128]{2,1,0:T(1,128)S(1)} %bitcast.36), channel_id=1, replica_groups=mesh['grid'=64,'scen'=8] {'grid'}, dimensions={0} | all-to-all | bytes 65536 | tf_op jit(solution)/shard_map/all_to_all | solution.py:326
  36.2 0.9 copy-done.4
  37.2 3.5 first_send.1
  40.7 4.7 %all-to-all-start.1 = ((f32[64,32,128]{2,1,0:T(8,128)}), f32[64,32,128]{2,1,0:T(8,128)S(1)}, u32[]{:S(2)}, u32[]{:S(2)}) async-start(f32[64,32,128]{2,1,0:T(8,128)} %first_send.1), calls=%async_computation.1 | async-start | bytes 2097152 | tf_op jit(solution)/shard_map/all_to_all | solution.py:326
  45.5 54.0 %all-to-all-done.1 = f32[64,32,128]{2,1,0:T(8,128)S(1)} async-done(((f32[64,32,128]{2,1,0:T(8,128)}), f32[64,32,128]{2,1,0:T(8,128)S(1)}, u32[]{:S(2)}, u32[]{:S(2)}) %all-to-all-start.1) | async-done | bytes 1048608 | tf_op jit(solution)/shard_map/all_to_all | solution.py:326
  99.5 3.5 lines1.1
  103.0 1.2 copy-done.2
  105.1 6.0 %all-to-all-start.2 = ((f32[64,48,128]{2,1,0:T(8,128)}), f32[64,48,128]{2,1,0:T(8,128)S(1)}, u32[]{:S(2)}, u32[]{:S(2)}) async-start(f32[64,48,128]{2,1,0:T(8,128)} %bitcast.30), calls=%async_computation.2 | async-start | bytes 3145728 | tf_op jit(solution)/shard_map/all_to_all | solution.py:326
  111.4 76.5 %all-to-all-done.2.recv_ref = f32[64,48,128]{2,1,0:T(8,128)S(1)} async-done(((f32[64,48,128]{2,1,0:T(8,128)}), f32[64,48,128]{2,1,0:T(8,128)S(1)}, u32[]{:S(2)}, u32[]{:S(2)}) %all-to-all-start.2) | async-done | bytes 1572896 | tf_op jit(solution)/shard_map/all_to_all | solution.py:326
  187.9 3.1 volt1.1
  191.1 1.0 copy-done.3
  192.8 5.8 %all-to-all-start.3 = ((f32[64,32,128]{2,1,0:T(8,128)}), f32[64,32,128]{2,1,0:T(8,128)S(1)}, u32[]{:S(2)}, u32[]{:S(2)}) async-start(f32[64,32,128]{2,1,0:T(8,128)} %copy-done.3), calls=%async_computation.3 | async-start | bytes 2097152 | tf_op jit(solution)/shard_map/all_to_all | solution.py:326
  199.5 0.9 copy-done.10
  203.3 3.5 collective-permute-start
  206.8 2.1 collective-permute-done
  209.0 4.9 %collective-permute-start.1 = (f32[16,128]{1,0:T(8,128)S(1)}, f32[16,128]{1,0:T(8,128)S(1)}, u32[]{:S(2)}, u32[]{:S(2)}) collective-permute-start(f32[16,128]{1,0:T(8,128)S(1)} %add.42), channel_id=1, source_target_pairs={{0,16},{8,24},{16,0},{24,8},{32,48},{40,56},{48,32},{56,40},{64,80... | collective-permute-start | bytes 24584 | tf_op jit(solution)/shard_map/ppermute | solution.py:406
  213.9 2.2 collective-permute-done.1
  216.1 5.2 %collective-permute-start.4 = (f32[16,128]{1,0:T(8,128)S(1)}, f32[16,128]{1,0:T(8,128)S(1)}, u32[]{:S(2)}, u32[]{:S(2)}) collective-permute-start(f32[16,128]{1,0:T(8,128)S(1)} %add.43), channel_id=1, source_target_pairs={{0,96},{8,104},{16,112},{24,120},{32,64},{40,72},{48,80},{56,88},{... | collective-permute-start | bytes 24584 | tf_op jit(solution)/shard_map/ppermute | solution.py:406
  221.3 1.9 collective-permute-start.3
  223.2 3.0 collective-permute-start.2
  226.2 18.4 %collective-permute-done.4 = f32[16,128]{1,0:T(8,128)S(1)} collective-permute-done((f32[16,128]{1,0:T(8,128)S(1)}, f32[16,128]{1,0:T(8,128)S(1)}, u32[]{:S(2)}, u32[]{:S(2)}) %collective-permute-start.4) | collective-permute-done | bytes 8224 | tf_op jit(solution)/shard_map/ppermute | solution.py:406
  244.6 8.5 %all-to-all-done.3 = f32[64,32,128]{2,1,0:T(8,128)S(1)} async-done(((f32[64,32,128]{2,1,0:T(8,128)}), f32[64,32,128]{2,1,0:T(8,128)S(1)}, u32[]{:S(2)}, u32[]{:S(2)}) %all-to-all-start.3) | async-done | bytes 1048608 | tf_op jit(solution)/shard_map/all_to_all | solution.py:326
  253.1 1.0 copy-done.7
  254.1 4.3 %lines2.1 = (f32[3072,128]{1,0:T(8,128)S(1)}, f32[4,256,128]{2,1,0:T(8,128)}) custom-call(s32[1]{0:T(128)S(6)} %copy.39.count_ref, s32[512]{0:T(512)S(1)} %bitcast.40, f32[2048,128]{1,0:T(8,128)S(1)} %bitcast.27, f32[4,256,128]{2,1,0:T(8,128)S(1)} %copy-done, f32[4,256,128]{2,1,0:T(8,128)S(1)} %copy-done.7, f32[256,2]{1,0:T(8,128)S(1)} %copy.32.refs_0_.refs_1_), custom_call_target="tpu_custom_call" | custom-call | tf_op jit(solution)/shard_map/lines2/pallas_call | solution.py:365
  258.4 1.2 copy-done.1
  259.6 6.2 %all-to-all-start.4 = ((f32[64,48,128]{2,1,0:T(8,128)}), f32[64,48,128]{2,1,0:T(8,128)S(1)}, u32[]{:S(2)}, u32[]{:S(2)}) async-start(f32[64,48,128]{2,1,0:T(8,128)} %bitcast.29), calls=%async_computation.4 | async-start | bytes 3145728 | tf_op jit(solution)/shard_map/all_to_all | solution.py:326
  265.8 2.1 collective-permute-start.8
  267.9 1.1 collective-permute-done.8
  269.0 2.7 collective-permute-start.9
  271.8 2.8 collective-permute-done.9
  274.6 3.3 collective-permute-start.10
  277.9 7.6 %collective-permute-start.7 = (f32[16,128]{1,0:T(8,128)S(1)}, f32[16,128]{1,0:T(8,128)S(1)}, u32[]{:S(2)}, u32[]{:S(2)}) collective-permute-start(f32[16,128]{1,0:T(8,128)S(1)} %add_add_fusion.1), channel_id=1, source_target_pairs={{0,384},{8,392},{16,400},{24,408},{32,416},{40,424},{48,432},{56,4... | collective-permute-start | bytes 24584 | tf_op jit(solution)/shard_map/ppermute | solution.py:406
  285.5 7.1 %collective-permute-start.6 = (f32[16,128]{1,0:T(8,128)S(1)}, f32[16,128]{1,0:T(8,128)S(1)}, u32[]{:S(2)}, u32[]{:S(2)}) collective-permute-start(f32[16,128]{1,0:T(8,128)S(1)} %add_add_fusion.1), channel_id=1, source_target_pairs={{0,256},{8,264},{16,272},{24,280},{32,288},{40,296},{48,304},{56,3... | collective-permute-start | bytes 24584 | tf_op jit(solution)/shard_map/ppermute | solution.py:406
  292.6 2.4 collective-permute-start.5
  295.0 39.4 %collective-permute-done.7 = f32[16,128]{1,0:T(8,128)S(1)} collective-permute-done((f32[16,128]{1,0:T(8,128)S(1)}, f32[16,128]{1,0:T(8,128)S(1)}, u32[]{:S(2)}, u32[]{:S(2)}) %collective-permute-start.7) | collective-permute-done | bytes 8224 | tf_op jit(solution)/shard_map/ppermute | solution.py:406
  334.4 9.1 %collective-permute-done.6 = f32[16,128]{1,0:T(8,128)S(1)} collective-permute-done((f32[16,128]{1,0:T(8,128)S(1)}, f32[16,128]{1,0:T(8,128)S(1)}, u32[]{:S(2)}, u32[]{:S(2)}) %collective-permute-start.6) | collective-permute-done | bytes 8224 | tf_op jit(solution)/shard_map/ppermute | solution.py:406
  343.5 1.4 dispatch2.1
  345.0 4.2 %all-to-all-start.5 = ((f32[4,16,128]{2,1,0:T(8,128)}), f32[4,16,128]{2,1,0:T(8,128)S(1)}, u32[]{:S(2)}, u32[]{:S(2)}) async-start(f32[4,16,128]{2,1,0:T(8,128)} %bitcast.20), calls=%async_computation.5 | async-start | bytes 65536 | tf_op jit(solution)/shard_map/all_to_all | solution.py:435
  349.2 1.9 collective-permute-start.11
  351.2 1.1 collective-permute-done.11
  352.3 2.7 collective-permute-start.12
  355.0 2.8 collective-permute-done.12
  358.5 3.5 all-to-all-start.6
  362.0 3.3 collective-permute-start.13
  365.4 2.4 volt2.1
  367.8 1.3 collective-permute-done.13
  369.7 6.5 %all-to-all-done.6 = f32[16,16,128]{2,1,0:T(8,128)S(1)} async-done(((f32[16,16,128]{2,1,0:T(8,128)}), f32[16,16,128]{2,1,0:T(8,128)S(1)}, u32[]{:S(2)}, u32[]{:S(2)}) %all-to-all-start.6) | async-done | bytes 131104 | tf_op jit(solution)/shard_map/all_to_all | solution.py:440
  376.1 0.9 close.1
  (83 shorter events, 8.8 us)
Async XLA Ops:
  36.2 1.0 copy-start.4
  37.2 8.2 %copy-start.29 = (f32[256]{0:T(256)S(1)}, f32[256]{0:T(256)}, u32[]{:S(2)}) copy-start(f32[256]{0:T(256)} %param.20) | copy-start | bytes 3076
  37.2 8.2 %copy-start.30 = (f32[256]{0:T(256)S(1)}, f32[256]{0:T(256)}, u32[]{:S(2)}) copy-start(f32[256]{0:T(256)} %param.19) | copy-start | bytes 3076
  37.2 62.3 %copy-start = (f32[4,256,128]{2,1,0:T(8,128)S(1)}, f32[4,256,128]{2,1,0:T(8,128)}, u32[]{:S(2)}) copy-start(f32[4,256,128]{2,1,0:T(8,128)} %dual_ref.3) | copy-start | bytes 1572868
  40.7 58.8 %all-to-all-start.1 = ((f32[64,32,128]{2,1,0:T(8,128)}), f32[64,32,128]{2,1,0:T(8,128)S(1)}, u32[]{:S(2)}, u32[]{:S(2)}) async-start(f32[64,32,128]{2,1,0:T(8,128)} %first_send.1), calls=%async_computation.1 | async-start | bytes 2097152 | tf_op jit(solution)/shard_map/all_to_all | solution.py:326
  103.0 1.2 copy-start.2
  104.2 0.8 copy-start.6
  105.0 6.1 %copy-start.20 = (s32[256]{0:T(256)S(1)}, s32[256]{0:T(256)}, u32[]{:S(2)}) copy-start(s32[256]{0:T(256)} %param.24) | copy-start | bytes 3076
  105.0 6.1 %copy-start.23 = (f32[256]{0:T(256)S(1)}, f32[256]{0:T(256)}, u32[]{:S(2)}) copy-start(f32[256]{0:T(256)} %param.26) | copy-start | bytes 3076
  105.0 6.1 %copy-start.24 = (f32[256]{0:T(256)S(1)}, f32[256]{0:T(256)}, u32[]{:S(2)}) copy-start(f32[256]{0:T(256)} %param.25) | copy-start | bytes 3076
  105.0 6.1 %copy-start.25 = (f32[256]{0:T(256)S(1)}, f32[256]{0:T(256)}, u32[]{:S(2)}) copy-start(f32[256]{0:T(256)} %param.31) | copy-start | bytes 3076
  105.0 6.1 %copy-start.26 = (f32[256]{0:T(256)S(1)}, f32[256]{0:T(256)}, u32[]{:S(2)}) copy-start(f32[256]{0:T(256)} %param.32) | copy-start | bytes 3076
  105.0 6.1 %copy-start.27 = (f32[256]{0:T(256)S(1)}, f32[256]{0:T(256)}, u32[]{:S(2)}) copy-start(f32[256]{0:T(256)} %param.33) | copy-start | bytes 3076
  105.0 6.1 %copy-start.28 = (f32[256]{0:T(256)S(1)}, f32[256]{0:T(256)}, u32[]{:S(2)}) copy-start(f32[256]{0:T(256)} %param.30) | copy-start | bytes 3076
  105.0 82.9 %copy-start.5 = (f32[2,256,128]{2,1,0:T(8,128)S(1)}, f32[2,256,128]{2,1,0:T(8,128)}, u32[]{:S(2)}) copy-start(f32[2,256,128]{2,1,0:T(8,128)} %volt_ref.3) | copy-start | bytes 786436
  105.1 82.8 %all-to-all-start.2 = ((f32[64,48,128]{2,1,0:T(8,128)}), f32[64,48,128]{2,1,0:T(8,128)S(1)}, u32[]{:S(2)}, u32[]{:S(2)}) async-start(f32[64,48,128]{2,1,0:T(8,128)} %bitcast.30), calls=%async_computation.2 | async-start | bytes 3145728 | tf_op jit(solution)/shard_map/all_to_all | solution.py:326
  191.0 1.0 copy-start.3
  192.1 0.7 copy-start.14
  192.8 60.3 %all-to-all-start.3 = ((f32[64,32,128]{2,1,0:T(8,128)}), f32[64,32,128]{2,1,0:T(8,128)S(1)}, u32[]{:S(2)}, u32[]{:S(2)}) async-start(f32[64,32,128]{2,1,0:T(8,128)} %copy-done.3), calls=%async_computation.3 | async-start | bytes 2097152 | tf_op jit(solution)/shard_map/all_to_all | solution.py:326
  198.6 0.9 copy-start.8
  199.5 0.9 copy-start.10
  200.4 0.9 copy-start.12
  202.0 0.7 copy-start.16
  203.3 5.6 %collective-permute-start = (f32[16,128]{1,0:T(8,128)S(1)}, f32[16,128]{1,0:T(8,128)S(1)}, u32[]{:S(2)}, u32[]{:S(2)}) collective-permute-start(f32[16,128]{1,0:T(8,128)S(1)} %get-tuple-element.29), channel_id=1, source_target_pairs={{0,8},{8,0},{16,24},{24,16},{32,40},{40,32},{48,56},{56,48},{64,72... | collective-permute-start | bytes 24584 | tf_op jit(solution)/shard_map/ppermute | solution.py:406
  209.0 7.1 %collective-permute-start.1 = (f32[16,128]{1,0:T(8,128)S(1)}, f32[16,128]{1,0:T(8,128)S(1)}, u32[]{:S(2)}, u32[]{:S(2)}) collective-permute-start(f32[16,128]{1,0:T(8,128)S(1)} %add.42), channel_id=1, source_target_pairs={{0,16},{8,24},{16,0},{24,8},{32,48},{40,56},{48,32},{56,40},{64,80... | collective-permute-start | bytes 24584 | tf_op jit(solution)/shard_map/ppermute | solution.py:406
  216.1 28.5 %collective-permute-start.4 = (f32[16,128]{1,0:T(8,128)S(1)}, f32[16,128]{1,0:T(8,128)S(1)}, u32[]{:S(2)}, u32[]{:S(2)}) collective-permute-start(f32[16,128]{1,0:T(8,128)S(1)} %add.43), channel_id=1, source_target_pairs={{0,96},{8,104},{16,112},{24,120},{32,64},{40,72},{48,80},{56,88},{... | collective-permute-start | bytes 24584 | tf_op jit(solution)/shard_map/ppermute | solution.py:406
  221.3 23.3 %collective-permute-start.3 = (f32[16,128]{1,0:T(8,128)S(1)}, f32[16,128]{1,0:T(8,128)S(1)}, u32[]{:S(2)}, u32[]{:S(2)}) collective-permute-start(f32[16,128]{1,0:T(8,128)S(1)} %add.43), channel_id=1, source_target_pairs={{0,64},{8,72},{16,80},{24,88},{32,96},{40,104},{48,112},{56,120},{... | collective-permute-start | bytes 24584 | tf_op jit(solution)/shard_map/ppermute | solution.py:406
  223.2 21.4 %collective-permute-start.2 = (f32[16,128]{1,0:T(8,128)S(1)}, f32[16,128]{1,0:T(8,128)S(1)}, u32[]{:S(2)}, u32[]{:S(2)}) collective-permute-start(f32[16,128]{1,0:T(8,128)S(1)} %add.43), channel_id=1, source_target_pairs={{0,32},{8,40},{16,48},{24,56},{32,0},{40,8},{48,16},{56,24},{64,96... | collective-permute-start | bytes 24584 | tf_op jit(solution)/shard_map/ppermute | solution.py:406
  253.1 1.0 copy-start.7
  258.4 1.2 copy-start.1
  259.6 83.9 %copy-start.9 = (f32[256,128]{1,0:T(8,128)S(1)}, f32[256,128]{1,0:T(8,128)}, u32[]{:S(2)}) copy-start(f32[256,128]{1,0:T(8,128)} %load_ref.3) | copy-start | bytes 393220
  259.6 83.9 %copy-start.11 = (f32[256,128]{1,0:T(8,128)S(1)}, f32[256,128]{1,0:T(8,128)}, u32[]{:S(2)}) copy-start(f32[256,128]{1,0:T(8,128)} %price_ref.3) | copy-start | bytes 393220
  259.6 83.9 %copy-start.13 = (f32[256,128]{1,0:T(8,128)S(1)}, f32[256,128]{1,0:T(8,128)}, u32[]{:S(2)}) copy-start(f32[256,128]{1,0:T(8,128)} %nadual_ref.3) | copy-start | bytes 393220
  259.6 83.9 %copy-start.17 = (f32[256,128]{1,0:T(8,128)S(1)}, f32[256,128]{1,0:T(8,128)}, u32[]{:S(2)}) copy-start(f32[256,128]{1,0:T(8,128)} %copy-done.16) | copy-start | bytes 393220
  259.6 83.9 %copy-start.19 = (f32[256,128]{1,0:T(8,128)S(1)}, f32[256,128]{1,0:T(8,128)}, u32[]{:S(2)}) copy-start(f32[256,128]{1,0:T(8,128)} %copy-done.18) | copy-start | bytes 393220
  259.6 83.9 %all-to-all-start.4 = ((f32[64,48,128]{2,1,0:T(8,128)}), f32[64,48,128]{2,1,0:T(8,128)S(1)}, u32[]{:S(2)}, u32[]{:S(2)}) async-start(f32[64,48,128]{2,1,0:T(8,128)} %bitcast.29), calls=%async_computation.4 | async-start | bytes 3145728 | tf_op jit(solution)/shard_map/all_to_all | solution.py:326
  265.8 99.5 %copy-start.15 = (f32[2,256,128]{2,1,0:T(8,128)S(1)}, f32[2,256,128]{2,1,0:T(8,128)}, u32[]{:S(2)}) copy-start(f32[2,256,128]{2,1,0:T(8,128)} %copy-done.14) | copy-start | bytes 786436
  265.8 3.2 collective-permute-start.8
  269.0 5.5 %collective-permute-start.9 = (f32[8,256]{1,0:T(8,128)S(1)}, f32[8,256]{1,0:T(8,128)S(1)}, u32[]{:S(2)}, u32[]{:S(2)}) collective-permute-start(f32[8,256]{1,0:T(8,128)S(1)} %add.50), channel_id=1, source_target_pairs={{0,2},{1,3},{2,0},{3,1},{4,6},{5,7},{6,4},{7,5},{8,10},{9,11},{10,... | collective-permute-start | bytes 24584 | tf_op jit(solution)/shard_map/ppermute | solution.py:406
  274.6 20.4 %collective-permute-start.10 = (f32[8,256]{1,0:T(8,128)S(1)}, f32[8,256]{1,0:T(8,128)S(1)}, u32[]{:S(2)}, u32[]{:S(2)}) collective-permute-start(f32[8,256]{1,0:T(8,128)S(1)} %add.51), channel_id=1, source_target_pairs={{0,4},{1,5},{2,6},{3,7},{4,0},{5,1},{6,2},{7,3},{8,12},{9,13},{10,... | collective-permute-start | bytes 24584 | tf_op jit(solution)/shard_map/ppermute | solution.py:406
  277.9 56.5 %collective-permute-start.7 = (f32[16,128]{1,0:T(8,128)S(1)}, f32[16,128]{1,0:T(8,128)S(1)}, u32[]{:S(2)}, u32[]{:S(2)}) collective-permute-start(f32[16,128]{1,0:T(8,128)S(1)} %add_add_fusion.1), channel_id=1, source_target_pairs={{0,384},{8,392},{16,400},{24,408},{32,416},{40,424},{48,432},{56,4... | collective-permute-start | bytes 24584 | tf_op jit(solution)/shard_map/ppermute | solution.py:406
  285.5 58.0 %collective-permute-start.6 = (f32[16,128]{1,0:T(8,128)S(1)}, f32[16,128]{1,0:T(8,128)S(1)}, u32[]{:S(2)}, u32[]{:S(2)}) collective-permute-start(f32[16,128]{1,0:T(8,128)S(1)} %add_add_fusion.1), channel_id=1, source_target_pairs={{0,256},{8,264},{16,272},{24,280},{32,288},{40,296},{48,304},{56,3... | collective-permute-start | bytes 24584 | tf_op jit(solution)/shard_map/ppermute | solution.py:406
  292.6 50.9 %collective-permute-start.5 = (f32[16,128]{1,0:T(8,128)S(1)}, f32[16,128]{1,0:T(8,128)S(1)}, u32[]{:S(2)}, u32[]{:S(2)}) collective-permute-start(f32[16,128]{1,0:T(8,128)S(1)} %add_add_fusion.1), channel_id=1, source_target_pairs={{0,128},{8,136},{16,144},{24,152},{32,160},{40,168},{48,176},{56,1... | collective-permute-start | bytes 24584 | tf_op jit(solution)/shard_map/ppermute | solution.py:406
  345.0 12.8 %all-to-all-start.5 = ((f32[4,16,128]{2,1,0:T(8,128)}), f32[4,16,128]{2,1,0:T(8,128)S(1)}, u32[]{:S(2)}, u32[]{:S(2)}) async-start(f32[4,16,128]{2,1,0:T(8,128)} %bitcast.20), calls=%async_computation.5 | async-start | bytes 65536 | tf_op jit(solution)/shard_map/all_to_all | solution.py:435
  349.2 3.1 collective-permute-start.11
  352.3 5.5 %collective-permute-start.12 = (f32[8,256]{1,0:T(8,128)S(1)}, f32[8,256]{1,0:T(8,128)S(1)}, u32[]{:S(2)}, u32[]{:S(2)}) collective-permute-start(f32[8,256]{1,0:T(8,128)S(1)} %add.53), channel_id=1, source_target_pairs={{0,2},{1,3},{2,0},{3,1},{4,6},{5,7},{6,4},{7,5},{8,10},{9,11},{10,... | collective-permute-start | bytes 24584 | tf_op jit(solution)/shard_map/ppermute | solution.py:406
  358.5 17.6 %all-to-all-start.6 = ((f32[16,16,128]{2,1,0:T(8,128)}), f32[16,16,128]{2,1,0:T(8,128)S(1)}, u32[]{:S(2)}, u32[]{:S(2)}) async-start(f32[16,16,128]{2,1,0:T(8,128)} %broadcast_in_dim.2), calls=%async_computation.6 | async-start | bytes 262144 | tf_op jit(solution)/shard_map/all_to_all | solution.py:440
  362.0 7.0 %collective-permute-start.13 = (f32[8,256]{1,0:T(8,128)S(1)}, f32[8,256]{1,0:T(8,128)S(1)}, u32[]{:S(2)}, u32[]{:S(2)}) collective-permute-start(f32[8,256]{1,0:T(8,128)S(1)} %add.54), channel_id=1, source_target_pairs={{0,4},{1,5},{2,6},{3,7},{4,0},{5,1},{6,2},{7,3},{8,12},{9,13},{10,... | collective-permute-start | bytes 24584 | tf_op jit(solution)/shard_map/ppermute | solution.py:406
  (3 other events, 2.0 us)

commit v5 on v4

--- a/solution.py
+++ b/solution.py
@@ -13,6 +13,8 @@
 LANES = 128
 REGION_GAIN = 10.0
 BLOCK = 16
+GROUP = 4
+PARTS = 4
 NEAR = 4
 GRANT = 16 * 2**20
 
@@ -28,6 +30,28 @@
 
 def vmem():
     return pl.BlockSpec(memory_space=VMEM)
+
+
+def hbm():
+    return pl.BlockSpec(memory_space=pltpu.HBM)
+
+
+def in_hbm(x):
+    return pltpu.with_memory_space_constraint(x, pltpu.HBM)
+
+
+def copies_of(pairs, sem):
+    return [pltpu.make_async_copy(a, b, sem.at[i]) for i, (a, b) in enumerate(pairs)]
+
+
+def start_all(copies):
+    for copy in copies:
+        copy.start()
+
+
+def wait_all(copies):
+    for copy in copies:
+        copy.wait()
 
 
 def pieces(x, count):
@@ -52,7 +76,10 @@
     return lax.dot_general(a, b, (((1,), (1,)), ((), ())), preferred_element_type=F32)
 
 
-def plan_kernel(count_ref, owner_ref, bus_ref, slot_ref, request_ref):
+def plan_kernel(count_ref, owner_hbm, bus_hbm, slot_ref, request_ref, owner_ref, bus_ref, sem):
+    fetch = copies_of([(owner_hbm, owner_ref), (bus_hbm, bus_ref)], sem)
+    start_all(fetch)
+    wait_all(fetch)
     ends = owner_ref.shape[1]
     owners = request_ref.shape[0]
     owner = owner_ref[...]
@@ -72,21 +99,37 @@
     request_ref[...] = table.astype(jnp.int32)
 
 
-def send_rows(asked_ref, volt_ref, out_ref):
+def send_rows(asked_ref, volt_ref, out_hbm, row_ref, sem):
     buses = volt_ref.shape[1]
-
-    def step(o, carry):
-        for r in range(CAP):
-            bus = (asked_ref[o, r] - 1) & (buses - 1)
-            for c in range(2):
-                out_ref[o, c * CAP + r : c * CAP + r + 1, :] = volt_ref[c, pl.ds(bus, 1), :]
+    groups = row_ref.shape[0] // GROUP
+
+    def ship(group):
+        part = pl.ds(group * GROUP, GROUP)
+        return pltpu.make_async_copy(row_ref.at[part], out_hbm.at[part], sem.at[group])
+
+    def step(group, carry):
+        for i in range(GROUP):
+            o = group * GROUP + i
+            for r in range(CAP):
+                bus = (asked_ref[o, r] - 1) & (buses - 1)
+                for c in range(2):
+                    row_ref[o, c * CAP + r : c * CAP + r + 1, :] = volt_ref[c, pl.ds(bus, 1), :]
+        ship(group).start()
         return carry
 
-    lax.fori_loop(0, out_ref.shape[0], step, 0, unroll=4)
-
-
-def first_send_kernel(asked_ref, volt_ref, out_ref):
-    send_rows(asked_ref, volt_ref, out_ref)
+    def done(group, carry):
+        ship(group).wait()
+        return carry
+
+    lax.fori_loop(0, groups, step, 0)
+    lax.fori_loop(0, groups, done, 0)
+
+
+def first_send_kernel(asked_ref, volt_hbm, out_hbm, volt_ref, row_ref, volt_sem, sem):
+    fetch = copies_of([(volt_hbm.at[c], volt_ref.at[c]) for c in range(2)], volt_sem)
+    start_all(fetch)
+    wait_all(fetch)
+    send_rows(asked_ref, volt_ref, out_hbm, row_ref, sem)
 
 
 def sin_cos(x):
@@ -142,12 +185,29 @@
 
 def line_kernel(second, count_ref, slot_ref, arrived_ref, dual_ref, *refs):
     if second:
-        previous_ref, param_ref, out_ref, dual_out_ref, *scratch = refs
-    else:
-        param_ref, out_ref, state_ref, *scratch = refs
-    near_refs, term_refs = scratch[:2], scratch[2:]
+        previous_hbm, *refs = refs
+    param_ref, out_hbm, other_hbm, *refs = refs
+    near_refs, term_refs = refs[:2], refs[2:4]
+    out_ref, other_ref, out_sem, other_sem, *refs = refs[4:]
+    if second:
+        previous_ref, previous_sem = refs
     lines = dual_ref.shape[1]
     blocks = lines // BLOCK
+
+    def pair_rows(pair):
+        return pl.ds(pl.multiple_of(pair * 2 * BLOCK, 2 * BLOCK), 2 * BLOCK)
+
+    def fetch(pair):
+        rows = pair_rows(pair)
+        return pltpu.make_async_copy(
+            previous_hbm.at[:, rows], previous_ref.at[:, rows], previous_sem.at[pair]
+        )
+
+    def keep(pair):
+        rows = pair_rows(pair)
+        return pltpu.make_async_copy(
+            other_ref.at[:, rows], other_hbm.at[:, rows], other_sem.at[pair]
+        )
 
     def gather(block, near_ref):
         for end in range(2):
@@ -178,7 +238,7 @@
                 for i in range(4)
             ]
             for i in range(4):
-                dual_out_ref[i, rows, :] = dual[i]
+                other_ref[i, rows, :] = dual[i]
         center = [near[i] - dual[i] for i in range(4)]
         param = param_ref[rows, :]
         cond = jnp.broadcast_to(param[:, 0:1], (BLOCK, LANES))
@@ -186,7 +246,7 @@
         state, flow_from, flow_to = branch_newton(center, cond, susc)
         if not second:
             for i in range(4):
-                state_ref[i, rows, :] = state[i]
+                other_ref[i, rows, :] = state[i]
         terms = [
             state[0] + dual[0], state[1] + dual[1], flow_from,
             state[2] + dual[2], state[3] + dual[3], flow_to,
@@ -196,19 +256,32 @@
 
     def step(pair, carry):
         block = 2 * pair
+        if second:
+            fetch(pair).wait()
         scatter(lax.rem(block + blocks - 1, blocks), term_refs[1])
         gather(block + 1, near_refs[1])
         solve(block, near_refs[0], term_refs[0])
         gather(lax.rem(block + 2, blocks), near_refs[0])
         scatter(block, term_refs[0])
         solve(block + 1, near_refs[1], term_refs[1])
+        keep(pair).start()
         return carry
 
+    if second:
+        for pair in range(blocks // 2):
+            fetch(pair).start()
     out_ref[...] = jnp.zeros_like(out_ref)
     term_refs[1][...] = jnp.zeros_like(term_refs[1])
     gather(0, near_refs[0])
     lax.fori_loop(0, blocks // 2, step, 0)
     scatter(blocks - 1, term_refs[1])
+    piece = out_ref.shape[0] // PARTS
+    rows = [pl.ds(i * piece, piece) for i in range(PARTS)]
+    ship = copies_of([(out_ref.at[r], out_hbm.at[r]) for r in rows], out_sem)
+    start_all(ship)
+    for pair in range(blocks // 2):
+        keep(pair).wait()
+    wait_all(ship)
 
 
 def column(param, index):
@@ -232,7 +305,11 @@
     return recv_ref[:, c * CAP : (c + 1) * CAP, :].reshape(recv_ref.shape[0] * CAP, LANES)
 
 
-def volt_kernel(send, asked_ref, row_ref, recv_ref, volt_ref, param_ref, volt_out, *refs):
+def volt_kernel(send, asked_ref, row_ref, recv_ref, volt_ref, param_ref, volt_hbm, *refs):
+    if send:
+        send_hbm, volt_out, rows_ref, volt_sem, sem = refs
+    else:
+        volt_out = volt_hbm
     hits = bus_hits(row_ref, volt_ref.shape[1])
     rows = jnp.concatenate([slot_rows(recv_ref, 0), slot_rows(recv_ref, 1)], axis=1)
     pair = picked(hits, rows, 2)
@@ -244,7 +321,10 @@
     volt_out[0] = (pair[:, :LANES] + weight * column(param, 1)) * inverse
     volt_out[1] = (pair[:, LANES:] + weight * volt_ref[1]) * inverse
     if send:
-        send_rows(asked_ref, volt_out, refs[0])
+        keep = pltpu.make_async_copy(volt_out, volt_hbm, volt_sem)
+        keep.start()
+        send_rows(asked_ref, volt_out, send_hbm, rows_ref, sem)
+        keep.wait()
 
 
 def dispatch_kernel(second, buses_all, scen_all, row_ref, recv_ref, param_ref, region_ref,
@@ -328,11 +408,12 @@
     slot, request = pl.pallas_call(
         plan_kernel,
         out_shape=(shape((1, ends), jnp.int32), shape((ngrid, LANES), jnp.int32)),
-        in_specs=[smem(), vmem(), vmem()],
+        in_specs=[smem(), hbm(), hbm()],
         out_specs=(vmem(), vmem()),
+        scratch_shapes=[VMEM((1, ends), jnp.int32)] * 2 + [pltpu.SemaphoreType.DMA((2,))],
         compiler_params=pltpu.CompilerParams(vmem_limit_bytes=GRANT),
         name="plan",
-    )(line_count, endpoint_owner.reshape(1, ends), endpoint_bus.reshape(1, ends))
+    )(line_count, in_hbm(endpoint_owner.reshape(1, ends)), in_hbm(endpoint_bus.reshape(1, ends)))
     slot = slot.reshape(ends)
     asked = exchange(request)
     asked_row = asked[:, :CAP].reshape(1, ngrid * CAP)
@@ -344,42 +425,55 @@
         axis=1,
     )
     region_row = bus_region.reshape(1, buses)
-    send_shape = shape((ngrid, 2 * CAP, LANES), F32)
+    send_shape = (ngrid, 2 * CAP, LANES)
+    send_hbm = pltpu.HBM(send_shape, F32)
     bus_shape = shape((buses, LANES), F32)
 
     sent = pl.pallas_call(
         first_send_kernel,
-        out_shape=send_shape,
-        in_specs=[smem(), vmem()],
-        out_specs=vmem(),
+        out_shape=send_hbm,
+        in_specs=[smem(), hbm()],
+        out_specs=hbm(),
+        scratch_shapes=[VMEM((2, buses, LANES), F32), VMEM(send_shape, F32),
+                        pltpu.SemaphoreType.DMA((2,)), pltpu.SemaphoreType.DMA((ngrid // GROUP,))],
         compiler_params=pltpu.CompilerParams(vmem_limit_bytes=GRANT),
         name="first_send",
-    )(asked, volt_init)
+    )(asked, in_hbm(volt_init))
 
     def line_call(second, arrived, previous):
-        outs = [shape((ngrid * 3 * CAP, LANES), F32), shape((4, lines, LANES), F32)]
+        outs = [pltpu.HBM((ngrid * 3 * CAP, LANES), F32), pltpu.HBM((4, lines, LANES), F32)]
         args = [line_count, slot, arrived.reshape(ngrid * 2 * CAP, LANES), line_dual]
         if second:
-            args.append(previous)
+            args.append(in_hbm(previous))
         args.append(line_param)
+        pair_sem = pltpu.SemaphoreType.DMA((lines // (2 * BLOCK),))
+        held = VMEM((4, lines, LANES), F32)
+        specs = [smem(), smem(), vmem(), vmem()] + [hbm()] * second + [vmem()]
+        scratch = [VMEM((4, BLOCK, LANES), F32)] * 2 + [VMEM((6, BLOCK, LANES), F32)] * 2
+        scratch += [VMEM(outs[0].shape, F32), held, pltpu.SemaphoreType.DMA((PARTS,)), pair_sem]
+        scratch += [held, pair_sem] * second
         out, other = pl.pallas_call(
             functools.partial(line_kernel, second),
             out_shape=outs,
-            in_specs=[smem(), smem()] + [vmem()] * (len(args) - 2),
-            out_specs=[vmem(), vmem()],
-            scratch_shapes=[VMEM((4, BLOCK, LANES), F32)] * 2 + [VMEM((6, BLOCK, LANES), F32)] * 2,
+            in_specs=specs,
+            out_specs=[hbm(), hbm()],
+            scratch_shapes=scratch,
             compiler_params=pltpu.CompilerParams(vmem_limit_bytes=GRANT),
             name="lines2" if second else "lines1",
         )(*args)
         return out.reshape(ngrid, 3 * CAP, LANES), other
 
     def volt_call(send, received, volt):
-        outs = [shape((2, buses, LANES), F32)] + ([send_shape] if send else [])
+        volt_shape = (2, buses, LANES)
+        outs = [pltpu.HBM(volt_shape, F32), send_hbm] if send else [shape(volt_shape, F32)]
         return pl.pallas_call(
             functools.partial(volt_kernel, send),
             out_shape=outs,
             in_specs=[smem()] + [vmem()] * 4,
-            out_specs=[vmem()] * len(outs),
+            out_specs=[hbm()] * 2 if send else [vmem()],
+            scratch_shapes=[VMEM(outs[0].shape, F32), VMEM(send_shape, F32),
+                            pltpu.SemaphoreType.DMA,
+                            pltpu.SemaphoreType.DMA((ngrid // GROUP,))] if send else [],
             compiler_params=pltpu.CompilerParams(vmem_limit_bytes=GRANT),
             name="volt1" if send else "volt2",
         )(asked, asked_row, received, volt, bus_param)
@@ -408,10 +502,9 @@
         ]
         return sum(parts, x)
 
-    def doubling_sum(x, axis, count):
-        step = 1
+    def doubling_sum(x, axis, count, step=1):
         while step < count:
-            x = near_sum(x, axis, lax.axis_size(axis), step, 2)
+            x = near_sum(x, axis, count, step, 2)
             step *= 2
         return x
 
@@ -433,12 +526,12 @@
     near = [[i * NEAR + j for j in range(NEAR)] for i in range(ngrid // NEAR)]
     far = [[i * NEAR + j for i in range(ngrid // NEAR)] for j in range(NEAR)]
     part = lax.all_to_all(part, "grid", 0, 0, axis_index_groups=near, tiled=True)
-    total = doubling_sum(total, "scen", nscen // 2)
+    total = near_sum(total, "scen", nscen, 1, 2)
     part, total = lax.optimization_barrier((part, total))
     part = jnp.sum(part.reshape(NEAR, REGIONS, LANES), axis=0)
     part = jnp.broadcast_to(part[None], (ngrid // NEAR, REGIONS, LANES))
     parts = lax.all_to_all(part, "grid", 0, 0, axis_index_groups=far, tiled=True)
-    commit = near_sum(total, "scen", nscen, nscen // 2, 2)[0] / (scen * nscen)
+    commit = doubling_sum(total, "scen", nscen, 2)[0] / (scen * nscen)
     (volt,) = volt_call(False, received, volt)
     price = pl.pallas_call(
         functools.partial(close_kernel, buses_all),

time: 379 us -> 371 us (0.979)
  local copies, waits for them, and re-layouts: 13.4 us -> 5.18 us
  Pallas kernels: 20.3 us -> 25.3 us
  waiting for transfers between devices: 226 us -> 222 us
    unnamed x62 -> x44, local copies, waits for them, and re-layouts: 12.3 us -> 4.14 us
    all_to_all x1, waiting for transfers between devices: 6.49 us -> 0.4 us  [on_device(): lax.all_to_all(part, 'grid', 0, 0, axis_index_groups=far, tiled=True)]
  transfers between devices with their start and end apart: 20 -> 20, of which waited for: 14 -> 15; matrix products, arithmetic and copies ran while one was open for 0% -> 0% of each run, Pallas kernels for 1% -> 1%
where the time goes in v5:
time: 371 us; the launch traced here: 370 us
  waiting for transfers between devices  222 us (60%)
  starting transfers between devices  82 us (22%)
  blocking collectives  33.2 us (9%)
  Pallas kernels  25.3 us (7%)
  local copies, waits for them, and re-layouts  5.18 us (1%)
    all_to_all x4, waiting for transfers between devices, exchange(): return lax.all_to_all(x, 'grid', split_axis=0, concat_axis=0, tiled=True)  139 us
    ppermute x14, waiting for transfers between devices, near_sum(): lax.ppermute(x, axis, [(i, i ^ k * step) for i in range(size)])  80.4 us
    ppermute x14, starting transfers between devices, near_sum(): lax.ppermute(x, axis, [(i, i ^ k * step) for i in range(size)])  51.6 us
    all_to_all x1, blocking collectives, exchange(): return lax.all_to_all(x, 'grid', split_axis=0, concat_axis=0, tiled=True)  33.2 us
    all_to_all x4, starting transfers between devices, exchange(): return lax.all_to_all(x, 'grid', split_axis=0, concat_axis=0, tiled=True)  22.7 us
    pallas_call x2, Pallas kernels, line_call(): pl.pallas_call(functools.partial(line_kernel, second), out_shape=outs, in...  10.5 us
  transfers between devices with their start and end apart: 20, of which 15 were waited for; matrix products, arithmetic and copies ran while one was open for 0% of the time, Pallas kernels for 1%

profile of v5, /device:TPU:6, one launch (start us, length us, event | category | flops | bytes accessed | tf_op | source)
XLA Modules:
  0.0 370.2 jit_solution(10643431759302542726)
XLA Ops:
  1.3 1.1 plan.1
  2.4 33.2 %all_to_all.48 = s32[64,1,128]{2,1,0:T(1,128)S(1)} all-to-all(s32[64,1,128]{2,1,0:T(1,128)S(1)} %bitcast.34), channel_id=1, replica_groups=mesh['grid'=64,'scen'=8] {'grid'}, dimensions={0} | all-to-all | bytes 65536 | tf_op jit(solution)/shard_map/all_to_all | solution.py:406
  35.6 4.3 %first_send.1 = f32[64,32,128]{2,1,0:T(8,128)} custom-call(s32[64,128]{1,0:T(8,128)S(1)} %bitcast.29, f32[2,256,128]{2,1,0:T(8,128)} %volt_ref.1), custom_call_target="tpu_custom_call" | custom-call | tf_op jit(solution)/shard_map/first_send/pallas_call | solution.py:432
  39.9 4.7 %all-to-all-start.1 = ((f32[64,32,128]{2,1,0:T(8,128)}), f32[64,32,128]{2,1,0:T(8,128)S(1)}, u32[]{:S(2)}, u32[]{:S(2)}) async-start(f32[64,32,128]{2,1,0:T(8,128)} %first_send.1), calls=%async_computation.1 | async-start | bytes 2097152 | tf_op jit(solution)/shard_map/all_to_all | solution.py:406
  44.7 54.0 %all-to-all-done.1 = f32[64,32,128]{2,1,0:T(8,128)S(1)} async-done(((f32[64,32,128]{2,1,0:T(8,128)}), f32[64,32,128]{2,1,0:T(8,128)S(1)}, u32[]{:S(2)}, u32[]{:S(2)}) %all-to-all-start.1) | async-done | bytes 1048608 | tf_op jit(solution)/shard_map/all_to_all | solution.py:406
  98.7 4.8 %lines1.1 = (f32[3072,128]{1,0:T(8,128)}, f32[4,256,128]{2,1,0:T(8,128)}) custom-call(s32[1]{0:T(128)S(6)} %copy.39.count_ref, s32[512]{0:T(512)S(1)} %bitcast.37, f32[2048,128]{1,0:T(8,128)S(1)} %bitcast.28, f32[4,256,128]{2,1,0:T(8,128)S(1)} %copy-done, f32[256,2]{1,0:T(8,128)S(1)} %copy.32.refs_0_.refs_1_), custom_call_target="tpu_custom_call" | custom-call | tf_op jit(solution)/shard_map/lines1/pallas_call | solution.py:455
  103.6 6.0 %all-to-all-start.2 = ((f32[64,48,128]{2,1,0:T(8,128)}), f32[64,48,128]{2,1,0:T(8,128)S(1)}, u32[]{:S(2)}, u32[]{:S(2)}) async-start(f32[64,48,128]{2,1,0:T(8,128)} %bitcast.40), calls=%async_computation.2 | async-start | bytes 3145728 | tf_op jit(solution)/shard_map/all_to_all | solution.py:406
  110.0 76.5 %all-to-all-done.2.recv_ref = f32[64,48,128]{2,1,0:T(8,128)S(1)} async-done(((f32[64,48,128]{2,1,0:T(8,128)}), f32[64,48,128]{2,1,0:T(8,128)S(1)}, u32[]{:S(2)}, u32[]{:S(2)}) %all-to-all-start.2) | async-done | bytes 1572896 | tf_op jit(solution)/shard_map/all_to_all | solution.py:406
  186.5 3.9 %volt1.1 = (f32[2,256,128]{2,1,0:T(8,128)}, f32[64,32,128]{2,1,0:T(8,128)}) custom-call(s32[64,128]{1,0:T(8,128)S(1)} %bitcast.31, s32[1,1024]{1,0:T(1,128)S(1)} %reshape.52.row_ref, f32[64,48,128]{2,1,0:T(8,128)S(1)} %all-to-all-done.2.recv_ref, f32[2,256,128]{2,1,0:T(8,128)S(1)} %copy-done.1, f32[256,8]{1,0:T(8,128)S(1)} %copy.33.param_ref), custom_call_target="tpu_custom_call" | custom-call | tf_op jit(solution)/shard_map/volt1/pallas_call | solution.py:469
  190.4 5.8 %all-to-all-start.3 = ((f32[64,32,128]{2,1,0:T(8,128)}), f32[64,32,128]{2,1,0:T(8,128)S(1)}, u32[]{:S(2)}, u32[]{:S(2)}) async-start(f32[64,32,128]{2,1,0:T(8,128)} %get-tuple-element.28), calls=%async_computation.3 | async-start | bytes 2097152 | tf_op jit(solution)/shard_map/all_to_all | solution.py:406
  196.3 0.9 copy-done.2
  197.2 0.9 copy-done.4
  198.1 0.9 copy-done.6
  199.0 0.7 dispatch1.1
  199.7 0.7 copy-done.9
  201.0 3.5 collective-permute-start
  204.5 2.1 collective-permute-done
  206.6 4.9 %collective-permute-start.1 = (f32[16,128]{1,0:T(8,128)S(1)}, f32[16,128]{1,0:T(8,128)S(1)}, u32[]{:S(2)}, u32[]{:S(2)}) collective-permute-start(f32[16,128]{1,0:T(8,128)S(1)} %add.42), channel_id=1, source_target_pairs={{0,16},{8,24},{16,0},{24,8},{32,48},{40,56},{48,32},{56,40},{64,80... | collective-permute-start | bytes 24584 | tf_op jit(solution)/shard_map/ppermute | solution.py:500
  211.5 2.2 collective-permute-done.1
  213.7 5.2 %collective-permute-start.4 = (f32[16,128]{1,0:T(8,128)S(1)}, f32[16,128]{1,0:T(8,128)S(1)}, u32[]{:S(2)}, u32[]{:S(2)}) collective-permute-start(f32[16,128]{1,0:T(8,128)S(1)} %add.43), channel_id=1, source_target_pairs={{0,96},{8,104},{16,112},{24,120},{32,64},{40,72},{48,80},{56,88},{... | collective-permute-start | bytes 24584 | tf_op jit(solution)/shard_map/ppermute | solution.py:500
  218.9 1.9 collective-permute-start.3
  220.9 3.0 collective-permute-start.2
  223.9 18.4 %collective-permute-done.4 = f32[16,128]{1,0:T(8,128)S(1)} collective-permute-done((f32[16,128]{1,0:T(8,128)S(1)}, f32[16,128]{1,0:T(8,128)S(1)}, u32[]{:S(2)}, u32[]{:S(2)}) %collective-permute-start.4) | collective-permute-done | bytes 8224 | tf_op jit(solution)/shard_map/ppermute | solution.py:500
  242.2 8.5 %all-to-all-done.3 = f32[64,32,128]{2,1,0:T(8,128)S(1)} async-done(((f32[64,32,128]{2,1,0:T(8,128)}), f32[64,32,128]{2,1,0:T(8,128)S(1)}, u32[]{:S(2)}, u32[]{:S(2)}) %all-to-all-start.3) | async-done | bytes 1048608 | tf_op jit(solution)/shard_map/all_to_all | solution.py:406
  250.7 5.7 %lines2.1 = (f32[3072,128]{1,0:T(8,128)}, f32[4,256,128]{2,1,0:T(8,128)}) custom-call(s32[1]{0:T(128)S(6)} %copy.39.count_ref, s32[512]{0:T(512)S(1)} %bitcast.38, f32[2048,128]{1,0:T(8,128)S(1)} %bitcast.27, f32[4,256,128]{2,1,0:T(8,128)S(1)} %copy-done, f32[4,256,128]{2,1,0:T(8,128)} %get-tuple-element.31.refs_0_, f32[256,2]{1,0:T(8,128)S(1)} %copy.32.refs_0_.refs_1_), custom_call_target="tpu_custom_call" | custom-call | tf_op jit(solution)/shard_map/lines2/pallas_call | solution.py:455
  256.4 6.2 %all-to-all-start.4 = ((f32[64,48,128]{2,1,0:T(8,128)}), f32[64,48,128]{2,1,0:T(8,128)S(1)}, u32[]{:S(2)}, u32[]{:S(2)}) async-start(f32[64,48,128]{2,1,0:T(8,128)} %bitcast.39), calls=%async_computation.4 | async-start | bytes 3145728 | tf_op jit(solution)/shard_map/all_to_all | solution.py:406
  262.7 2.1 collective-permute-start.8
  264.7 1.1 collective-permute-done.8
  265.9 2.7 collective-permute-start.9
  268.6 2.8 collective-permute-done.9
  271.4 3.3 collective-permute-start.10
  274.7 7.6 %collective-permute-start.7 = (f32[16,128]{1,0:T(8,128)S(1)}, f32[16,128]{1,0:T(8,128)S(1)}, u32[]{:S(2)}, u32[]{:S(2)}) collective-permute-start(f32[16,128]{1,0:T(8,128)S(1)} %add_add_fusion.1), channel_id=1, source_target_pairs={{0,384},{8,392},{16,400},{24,408},{32,416},{40,424},{48,432},{56,4... | collective-permute-start | bytes 24584 | tf_op jit(solution)/shard_map/ppermute | solution.py:500
  282.3 7.1 %collective-permute-start.6 = (f32[16,128]{1,0:T(8,128)S(1)}, f32[16,128]{1,0:T(8,128)S(1)}, u32[]{:S(2)}, u32[]{:S(2)}) collective-permute-start(f32[16,128]{1,0:T(8,128)S(1)} %add_add_fusion.1), channel_id=1, source_target_pairs={{0,256},{8,264},{16,272},{24,280},{32,288},{40,296},{48,304},{56,3... | collective-permute-start | bytes 24584 | tf_op jit(solution)/shard_map/ppermute | solution.py:500
  289.4 2.4 collective-permute-start.5
  291.8 39.4 %collective-permute-done.7 = f32[16,128]{1,0:T(8,128)S(1)} collective-permute-done((f32[16,128]{1,0:T(8,128)S(1)}, f32[16,128]{1,0:T(8,128)S(1)}, u32[]{:S(2)}, u32[]{:S(2)}) %collective-permute-start.7) | collective-permute-done | bytes 8224 | tf_op jit(solution)/shard_map/ppermute | solution.py:500
  331.2 9.1 %collective-permute-done.6 = f32[16,128]{1,0:T(8,128)S(1)} collective-permute-done((f32[16,128]{1,0:T(8,128)S(1)}, f32[16,128]{1,0:T(8,128)S(1)}, u32[]{:S(2)}, u32[]{:S(2)}) %collective-permute-start.6) | collective-permute-done | bytes 8224 | tf_op jit(solution)/shard_map/ppermute | solution.py:500
  340.4 1.4 dispatch2.1
  341.8 4.2 %all-to-all-start.5 = ((f32[4,16,128]{2,1,0:T(8,128)}), f32[4,16,128]{2,1,0:T(8,128)S(1)}, u32[]{:S(2)}, u32[]{:S(2)}) async-start(f32[4,16,128]{2,1,0:T(8,128)} %bitcast.20), calls=%async_computation.5 | async-start | bytes 65536 | tf_op jit(solution)/shard_map/all_to_all | solution.py:528
  346.1 1.9 collective-permute-start.11
  348.0 1.1 collective-permute-done.11
  349.1 2.4 all-to-all-done.5
  352.2 3.5 all-to-all-start.6
  355.7 2.7 collective-permute-start.12
  358.5 2.8 collective-permute-done.12
  361.3 3.3 collective-permute-start.13
  364.6 2.4 volt2.1
  367.0 1.3 collective-permute-done.13
  369.3 0.9 close.1
  (65 shorter events, 2.8 us)
Async XLA Ops:
  35.6 8.9 %copy-start.20 = (f32[256]{0:T(256)S(1)}, f32[256]{0:T(256)}, u32[]{:S(2)}) copy-start(f32[256]{0:T(256)} %param.20) | copy-start | bytes 3076
  35.6 9.0 %copy-start.21 = (f32[256]{0:T(256)S(1)}, f32[256]{0:T(256)}, u32[]{:S(2)}) copy-start(f32[256]{0:T(256)} %param.19) | copy-start | bytes 3076
  35.6 63.1 %copy-start = (f32[4,256,128]{2,1,0:T(8,128)S(1)}, f32[4,256,128]{2,1,0:T(8,128)}, u32[]{:S(2)}) copy-start(f32[4,256,128]{2,1,0:T(8,128)} %dual_ref.3) | copy-start | bytes 1572868
  39.9 58.8 %all-to-all-start.1 = ((f32[64,32,128]{2,1,0:T(8,128)}), f32[64,32,128]{2,1,0:T(8,128)S(1)}, u32[]{:S(2)}, u32[]{:S(2)}) async-start(f32[64,32,128]{2,1,0:T(8,128)} %first_send.1), calls=%async_computation.1 | async-start | bytes 2097152 | tf_op jit(solution)/shard_map/all_to_all | solution.py:406
  103.5 6.1 %copy-start.13 = (s32[256]{0:T(256)S(1)}, s32[256]{0:T(256)}, u32[]{:S(2)}) copy-start(s32[256]{0:T(256)} %param.24) | copy-start | bytes 3076
  103.5 6.1 %copy-start.14 = (f32[256]{0:T(256)S(1)}, f32[256]{0:T(256)}, u32[]{:S(2)}) copy-start(f32[256]{0:T(256)} %param.26) | copy-start | bytes 3076
  103.5 6.1 %copy-start.15 = (f32[256]{0:T(256)S(1)}, f32[256]{0:T(256)}, u32[]{:S(2)}) copy-start(f32[256]{0:T(256)} %param.25) | copy-start | bytes 3076
  103.6 6.1 %copy-start.16 = (f32[256]{0:T(256)S(1)}, f32[256]{0:T(256)}, u32[]{:S(2)}) copy-start(f32[256]{0:T(256)} %param.31) | copy-start | bytes 3076
  103.6 6.1 %copy-start.17 = (f32[256]{0:T(256)S(1)}, f32[256]{0:T(256)}, u32[]{:S(2)}) copy-start(f32[256]{0:T(256)} %param.32) | copy-start | bytes 3076
  103.6 6.1 %copy-start.18 = (f32[256]{0:T(256)S(1)}, f32[256]{0:T(256)}, u32[]{:S(2)}) copy-start(f32[256]{0:T(256)} %param.33) | copy-start | bytes 3076
  103.6 6.1 %copy-start.19 = (f32[256]{0:T(256)S(1)}, f32[256]{0:T(256)}, u32[]{:S(2)}) copy-start(f32[256]{0:T(256)} %param.30) | copy-start | bytes 3076
  103.6 82.9 %copy-start.1 = (f32[2,256,128]{2,1,0:T(8,128)S(1)}, f32[2,256,128]{2,1,0:T(8,128)}, u32[]{:S(2)}) copy-start(f32[2,256,128]{2,1,0:T(8,128)} %volt_ref.1) | copy-start | bytes 786436
  103.6 82.8 %all-to-all-start.2 = ((f32[64,48,128]{2,1,0:T(8,128)}), f32[64,48,128]{2,1,0:T(8,128)S(1)}, u32[]{:S(2)}, u32[]{:S(2)}) async-start(f32[64,48,128]{2,1,0:T(8,128)} %bitcast.40), calls=%async_computation.2 | async-start | bytes 3145728 | tf_op jit(solution)/shard_map/all_to_all | solution.py:406
  190.4 60.3 %all-to-all-start.3 = ((f32[64,32,128]{2,1,0:T(8,128)}), f32[64,32,128]{2,1,0:T(8,128)S(1)}, u32[]{:S(2)}, u32[]{:S(2)}) async-start(f32[64,32,128]{2,1,0:T(8,128)} %get-tuple-element.28), calls=%async_computation.3 | async-start | bytes 2097152 | tf_op jit(solution)/shard_map/all_to_all | solution.py:406
  196.2 0.9 copy-start.2
  197.2 0.9 copy-start.4
  198.1 0.9 copy-start.6
  199.7 0.7 copy-start.9
  200.3 0.7 copy-start.11
  201.0 5.6 %collective-permute-start = (f32[16,128]{1,0:T(8,128)S(1)}, f32[16,128]{1,0:T(8,128)S(1)}, u32[]{:S(2)}, u32[]{:S(2)}) collective-permute-start(f32[16,128]{1,0:T(8,128)S(1)} %get-tuple-element.29), channel_id=1, source_target_pairs={{0,8},{8,0},{16,24},{24,16},{32,40},{40,32},{48,56},{56,48},{64,72... | collective-permute-start | bytes 24584 | tf_op jit(solution)/shard_map/ppermute | solution.py:500
  206.6 7.1 %collective-permute-start.1 = (f32[16,128]{1,0:T(8,128)S(1)}, f32[16,128]{1,0:T(8,128)S(1)}, u32[]{:S(2)}, u32[]{:S(2)}) collective-permute-start(f32[16,128]{1,0:T(8,128)S(1)} %add.42), channel_id=1, source_target_pairs={{0,16},{8,24},{16,0},{24,8},{32,48},{40,56},{48,32},{56,40},{64,80... | collective-permute-start | bytes 24584 | tf_op jit(solution)/shard_map/ppermute | solution.py:500
  213.7 28.5 %collective-permute-start.4 = (f32[16,128]{1,0:T(8,128)S(1)}, f32[16,128]{1,0:T(8,128)S(1)}, u32[]{:S(2)}, u32[]{:S(2)}) collective-permute-start(f32[16,128]{1,0:T(8,128)S(1)} %add.43), channel_id=1, source_target_pairs={{0,96},{8,104},{16,112},{24,120},{32,64},{40,72},{48,80},{56,88},{... | collective-permute-start | bytes 24584 | tf_op jit(solution)/shard_map/ppermute | solution.py:500
  218.9 23.3 %collective-permute-start.3 = (f32[16,128]{1,0:T(8,128)S(1)}, f32[16,128]{1,0:T(8,128)S(1)}, u32[]{:S(2)}, u32[]{:S(2)}) collective-permute-start(f32[16,128]{1,0:T(8,128)S(1)} %add.43), channel_id=1, source_target_pairs={{0,64},{8,72},{16,80},{24,88},{32,96},{40,104},{48,112},{56,120},{... | collective-permute-start | bytes 24584 | tf_op jit(solution)/shard_map/ppermute | solution.py:500
  220.9 21.4 %collective-permute-start.2 = (f32[16,128]{1,0:T(8,128)S(1)}, f32[16,128]{1,0:T(8,128)S(1)}, u32[]{:S(2)}, u32[]{:S(2)}) collective-permute-start(f32[16,128]{1,0:T(8,128)S(1)} %add.43), channel_id=1, source_target_pairs={{0,32},{8,40},{16,48},{24,56},{32,0},{40,8},{48,16},{56,24},{64,96... | collective-permute-start | bytes 24584 | tf_op jit(solution)/shard_map/ppermute | solution.py:500
  256.4 83.9 %copy-start.3 = (f32[256,128]{1,0:T(8,128)S(1)}, f32[256,128]{1,0:T(8,128)}, u32[]{:S(2)}) copy-start(f32[256,128]{1,0:T(8,128)} %load_ref.3) | copy-start | bytes 393220
  256.4 83.9 %copy-start.5 = (f32[256,128]{1,0:T(8,128)S(1)}, f32[256,128]{1,0:T(8,128)}, u32[]{:S(2)}) copy-start(f32[256,128]{1,0:T(8,128)} %price_ref.3) | copy-start | bytes 393220
  256.4 83.9 %copy-start.7 = (f32[256,128]{1,0:T(8,128)S(1)}, f32[256,128]{1,0:T(8,128)}, u32[]{:S(2)}) copy-start(f32[256,128]{1,0:T(8,128)} %nadual_ref.3) | copy-start | bytes 393220
  256.4 83.9 %copy-start.10 = (f32[256,128]{1,0:T(8,128)S(1)}, f32[256,128]{1,0:T(8,128)}, u32[]{:S(2)}) copy-start(f32[256,128]{1,0:T(8,128)} %copy-done.9) | copy-start | bytes 393220
  256.4 83.9 %copy-start.12 = (f32[256,128]{1,0:T(8,128)S(1)}, f32[256,128]{1,0:T(8,128)}, u32[]{:S(2)}) copy-start(f32[256,128]{1,0:T(8,128)} %copy-done.11) | copy-start | bytes 393220
  256.4 83.9 %all-to-all-start.4 = ((f32[64,48,128]{2,1,0:T(8,128)}), f32[64,48,128]{2,1,0:T(8,128)S(1)}, u32[]{:S(2)}, u32[]{:S(2)}) async-start(f32[64,48,128]{2,1,0:T(8,128)} %bitcast.39), calls=%async_computation.4 | async-start | bytes 3145728 | tf_op jit(solution)/shard_map/all_to_all | solution.py:406
  262.7 101.9 %copy-start.8 = (f32[2,256,128]{2,1,0:T(8,128)S(1)}, f32[2,256,128]{2,1,0:T(8,128)}, u32[]{:S(2)}) copy-start(f32[2,256,128]{2,1,0:T(8,128)} %get-tuple-element.33.volt_ref) | copy-start | bytes 786436
  262.7 3.2 collective-permute-start.8
  265.9 5.5 %collective-permute-start.9 = (f32[8,256]{1,0:T(8,128)S(1)}, f32[8,256]{1,0:T(8,128)S(1)}, u32[]{:S(2)}, u32[]{:S(2)}) collective-permute-start(f32[8,256]{1,0:T(8,128)S(1)} %add.50), channel_id=1, source_target_pairs={{0,2},{1,3},{2,0},{3,1},{4,6},{5,7},{6,4},{7,5},{8,10},{9,11},{10,... | collective-permute-start | bytes 24584 | tf_op jit(solution)/shard_map/ppermute | solution.py:500
  271.4 20.4 %collective-permute-start.10 = (f32[8,256]{1,0:T(8,128)S(1)}, f32[8,256]{1,0:T(8,128)S(1)}, u32[]{:S(2)}, u32[]{:S(2)}) collective-permute-start(f32[8,256]{1,0:T(8,128)S(1)} %add.51), channel_id=1, source_target_pairs={{0,4},{1,5},{2,6},{3,7},{4,0},{5,1},{6,2},{7,3},{8,12},{9,13},{10,... | collective-permute-start | bytes 24584 | tf_op jit(solution)/shard_map/ppermute | solution.py:500
  274.7 56.5 %collective-permute-start.7 = (f32[16,128]{1,0:T(8,128)S(1)}, f32[16,128]{1,0:T(8,128)S(1)}, u32[]{:S(2)}, u32[]{:S(2)}) collective-permute-start(f32[16,128]{1,0:T(8,128)S(1)} %add_add_fusion.1), channel_id=1, source_target_pairs={{0,384},{8,392},{16,400},{24,408},{32,416},{40,424},{48,432},{56,4... | collective-permute-start | bytes 24584 | tf_op jit(solution)/shard_map/ppermute | solution.py:500
  282.3 58.0 %collective-permute-start.6 = (f32[16,128]{1,0:T(8,128)S(1)}, f32[16,128]{1,0:T(8,128)S(1)}, u32[]{:S(2)}, u32[]{:S(2)}) collective-permute-start(f32[16,128]{1,0:T(8,128)S(1)} %add_add_fusion.1), channel_id=1, source_target_pairs={{0,256},{8,264},{16,272},{24,280},{32,288},{40,296},{48,304},{56,3... | collective-permute-start | bytes 24584 | tf_op jit(solution)/shard_map/ppermute | solution.py:500
  289.4 50.9 %collective-permute-start.5 = (f32[16,128]{1,0:T(8,128)S(1)}, f32[16,128]{1,0:T(8,128)S(1)}, u32[]{:S(2)}, u32[]{:S(2)}) collective-permute-start(f32[16,128]{1,0:T(8,128)S(1)} %add_add_fusion.1), channel_id=1, source_target_pairs={{0,128},{8,136},{16,144},{24,152},{32,160},{40,168},{48,176},{56,1... | collective-permute-start | bytes 24584 | tf_op jit(solution)/shard_map/ppermute | solution.py:500
  341.8 9.7 %all-to-all-start.5 = ((f32[4,16,128]{2,1,0:T(8,128)}), f32[4,16,128]{2,1,0:T(8,128)S(1)}, u32[]{:S(2)}, u32[]{:S(2)}) async-start(f32[4,16,128]{2,1,0:T(8,128)} %bitcast.20), calls=%async_computation.5 | async-start | bytes 65536 | tf_op jit(solution)/shard_map/all_to_all | solution.py:528
  346.1 3.1 collective-permute-start.11
  352.2 17.1 %all-to-all-start.6 = ((f32[16,16,128]{2,1,0:T(8,128)}), f32[16,16,128]{2,1,0:T(8,128)S(1)}, u32[]{:S(2)}, u32[]{:S(2)}) async-start(f32[16,16,128]{2,1,0:T(8,128)} %broadcast_in_dim.2), calls=%async_computation.6 | async-start | bytes 262144 | tf_op jit(solution)/shard_map/all_to_all | solution.py:533
  355.7 5.5 %collective-permute-start.12 = (f32[8,256]{1,0:T(8,128)S(1)}, f32[8,256]{1,0:T(8,128)S(1)}, u32[]{:S(2)}, u32[]{:S(2)}) collective-permute-start(f32[8,256]{1,0:T(8,128)S(1)} %add.53), channel_id=1, source_target_pairs={{0,2},{1,3},{2,0},{3,1},{4,6},{5,7},{6,4},{7,5},{8,10},{9,11},{10,... | collective-permute-start | bytes 24584 | tf_op jit(solution)/shard_map/ppermute | solution.py:500
  361.3 7.0 %collective-permute-start.13 = (f32[8,256]{1,0:T(8,128)S(1)}, f32[8,256]{1,0:T(8,128)S(1)}, u32[]{:S(2)}, u32[]{:S(2)}) collective-permute-start(f32[8,256]{1,0:T(8,128)S(1)} %add.54), channel_id=1, source_target_pairs={{0,4},{1,5},{2,6},{3,7},{4,0},{5,1},{6,2},{7,3},{8,12},{9,13},{10,... | collective-permute-start | bytes 24584 | tf_op jit(solution)/shard_map/ppermute | solution.py:500

commit v6 on v5

--- a/solution.py
+++ b/solution.py
@@ -32,6 +32,10 @@
     return pl.BlockSpec(memory_space=VMEM)
 
 
+def anywhere():
+    return pl.BlockSpec(memory_space=pl.ANY)
+
+
 def hbm():
     return pl.BlockSpec(memory_space=pltpu.HBM)
 
@@ -76,7 +80,7 @@
     return lax.dot_general(a, b, (((1,), (1,)), ((), ())), preferred_element_type=F32)
 
 
-def plan_kernel(count_ref, owner_hbm, bus_hbm, slot_ref, request_ref, owner_ref, bus_ref, sem):
+def plan_kernel(count_ref, owner_hbm, bus_hbm, near_ref, term_ref, request_ref, owner_ref, bus_ref, sem):
     fetch = copies_of([(owner_hbm, owner_ref), (bus_hbm, bus_ref)], sem)
     start_all(fetch)
     wait_all(fetch)
@@ -93,7 +97,8 @@
     )
     earlier = jnp.dot(hits.astype(BF16), before.astype(BF16), preferred_element_type=F32)
     rank = jnp.sum(hits * earlier, axis=0, keepdims=True).astype(jnp.int32)
-    slot_ref[...] = owner * CAP + rank
+    near_ref[...] = owner * (2 * CAP) + rank
+    term_ref[...] = owner * (3 * CAP) + rank
     ranks = lax.broadcasted_iota(jnp.int32, (LANES, ends), 0) == rank
     table = dot_lanes((hits * code).astype(BF16), ranks.astype(BF16))
     request_ref[...] = table.astype(jnp.int32)
@@ -125,8 +130,10 @@
     lax.fori_loop(0, groups, done, 0)
 
 
-def first_send_kernel(asked_ref, volt_hbm, out_hbm, volt_ref, row_ref, volt_sem, sem):
-    fetch = copies_of([(volt_hbm.at[c], volt_ref.at[c]) for c in range(2)], volt_sem)
+def first_send_kernel(asked_any, volt_hbm, out_hbm, asked_ref, volt_ref, row_ref, in_sem, sem):
+    fetch = copies_of(
+        [(asked_any, asked_ref)] + [(volt_hbm.at[c], volt_ref.at[c]) for c in range(2)], in_sem
+    )
     start_all(fetch)
     wait_all(fetch)
     send_rows(asked_ref, volt_ref, out_hbm, row_ref, sem)
@@ -183,12 +190,14 @@
     return (vf, af, vt, at), flow_from, flow_to
 
 
-def line_kernel(second, count_ref, slot_ref, arrived_ref, dual_ref, *refs):
+def line_kernel(second, count_ref, near_any, term_any, arrived_ref, dual_ref, *refs):
     if second:
         previous_hbm, *refs = refs
     param_ref, out_hbm, other_hbm, *refs = refs
     near_refs, term_refs = refs[:2], refs[2:4]
-    out_ref, other_ref, out_sem, other_sem, *refs = refs[4:]
+    out_ref, other_ref, near_start, term_start, out_sem, other_sem, start_sem, *refs = refs[4:]
+    index = copies_of([(near_any, near_start), (term_any, term_start)], start_sem)
+    start_all(index)
     if second:
         previous_ref, previous_sem = refs
     lines = dual_ref.shape[1]
@@ -212,16 +221,14 @@
     def gather(block, near_ref):
         for end in range(2):
             for j in range(BLOCK):
-                slot = slot_ref[end * lines + block * BLOCK + j]
-                start = slot + (slot & -CAP)
+                start = near_start[0, end * lines + block * BLOCK + j]
                 for c in range(2):
                     near_ref[2 * end + c, j : j + 1, :] = arrived_ref[pl.ds(start + c * CAP, 1), :]
 
     def scatter(block, term_ref):
         for end in range(2):
             for j in range(BLOCK):
-                slot = slot_ref[end * lines + block * BLOCK + j]
-                start = slot + 2 * (slot & -CAP)
+                start = term_start[0, end * lines + block * BLOCK + j]
                 for c in range(3):
                     out_ref[pl.ds(start + c * CAP, 1), :] = term_ref[3 * end + c, j : j + 1, :]
 
@@ -272,6 +279,7 @@
             fetch(pair).start()
     out_ref[...] = jnp.zeros_like(out_ref)
     term_refs[1][...] = jnp.zeros_like(term_refs[1])
+    wait_all(index)
     gather(0, near_refs[0])
     lax.fori_loop(0, blocks // 2, step, 0)
     scatter(blocks - 1, term_refs[1])
@@ -305,9 +313,11 @@
     return recv_ref[:, c * CAP : (c + 1) * CAP, :].reshape(recv_ref.shape[0] * CAP, LANES)
 
 
-def volt_kernel(send, asked_ref, row_ref, recv_ref, volt_ref, param_ref, volt_hbm, *refs):
+def volt_kernel(send, asked_any, row_ref, recv_ref, volt_ref, param_ref, volt_hbm, *refs):
     if send:
-        send_hbm, volt_out, rows_ref, volt_sem, sem = refs
+        send_hbm, asked_ref, volt_out, rows_ref, asked_sem, volt_sem, sem = refs
+        index = pltpu.make_async_copy(asked_any, asked_ref, asked_sem)
+        index.start()
     else:
         volt_out = volt_hbm
     hits = bus_hits(row_ref, volt_ref.shape[1])
@@ -323,6 +333,7 @@
     if send:
         keep = pltpu.make_async_copy(volt_out, volt_hbm, volt_sem)
         keep.start()
+        index.wait()
         send_rows(asked_ref, volt_out, send_hbm, rows_ref, sem)
         keep.wait()
 
@@ -405,16 +416,15 @@
     def exchange(x):
         return lax.all_to_all(x, "grid", split_axis=0, concat_axis=0, tiled=True)
 
-    slot, request = pl.pallas_call(
+    *starts, request = pl.pallas_call(
         plan_kernel,
-        out_shape=(shape((1, ends), jnp.int32), shape((ngrid, LANES), jnp.int32)),
+        out_shape=[shape((1, ends), jnp.int32)] * 2 + [shape((ngrid, LANES), jnp.int32)],
         in_specs=[smem(), hbm(), hbm()],
-        out_specs=(vmem(), vmem()),
+        out_specs=[vmem()] * 3,
         scratch_shapes=[VMEM((1, ends), jnp.int32)] * 2 + [pltpu.SemaphoreType.DMA((2,))],
         compiler_params=pltpu.CompilerParams(vmem_limit_bytes=GRANT),
         name="plan",
     )(line_count, in_hbm(endpoint_owner.reshape(1, ends)), in_hbm(endpoint_bus.reshape(1, ends)))
-    slot = slot.reshape(ends)
     asked = exchange(request)
     asked_row = asked[:, :CAP].reshape(1, ngrid * CAP)
 
@@ -432,25 +442,28 @@
     sent = pl.pallas_call(
         first_send_kernel,
         out_shape=send_hbm,
-        in_specs=[smem(), hbm()],
+        in_specs=[anywhere(), hbm()],
         out_specs=hbm(),
-        scratch_shapes=[VMEM((2, buses, LANES), F32), VMEM(send_shape, F32),
-                        pltpu.SemaphoreType.DMA((2,)), pltpu.SemaphoreType.DMA((ngrid // GROUP,))],
+        scratch_shapes=[SMEM(request.shape, jnp.int32), VMEM((2, buses, LANES), F32),
+                        VMEM(send_shape, F32), pltpu.SemaphoreType.DMA((3,)),
+                        pltpu.SemaphoreType.DMA((ngrid // GROUP,))],
         compiler_params=pltpu.CompilerParams(vmem_limit_bytes=GRANT),
         name="first_send",
     )(asked, in_hbm(volt_init))
 
     def line_call(second, arrived, previous):
         outs = [pltpu.HBM((ngrid * 3 * CAP, LANES), F32), pltpu.HBM((4, lines, LANES), F32)]
-        args = [line_count, slot, arrived.reshape(ngrid * 2 * CAP, LANES), line_dual]
+        args = [line_count, *starts, arrived.reshape(ngrid * 2 * CAP, LANES), line_dual]
         if second:
             args.append(in_hbm(previous))
         args.append(line_param)
         pair_sem = pltpu.SemaphoreType.DMA((lines // (2 * BLOCK),))
         held = VMEM((4, lines, LANES), F32)
-        specs = [smem(), smem(), vmem(), vmem()] + [hbm()] * second + [vmem()]
+        specs = [smem(), anywhere(), anywhere(), vmem(), vmem()] + [hbm()] * second + [vmem()]
         scratch = [VMEM((4, BLOCK, LANES), F32)] * 2 + [VMEM((6, BLOCK, LANES), F32)] * 2
-        scratch += [VMEM(outs[0].shape, F32), held, pltpu.SemaphoreType.DMA((PARTS,)), pair_sem]
+        scratch += [VMEM((ngrid * 3 * CAP, LANES), F32), held]
+        scratch += [SMEM((1, ends), jnp.int32)] * 2
+        scratch += [pltpu.SemaphoreType.DMA((PARTS,)), pair_sem, pltpu.SemaphoreType.DMA((2,))]
         scratch += [held, pair_sem] * second
         out, other = pl.pallas_call(
             functools.partial(line_kernel, second),
@@ -469,9 +482,10 @@
         return pl.pallas_call(
             functools.partial(volt_kernel, send),
             out_shape=outs,
-            in_specs=[smem()] + [vmem()] * 4,
+            in_specs=[anywhere()] + [vmem()] * 4,
             out_specs=[hbm()] * 2 if send else [vmem()],
-            scratch_shapes=[VMEM(outs[0].shape, F32), VMEM(send_shape, F32),
+            scratch_shapes=[SMEM(asked.shape, jnp.int32), VMEM(volt_shape, F32),
+                            VMEM(send_shape, F32), pltpu.SemaphoreType.DMA,
                             pltpu.SemaphoreType.DMA,
                             pltpu.SemaphoreType.DMA((ngrid // GROUP,))] if send else [],
             compiler_params=pltpu.CompilerParams(vmem_limit_bytes=GRANT),

time: 371 us -> 369 us (level)
  no operation moved by 1% of the time
where the time goes in v6:
time: 369 us; the launch traced here: 368 us
  waiting for transfers between devices  223 us (60%)
  starting transfers between devices  82 us (22%)
  blocking collectives  33.2 us (9%)
  Pallas kernels  21.7 us (6%)
  local copies, waits for them, and re-layouts  5.18 us (1%)
    all_to_all x4, waiting for transfers between devices, exchange(): return lax.all_to_all(x, 'grid', split_axis=0, concat_axis=0, tiled=True)  139 us
    ppermute x14, waiting for transfers between devices, near_sum(): lax.ppermute(x, axis, [(i, i ^ k * step) for i in range(size)])  81.5 us
    ppermute x14, starting transfers between devices, near_sum(): lax.ppermute(x, axis, [(i, i ^ k * step) for i in range(size)])  51.5 us
    all_to_all x1, blocking collectives, exchange(): return lax.all_to_all(x, 'grid', split_axis=0, concat_axis=0, tiled=True)  33.2 us
    all_to_all x4, starting transfers between devices, exchange(): return lax.all_to_all(x, 'grid', split_axis=0, concat_axis=0, tiled=True)  22.7 us
    pallas_call x2, Pallas kernels, line_call(): pl.pallas_call(functools.partial(line_kernel, second), out_shape=outs, in...  9.6 us
  transfers between devices with their start and end apart: 20, of which 15 were waited for; matrix products, arithmetic and copies ran while one was open for 0% of the time, Pallas kernels for 1%

profile of v6, /device:TPU:6, one launch (start us, length us, event | category | flops | bytes accessed | tf_op | source)
XLA Modules:
  0.0 367.7 jit_solution(13521727282056306765)
XLA Ops:
  1.3 1.1 plan.1
  2.4 33.2 %all_to_all.48 = s32[64,1,128]{2,1,0:T(1,128)S(1)} all-to-all(s32[64,1,128]{2,1,0:T(1,128)S(1)} %bitcast.33), channel_id=1, replica_groups=mesh['grid'=64,'scen'=8] {'grid'}, dimensions={0} | all-to-all | bytes 65536 | tf_op jit(solution)/shard_map/all_to_all | solution.py:417
  35.6 3.3 first_send.1
  38.9 4.7 %all-to-all-start.1 = ((f32[64,32,128]{2,1,0:T(8,128)}), f32[64,32,128]{2,1,0:T(8,128)S(1)}, u32[]{:S(2)}, u32[]{:S(2)}) async-start(f32[64,32,128]{2,1,0:T(8,128)} %first_send.1), calls=%async_computation.1 | async-start | bytes 2097152 | tf_op jit(solution)/shard_map/all_to_all | solution.py:417
  43.8 54.0 %all-to-all-done.1 = f32[64,32,128]{2,1,0:T(8,128)S(1)} async-done(((f32[64,32,128]{2,1,0:T(8,128)}), f32[64,32,128]{2,1,0:T(8,128)S(1)}, u32[]{:S(2)}, u32[]{:S(2)}) %all-to-all-start.1) | async-done | bytes 1048608 | tf_op jit(solution)/shard_map/all_to_all | solution.py:417
  97.7 4.6 %lines1.1 = (f32[3072,128]{1,0:T(8,128)}, f32[4,256,128]{2,1,0:T(8,128)}) custom-call(s32[1]{0:T(128)S(6)} %copy.39.count_ref, s32[1,512]{1,0:T(1,128)S(1)} %get-tuple-element.27.near_any, s32[1,512]{1,0:T(1,128)S(1)} %get-tuple-element.28.term_any, f32[2048,128]{1,0:T(8,128)S(1)} %bitcast.27, f32[4,256,128]{2,1,0:T(8,128)S(1)} %copy-done, ...), custom_call_target="tpu_custom_call" | custom-call | tf_op jit(solution)/shard_map/lines1/pallas_call | solution.py:468
  102.4 6.0 %all-to-all-start.2 = ((f32[64,48,128]{2,1,0:T(8,128)}), f32[64,48,128]{2,1,0:T(8,128)S(1)}, u32[]{:S(2)}, u32[]{:S(2)}) async-start(f32[64,48,128]{2,1,0:T(8,128)} %bitcast.37), calls=%async_computation.2 | async-start | bytes 3145728 | tf_op jit(solution)/shard_map/all_to_all | solution.py:417
  108.8 76.5 %all-to-all-done.2.recv_ref = f32[64,48,128]{2,1,0:T(8,128)S(1)} async-done(((f32[64,48,128]{2,1,0:T(8,128)}), f32[64,48,128]{2,1,0:T(8,128)S(1)}, u32[]{:S(2)}, u32[]{:S(2)}) %all-to-all-start.2) | async-done | bytes 1572896 | tf_op jit(solution)/shard_map/all_to_all | solution.py:417
  185.3 3.3 volt1.1
  188.6 5.8 %all-to-all-start.3 = ((f32[64,32,128]{2,1,0:T(8,128)}), f32[64,32,128]{2,1,0:T(8,128)S(1)}, u32[]{:S(2)}, u32[]{:S(2)}) async-start(f32[64,32,128]{2,1,0:T(8,128)} %get-tuple-element.30), calls=%async_computation.3 | async-start | bytes 2097152 | tf_op jit(solution)/shard_map/all_to_all | solution.py:417
  194.5 0.9 copy-done.2
  195.4 0.9 copy-done.4
  196.3 0.9 copy-done.6
  197.2 0.7 dispatch1.1
  197.9 0.7 copy-done.9
  199.2 3.5 collective-permute-start
  202.7 2.1 collective-permute-done
  204.8 4.9 %collective-permute-start.1 = (f32[16,128]{1,0:T(8,128)S(1)}, f32[16,128]{1,0:T(8,128)S(1)}, u32[]{:S(2)}, u32[]{:S(2)}) collective-permute-start(f32[16,128]{1,0:T(8,128)S(1)} %add.42), channel_id=1, source_target_pairs={{0,16},{8,24},{16,0},{24,8},{32,48},{40,56},{48,32},{56,40},{64,80... | collective-permute-start | bytes 24584 | tf_op jit(solution)/shard_map/ppermute | solution.py:514
  209.7 2.2 collective-permute-done.1
  211.9 5.2 %collective-permute-start.4 = (f32[16,128]{1,0:T(8,128)S(1)}, f32[16,128]{1,0:T(8,128)S(1)}, u32[]{:S(2)}, u32[]{:S(2)}) collective-permute-start(f32[16,128]{1,0:T(8,128)S(1)} %add.43), channel_id=1, source_target_pairs={{0,96},{8,104},{16,112},{24,120},{32,64},{40,72},{48,80},{56,88},{... | collective-permute-start | bytes 24584 | tf_op jit(solution)/shard_map/ppermute | solution.py:514
  217.1 1.9 collective-permute-start.3
  219.1 3.0 collective-permute-start.2
  222.1 18.4 %collective-permute-done.4 = f32[16,128]{1,0:T(8,128)S(1)} collective-permute-done((f32[16,128]{1,0:T(8,128)S(1)}, f32[16,128]{1,0:T(8,128)S(1)}, u32[]{:S(2)}, u32[]{:S(2)}) %collective-permute-start.4) | collective-permute-done | bytes 8224 | tf_op jit(solution)/shard_map/ppermute | solution.py:514
  240.4 8.5 %all-to-all-done.3 = f32[64,32,128]{2,1,0:T(8,128)S(1)} async-done(((f32[64,32,128]{2,1,0:T(8,128)}), f32[64,32,128]{2,1,0:T(8,128)S(1)}, u32[]{:S(2)}, u32[]{:S(2)}) %all-to-all-start.3) | async-done | bytes 1048608 | tf_op jit(solution)/shard_map/all_to_all | solution.py:417
  248.9 5.0 %lines2.1 = (f32[3072,128]{1,0:T(8,128)}, f32[4,256,128]{2,1,0:T(8,128)}) custom-call(s32[1]{0:T(128)S(6)} %copy.39.count_ref, s32[1,512]{1,0:T(1,128)S(1)} %get-tuple-element.27.near_any, s32[1,512]{1,0:T(1,128)S(1)} %get-tuple-element.28.term_any, f32[2048,128]{1,0:T(8,128)S(1)} %bitcast.26, f32[4,256,128]{2,1,0:T(8,128)S(1)} %copy-done, ...), custom_call_target="tpu_custom_call" | custom-call | tf_op jit(solution)/shard_map/lines2/pallas_call | solution.py:468
  254.0 6.2 %all-to-all-start.4 = ((f32[64,48,128]{2,1,0:T(8,128)}), f32[64,48,128]{2,1,0:T(8,128)S(1)}, u32[]{:S(2)}, u32[]{:S(2)}) async-start(f32[64,48,128]{2,1,0:T(8,128)} %bitcast.36), calls=%async_computation.4 | async-start | bytes 3145728 | tf_op jit(solution)/shard_map/all_to_all | solution.py:417
  260.2 2.1 collective-permute-start.8
  262.2 1.1 collective-permute-done.8
  263.4 2.7 collective-permute-start.9
  266.1 2.8 collective-permute-done.9
  268.9 3.3 collective-permute-start.10
  272.2 7.6 %collective-permute-start.7 = (f32[16,128]{1,0:T(8,128)S(1)}, f32[16,128]{1,0:T(8,128)S(1)}, u32[]{:S(2)}, u32[]{:S(2)}) collective-permute-start(f32[16,128]{1,0:T(8,128)S(1)} %add_add_fusion.1), channel_id=1, source_target_pairs={{0,384},{8,392},{16,400},{24,408},{32,416},{40,424},{48,432},{56,4... | collective-permute-start | bytes 24584 | tf_op jit(solution)/shard_map/ppermute | solution.py:514
  279.8 7.1 %collective-permute-start.6 = (f32[16,128]{1,0:T(8,128)S(1)}, f32[16,128]{1,0:T(8,128)S(1)}, u32[]{:S(2)}, u32[]{:S(2)}) collective-permute-start(f32[16,128]{1,0:T(8,128)S(1)} %add_add_fusion.1), channel_id=1, source_target_pairs={{0,256},{8,264},{16,272},{24,280},{32,288},{40,296},{48,304},{56,3... | collective-permute-start | bytes 24584 | tf_op jit(solution)/shard_map/ppermute | solution.py:514
  286.9 2.4 collective-permute-start.5
  289.3 39.4 %collective-permute-done.7 = f32[16,128]{1,0:T(8,128)S(1)} collective-permute-done((f32[16,128]{1,0:T(8,128)S(1)}, f32[16,128]{1,0:T(8,128)S(1)}, u32[]{:S(2)}, u32[]{:S(2)}) %collective-permute-start.7) | collective-permute-done | bytes 8224 | tf_op jit(solution)/shard_map/ppermute | solution.py:514
  328.7 9.1 %collective-permute-done.6 = f32[16,128]{1,0:T(8,128)S(1)} collective-permute-done((f32[16,128]{1,0:T(8,128)S(1)}, f32[16,128]{1,0:T(8,128)S(1)}, u32[]{:S(2)}, u32[]{:S(2)}) %collective-permute-start.6) | collective-permute-done | bytes 8224 | tf_op jit(solution)/shard_map/ppermute | solution.py:514
  337.9 1.4 dispatch2.1
  339.3 4.2 %all-to-all-start.5 = ((f32[4,16,128]{2,1,0:T(8,128)}), f32[4,16,128]{2,1,0:T(8,128)S(1)}, u32[]{:S(2)}, u32[]{:S(2)}) async-start(f32[4,16,128]{2,1,0:T(8,128)} %bitcast.19), calls=%async_computation.5 | async-start | bytes 65536 | tf_op jit(solution)/shard_map/all_to_all | solution.py:542
  343.6 1.9 collective-permute-start.11
  345.5 1.1 collective-permute-done.11
  346.6 2.4 all-to-all-done.5
  349.7 3.5 all-to-all-start.6
  353.2 2.7 collective-permute-start.12
  356.0 2.8 collective-permute-done.12
  358.8 3.3 collective-permute-start.13
  362.1 1.3 volt2.1
  363.4 2.4 collective-permute-done.13
  366.8 0.9 close.1
  (65 shorter events, 2.8 us)
Async XLA Ops:
  35.6 8.0 %copy-start.20 = (f32[256]{0:T(256)S(1)}, f32[256]{0:T(256)}, u32[]{:S(2)}) copy-start(f32[256]{0:T(256)} %param.20) | copy-start | bytes 3076
  35.6 8.0 %copy-start.21 = (f32[256]{0:T(256)S(1)}, f32[256]{0:T(256)}, u32[]{:S(2)}) copy-start(f32[256]{0:T(256)} %param.19) | copy-start | bytes 3076
  35.6 62.1 %copy-start = (f32[4,256,128]{2,1,0:T(8,128)S(1)}, f32[4,256,128]{2,1,0:T(8,128)}, u32[]{:S(2)}) copy-start(f32[4,256,128]{2,1,0:T(8,128)} %dual_ref.3) | copy-start | bytes 1572868
  38.9 58.8 %all-to-all-start.1 = ((f32[64,32,128]{2,1,0:T(8,128)}), f32[64,32,128]{2,1,0:T(8,128)S(1)}, u32[]{:S(2)}, u32[]{:S(2)}) async-start(f32[64,32,128]{2,1,0:T(8,128)} %first_send.1), calls=%async_computation.1 | async-start | bytes 2097152 | tf_op jit(solution)/shard_map/all_to_all | solution.py:417
  102.3 6.1 %copy-start.13 = (s32[256]{0:T(256)S(1)}, s32[256]{0:T(256)}, u32[]{:S(2)}) copy-start(s32[256]{0:T(256)} %param.24) | copy-start | bytes 3076
  102.3 6.1 %copy-start.14 = (f32[256]{0:T(256)S(1)}, f32[256]{0:T(256)}, u32[]{:S(2)}) copy-start(f32[256]{0:T(256)} %param.26) | copy-start | bytes 3076
  102.4 6.1 %copy-start.15 = (f32[256]{0:T(256)S(1)}, f32[256]{0:T(256)}, u32[]{:S(2)}) copy-start(f32[256]{0:T(256)} %param.25) | copy-start | bytes 3076
  102.4 6.1 %copy-start.16 = (f32[256]{0:T(256)S(1)}, f32[256]{0:T(256)}, u32[]{:S(2)}) copy-start(f32[256]{0:T(256)} %param.31) | copy-start | bytes 3076
  102.4 6.1 %copy-start.17 = (f32[256]{0:T(256)S(1)}, f32[256]{0:T(256)}, u32[]{:S(2)}) copy-start(f32[256]{0:T(256)} %param.32) | copy-start | bytes 3076
  102.4 6.1 %copy-start.18 = (f32[256]{0:T(256)S(1)}, f32[256]{0:T(256)}, u32[]{:S(2)}) copy-start(f32[256]{0:T(256)} %param.33) | copy-start | bytes 3076
  102.4 6.1 %copy-start.19 = (f32[256]{0:T(256)S(1)}, f32[256]{0:T(256)}, u32[]{:S(2)}) copy-start(f32[256]{0:T(256)} %param.30) | copy-start | bytes 3076
  102.4 82.9 %copy-start.1 = (f32[2,256,128]{2,1,0:T(8,128)S(1)}, f32[2,256,128]{2,1,0:T(8,128)}, u32[]{:S(2)}) copy-start(f32[2,256,128]{2,1,0:T(8,128)} %volt_ref.1) | copy-start | bytes 786436
  102.4 82.8 %all-to-all-start.2 = ((f32[64,48,128]{2,1,0:T(8,128)}), f32[64,48,128]{2,1,0:T(8,128)S(1)}, u32[]{:S(2)}, u32[]{:S(2)}) async-start(f32[64,48,128]{2,1,0:T(8,128)} %bitcast.37), calls=%async_computation.2 | async-start | bytes 3145728 | tf_op jit(solution)/shard_map/all_to_all | solution.py:417
  188.6 60.3 %all-to-all-start.3 = ((f32[64,32,128]{2,1,0:T(8,128)}), f32[64,32,128]{2,1,0:T(8,128)S(1)}, u32[]{:S(2)}, u32[]{:S(2)}) async-start(f32[64,32,128]{2,1,0:T(8,128)} %get-tuple-element.30), calls=%async_computation.3 | async-start | bytes 2097152 | tf_op jit(solution)/shard_map/all_to_all | solution.py:417
  194.4 0.9 copy-start.2
  195.4 0.9 copy-start.4
  196.3 0.9 copy-start.6
  197.9 0.7 copy-start.9
  198.5 0.7 copy-start.11
  199.2 5.6 %collective-permute-start = (f32[16,128]{1,0:T(8,128)S(1)}, f32[16,128]{1,0:T(8,128)S(1)}, u32[]{:S(2)}, u32[]{:S(2)}) collective-permute-start(f32[16,128]{1,0:T(8,128)S(1)} %get-tuple-element.31), channel_id=1, source_target_pairs={{0,8},{8,0},{16,24},{24,16},{32,40},{40,32},{48,56},{56,48},{64,72... | collective-permute-start | bytes 24584 | tf_op jit(solution)/shard_map/ppermute | solution.py:514
  204.8 7.1 %collective-permute-start.1 = (f32[16,128]{1,0:T(8,128)S(1)}, f32[16,128]{1,0:T(8,128)S(1)}, u32[]{:S(2)}, u32[]{:S(2)}) collective-permute-start(f32[16,128]{1,0:T(8,128)S(1)} %add.42), channel_id=1, source_target_pairs={{0,16},{8,24},{16,0},{24,8},{32,48},{40,56},{48,32},{56,40},{64,80... | collective-permute-start | bytes 24584 | tf_op jit(solution)/shard_map/ppermute | solution.py:514
  211.9 28.5 %collective-permute-start.4 = (f32[16,128]{1,0:T(8,128)S(1)}, f32[16,128]{1,0:T(8,128)S(1)}, u32[]{:S(2)}, u32[]{:S(2)}) collective-permute-start(f32[16,128]{1,0:T(8,128)S(1)} %add.43), channel_id=1, source_target_pairs={{0,96},{8,104},{16,112},{24,120},{32,64},{40,72},{48,80},{56,88},{... | collective-permute-start | bytes 24584 | tf_op jit(solution)/shard_map/ppermute | solution.py:514
  217.1 23.3 %collective-permute-start.3 = (f32[16,128]{1,0:T(8,128)S(1)}, f32[16,128]{1,0:T(8,128)S(1)}, u32[]{:S(2)}, u32[]{:S(2)}) collective-permute-start(f32[16,128]{1,0:T(8,128)S(1)} %add.43), channel_id=1, source_target_pairs={{0,64},{8,72},{16,80},{24,88},{32,96},{40,104},{48,112},{56,120},{... | collective-permute-start | bytes 24584 | tf_op jit(solution)/shard_map/ppermute | solution.py:514
  219.1 21.4 %collective-permute-start.2 = (f32[16,128]{1,0:T(8,128)S(1)}, f32[16,128]{1,0:T(8,128)S(1)}, u32[]{:S(2)}, u32[]{:S(2)}) collective-permute-start(f32[16,128]{1,0:T(8,128)S(1)} %add.43), channel_id=1, source_target_pairs={{0,32},{8,40},{16,48},{24,56},{32,0},{40,8},{48,16},{56,24},{64,96... | collective-permute-start | bytes 24584 | tf_op jit(solution)/shard_map/ppermute | solution.py:514
  253.9 83.9 %copy-start.3 = (f32[256,128]{1,0:T(8,128)S(1)}, f32[256,128]{1,0:T(8,128)}, u32[]{:S(2)}) copy-start(f32[256,128]{1,0:T(8,128)} %load_ref.3) | copy-start | bytes 393220
  253.9 83.9 %copy-start.5 = (f32[256,128]{1,0:T(8,128)S(1)}, f32[256,128]{1,0:T(8,128)}, u32[]{:S(2)}) copy-start(f32[256,128]{1,0:T(8,128)} %price_ref.3) | copy-start | bytes 393220
  253.9 83.9 %copy-start.7 = (f32[256,128]{1,0:T(8,128)S(1)}, f32[256,128]{1,0:T(8,128)}, u32[]{:S(2)}) copy-start(f32[256,128]{1,0:T(8,128)} %nadual_ref.3) | copy-start | bytes 393220
  253.9 83.9 %copy-start.10 = (f32[256,128]{1,0:T(8,128)S(1)}, f32[256,128]{1,0:T(8,128)}, u32[]{:S(2)}) copy-start(f32[256,128]{1,0:T(8,128)} %copy-done.9) | copy-start | bytes 393220
  254.0 83.9 %copy-start.12 = (f32[256,128]{1,0:T(8,128)S(1)}, f32[256,128]{1,0:T(8,128)}, u32[]{:S(2)}) copy-start(f32[256,128]{1,0:T(8,128)} %copy-done.11) | copy-start | bytes 393220
  254.0 83.9 %all-to-all-start.4 = ((f32[64,48,128]{2,1,0:T(8,128)}), f32[64,48,128]{2,1,0:T(8,128)S(1)}, u32[]{:S(2)}, u32[]{:S(2)}) async-start(f32[64,48,128]{2,1,0:T(8,128)} %bitcast.36), calls=%async_computation.4 | async-start | bytes 3145728 | tf_op jit(solution)/shard_map/all_to_all | solution.py:417
  260.2 101.9 %copy-start.8 = (f32[2,256,128]{2,1,0:T(8,128)S(1)}, f32[2,256,128]{2,1,0:T(8,128)}, u32[]{:S(2)}) copy-start(f32[2,256,128]{2,1,0:T(8,128)} %get-tuple-element.35.volt_ref) | copy-start | bytes 786436
  260.2 3.2 collective-permute-start.8
  263.4 5.5 %collective-permute-start.9 = (f32[8,256]{1,0:T(8,128)S(1)}, f32[8,256]{1,0:T(8,128)S(1)}, u32[]{:S(2)}, u32[]{:S(2)}) collective-permute-start(f32[8,256]{1,0:T(8,128)S(1)} %add.50), channel_id=1, source_target_pairs={{0,2},{1,3},{2,0},{3,1},{4,6},{5,7},{6,4},{7,5},{8,10},{9,11},{10,... | collective-permute-start | bytes 24584 | tf_op jit(solution)/shard_map/ppermute | solution.py:514
  268.9 20.4 %collective-permute-start.10 = (f32[8,256]{1,0:T(8,128)S(1)}, f32[8,256]{1,0:T(8,128)S(1)}, u32[]{:S(2)}, u32[]{:S(2)}) collective-permute-start(f32[8,256]{1,0:T(8,128)S(1)} %add.51), channel_id=1, source_target_pairs={{0,4},{1,5},{2,6},{3,7},{4,0},{5,1},{6,2},{7,3},{8,12},{9,13},{10,... | collective-permute-start | bytes 24584 | tf_op jit(solution)/shard_map/ppermute | solution.py:514
  272.2 56.5 %collective-permute-start.7 = (f32[16,128]{1,0:T(8,128)S(1)}, f32[16,128]{1,0:T(8,128)S(1)}, u32[]{:S(2)}, u32[]{:S(2)}) collective-permute-start(f32[16,128]{1,0:T(8,128)S(1)} %add_add_fusion.1), channel_id=1, source_target_pairs={{0,384},{8,392},{16,400},{24,408},{32,416},{40,424},{48,432},{56,4... | collective-permute-start | bytes 24584 | tf_op jit(solution)/shard_map/ppermute | solution.py:514
  279.8 58.0 %collective-permute-start.6 = (f32[16,128]{1,0:T(8,128)S(1)}, f32[16,128]{1,0:T(8,128)S(1)}, u32[]{:S(2)}, u32[]{:S(2)}) collective-permute-start(f32[16,128]{1,0:T(8,128)S(1)} %add_add_fusion.1), channel_id=1, source_target_pairs={{0,256},{8,264},{16,272},{24,280},{32,288},{40,296},{48,304},{56,3... | collective-permute-start | bytes 24584 | tf_op jit(solution)/shard_map/ppermute | solution.py:514
  286.9 50.9 %collective-permute-start.5 = (f32[16,128]{1,0:T(8,128)S(1)}, f32[16,128]{1,0:T(8,128)S(1)}, u32[]{:S(2)}, u32[]{:S(2)}) collective-permute-start(f32[16,128]{1,0:T(8,128)S(1)} %add_add_fusion.1), channel_id=1, source_target_pairs={{0,128},{8,136},{16,144},{24,152},{32,160},{40,168},{48,176},{56,1... | collective-permute-start | bytes 24584 | tf_op jit(solution)/shard_map/ppermute | solution.py:514
  339.3 9.7 %all-to-all-start.5 = ((f32[4,16,128]{2,1,0:T(8,128)}), f32[4,16,128]{2,1,0:T(8,128)S(1)}, u32[]{:S(2)}, u32[]{:S(2)}) async-start(f32[4,16,128]{2,1,0:T(8,128)} %bitcast.19), calls=%async_computation.5 | async-start | bytes 65536 | tf_op jit(solution)/shard_map/all_to_all | solution.py:542
  343.6 3.1 collective-permute-start.11
  349.7 17.1 %all-to-all-start.6 = ((f32[16,16,128]{2,1,0:T(8,128)}), f32[16,16,128]{2,1,0:T(8,128)S(1)}, u32[]{:S(2)}, u32[]{:S(2)}) async-start(f32[16,16,128]{2,1,0:T(8,128)} %broadcast_in_dim.2), calls=%async_computation.6 | async-start | bytes 262144 | tf_op jit(solution)/shard_map/all_to_all | solution.py:547
  353.2 5.5 %collective-permute-start.12 = (f32[8,256]{1,0:T(8,128)S(1)}, f32[8,256]{1,0:T(8,128)S(1)}, u32[]{:S(2)}, u32[]{:S(2)}) collective-permute-start(f32[8,256]{1,0:T(8,128)S(1)} %add.53), channel_id=1, source_target_pairs={{0,2},{1,3},{2,0},{3,1},{4,6},{5,7},{6,4},{7,5},{8,10},{9,11},{10,... | collective-permute-start | bytes 24584 | tf_op jit(solution)/shard_map/ppermute | solution.py:514
  358.8 7.0 %collective-permute-start.13 = (f32[8,256]{1,0:T(8,128)S(1)}, f32[8,256]{1,0:T(8,128)S(1)}, u32[]{:S(2)}, u32[]{:S(2)}) collective-permute-start(f32[8,256]{1,0:T(8,128)S(1)} %add.54), channel_id=1, source_target_pairs={{0,4},{1,5},{2,6},{3,7},{4,0},{5,1},{6,2},{7,3},{8,12},{9,13},{10,... | collective-permute-start | bytes 24584 | tf_op jit(solution)/shard_map/ppermute | solution.py:514

commit v7 on v6

--- a/solution.py
+++ b/solution.py
@@ -14,7 +14,6 @@
 REGION_GAIN = 10.0
 BLOCK = 16
 GROUP = 4
-PARTS = 4
 NEAR = 4
 GRANT = 16 * 2**20
 
@@ -80,7 +79,7 @@
     return lax.dot_general(a, b, (((1,), (1,)), ((), ())), preferred_element_type=F32)
 
 
-def plan_kernel(count_ref, owner_hbm, bus_hbm, near_ref, term_ref, request_ref, owner_ref, bus_ref, sem):
+def plan_kernel(count_ref, owner_hbm, bus_hbm, pair_ref, slot_ref, request_ref, owner_ref, bus_ref, sem):
     fetch = copies_of([(owner_hbm, owner_ref), (bus_hbm, bus_ref)], sem)
     start_all(fetch)
     wait_all(fetch)
@@ -97,8 +96,8 @@
     )
     earlier = jnp.dot(hits.astype(BF16), before.astype(BF16), preferred_element_type=F32)
     rank = jnp.sum(hits * earlier, axis=0, keepdims=True).astype(jnp.int32)
-    near_ref[...] = owner * (2 * CAP) + rank
-    term_ref[...] = owner * (3 * CAP) + rank
+    pair_ref[...] = owner * (2 * CAP) + rank
+    slot_ref[...] = owner * CAP + rank
     ranks = lax.broadcasted_iota(jnp.int32, (LANES, ends), 0) == rank
     table = dot_lanes((hits * code).astype(BF16), ranks.astype(BF16))
     request_ref[...] = table.astype(jnp.int32)
@@ -190,13 +189,16 @@
     return (vf, af, vt, at), flow_from, flow_to
 
 
-def line_kernel(second, count_ref, near_any, term_any, arrived_ref, dual_ref, *refs):
+def line_kernel(second, count_ref, pair_any, slot_any, arrived_ref, dual_ref, *refs):
     if second:
         previous_hbm, *refs = refs
-    param_ref, out_hbm, other_hbm, *refs = refs
-    near_refs, term_refs = refs[:2], refs[2:4]
-    out_ref, other_ref, near_start, term_start, out_sem, other_sem, start_sem, *refs = refs[4:]
-    index = copies_of([(near_any, near_start), (term_any, term_start)], start_sem)
+    count = 3 if second else 2
+    param_ref, *refs = refs
+    out_hbm, (other_hbm, *refs) = refs[:count], refs[count:]
+    near_refs, term_refs, refs = refs[:2], refs[2:4], refs[4:]
+    out_refs, (other_ref, pair_start, slot_start, *refs) = refs[:count], refs[count:]
+    out_sem, other_sem, start_sem, *refs = refs
+    index = copies_of([(pair_any, pair_start), (slot_any, slot_start)], start_sem)
     start_all(index)
     if second:
         previous_ref, previous_sem = refs
@@ -221,16 +223,21 @@
     def gather(block, near_ref):
         for end in range(2):
             for j in range(BLOCK):
-                start = near_start[0, end * lines + block * BLOCK + j]
+                start = pair_start[0, end * lines + block * BLOCK + j]
                 for c in range(2):
                     near_ref[2 * end + c, j : j + 1, :] = arrived_ref[pl.ds(start + c * CAP, 1), :]
 
     def scatter(block, term_ref):
         for end in range(2):
             for j in range(BLOCK):
-                start = term_start[0, end * lines + block * BLOCK + j]
-                for c in range(3):
-                    out_ref[pl.ds(start + c * CAP, 1), :] = term_ref[3 * end + c, j : j + 1, :]
+                slot = slot_start[0, end * lines + block * BLOCK + j]
+                if second:
+                    places = [(out_refs[c], slot) for c in range(3)]
+                else:
+                    pair = pair_start[0, end * lines + block * BLOCK + j]
+                    places = [(out_refs[0], pair), (out_refs[0], pair + CAP), (out_refs[1], slot)]
+                for c, (out_ref, row) in enumerate(places):
+                    out_ref[pl.ds(row, 1), :] = term_ref[3 * end + c, j : j + 1, :]
 
     def solve(block, near_ref, term_ref):
         base = pl.multiple_of(block * BLOCK, BLOCK)
@@ -277,15 +284,14 @@
     if second:
         for pair in range(blocks // 2):
             fetch(pair).start()
-    out_ref[...] = jnp.zeros_like(out_ref)
+    for out_ref in out_refs:
+        out_ref[...] = jnp.zeros_like(out_ref)
     term_refs[1][...] = jnp.zeros_like(term_refs[1])
     wait_all(index)
     gather(0, near_refs[0])
     lax.fori_loop(0, blocks // 2, step, 0)
     scatter(blocks - 1, term_refs[1])
-    piece = out_ref.shape[0] // PARTS
-    rows = [pl.ds(i * piece, piece) for i in range(PARTS)]
-    ship = copies_of([(out_ref.at[r], out_hbm.at[r]) for r in rows], out_sem)
+    ship = copies_of(list(zip(out_refs, out_hbm)), out_sem)
     start_all(ship)
     for pair in range(blocks // 2):
         keep(pair).wait()
@@ -313,16 +319,18 @@
     return recv_ref[:, c * CAP : (c + 1) * CAP, :].reshape(recv_ref.shape[0] * CAP, LANES)
 
 
-def volt_kernel(send, asked_any, row_ref, recv_ref, volt_ref, param_ref, volt_hbm, *refs):
+def volt_kernel(send, *refs):
     if send:
+        asked_any, row_ref, recv_ref, volt_ref, param_ref, volt_hbm, *refs = refs
+        terms = [slot_rows(recv_ref, c) for c in range(2)]
         send_hbm, asked_ref, volt_out, rows_ref, asked_sem, volt_sem, sem = refs
         index = pltpu.make_async_copy(asked_any, asked_ref, asked_sem)
         index.start()
     else:
-        volt_out = volt_hbm
+        row_ref, mag_ref, ang_ref, volt_ref, param_ref, volt_out = refs
+        terms = [slot_rows(mag_ref, 0), slot_rows(ang_ref, 0)]
     hits = bus_hits(row_ref, volt_ref.shape[1])
-    rows = jnp.concatenate([slot_rows(recv_ref, 0), slot_rows(recv_ref, 1)], axis=1)
-    pair = picked(hits, rows, 2)
+    pair = picked(hits, jnp.concatenate(terms, axis=1), 2)
     ones = jnp.ones((hits.shape[1], LANES), BF16)
     degree = jnp.dot(hits, ones, preferred_element_type=F32)
     param = param_ref[...]
@@ -346,7 +354,7 @@
     else:
         disp_out, mism_out, part_out, total_out = refs
     buses = load_ref.shape[0]
-    net = picked(bus_hits(row_ref, buses), slot_rows(recv_ref, 2), 2)
+    net = picked(bus_hits(row_ref, buses), slot_rows(recv_ref, 0), 2)
     param = param_ref[...]
     load, price, nadual = load_ref[...], price_ref[...], nadual_ref[...]
     if second:
@@ -367,9 +375,7 @@
     else:
         mism_out[...] = mismatch
     region = lax.broadcasted_iota(jnp.int32, (REGIONS, buses), 0) == region_ref[...]
-    part = picked(region.astype(BF16), mismatch, 3)
-    for copy in range(part_out.shape[0] // REGIONS):
-        part_out[copy * REGIONS : (copy + 1) * REGIONS, :] = part
+    part_out[...] = picked(region.astype(BF16), mismatch, 3)
     total = None
     ones = jnp.ones((total_out.shape[0], LANES), BF16)
     for piece in pieces(dispatch + nadual, 3):
@@ -379,10 +385,7 @@
 
 
 def close_kernel(buses_all, param_ref, regional_ref, price_ref, out_ref):
-    regional = regional_ref[0:REGIONS, :]
-    for part in range(1, regional_ref.shape[0] // REGIONS):
-        regional = regional + regional_ref[part * REGIONS : (part + 1) * REGIONS, :]
-    out_ref[...] = price_ref[...] + region_term(param_ref[...], regional, buses_all)
+    out_ref[...] = price_ref[...] + region_term(param_ref[...], regional_ref[...], buses_all)
 
 
 def on_device(
@@ -452,7 +455,8 @@
     )(asked, in_hbm(volt_init))
 
     def line_call(second, arrived, previous):
-        outs = [pltpu.HBM((ngrid * 3 * CAP, LANES), F32), pltpu.HBM((4, lines, LANES), F32)]
+        widths = [1, 1, 1] if second else [2, 1]
+        outs = [pltpu.HBM((ngrid * w * CAP, LANES), F32) for w in widths]
         args = [line_count, *starts, arrived.reshape(ngrid * 2 * CAP, LANES), line_dual]
         if second:
             args.append(in_hbm(previous))
@@ -461,28 +465,30 @@
         held = VMEM((4, lines, LANES), F32)
         specs = [smem(), anywhere(), anywhere(), vmem(), vmem()] + [hbm()] * second + [vmem()]
         scratch = [VMEM((4, BLOCK, LANES), F32)] * 2 + [VMEM((6, BLOCK, LANES), F32)] * 2
-        scratch += [VMEM((ngrid * 3 * CAP, LANES), F32), held]
+        scratch += [VMEM((ngrid * w * CAP, LANES), F32) for w in widths] + [held]
         scratch += [SMEM((1, ends), jnp.int32)] * 2
-        scratch += [pltpu.SemaphoreType.DMA((PARTS,)), pair_sem, pltpu.SemaphoreType.DMA((2,))]
+        scratch += [pltpu.SemaphoreType.DMA((len(widths),)), pair_sem,
+                    pltpu.SemaphoreType.DMA((2,))]
         scratch += [held, pair_sem] * second
-        out, other = pl.pallas_call(
+        *terms, other = pl.pallas_call(
             functools.partial(line_kernel, second),
-            out_shape=outs,
+            out_shape=outs + [pltpu.HBM((4, lines, LANES), F32)],
             in_specs=specs,
-            out_specs=[hbm(), hbm()],
+            out_specs=[hbm()] * (len(outs) + 1),
             scratch_shapes=scratch,
             compiler_params=pltpu.CompilerParams(vmem_limit_bytes=GRANT),
             name="lines2" if second else "lines1",
         )(*args)
-        return out.reshape(ngrid, 3 * CAP, LANES), other
+        return [t.reshape(ngrid, w * CAP, LANES) for t, w in zip(terms, widths)] + [other]
 
     def volt_call(send, received, volt):
         volt_shape = (2, buses, LANES)
+        args = [asked] * send + [asked_row, *received, volt, bus_param]
         outs = [pltpu.HBM(volt_shape, F32), send_hbm] if send else [shape(volt_shape, F32)]
         return pl.pallas_call(
             functools.partial(volt_kernel, send),
             out_shape=outs,
-            in_specs=[anywhere()] + [vmem()] * 4,
+            in_specs=[anywhere()] * send + [vmem()] * (len(args) - send),
             out_specs=[hbm()] * 2 if send else [vmem()],
             scratch_shapes=[SMEM(asked.shape, jnp.int32), VMEM(volt_shape, F32),
                             VMEM(send_shape, F32), pltpu.SemaphoreType.DMA,
@@ -490,12 +496,11 @@
                             pltpu.SemaphoreType.DMA((ngrid // GROUP,))] if send else [],
             compiler_params=pltpu.CompilerParams(vmem_limit_bytes=GRANT),
             name="volt1" if send else "volt2",
-        )(asked, asked_row, received, volt, bus_param)
+        )(*args)
 
     def dispatch_call(second, received, extra):
         outs = [bus_shape] if second else [bus_shape] * 2
-        copies = NEAR if second else 1
-        outs += [shape((copies * REGIONS, LANES), F32), shape((8, buses), F32)]
+        outs += [shape((REGIONS, LANES), F32), shape((8, buses), F32)]
         if second:
             outs.append(bus_shape)
         args = [asked_row, received, bus_param, region_row, load, price_init, na_dual_init]
@@ -522,31 +527,32 @@
             step *= 2
         return x
 
-    out, state = line_call(False, exchange(sent), None)
-    received = exchange(out)
-    volt, sent = volt_call(True, received, volt_init)
+    def coarse_sum(part):
+        return near_sum(part, "grid", ngrid, NEAR * NEAR, ngrid // (NEAR * NEAR))
+
+    def fine_sum(part):
+        for step in range(1, NEAR):
+            if step & (step - 1) == 0:
+                part = near_sum(part, "grid", ngrid, step, 2)
+        return near_sum(part, "grid", ngrid, NEAR, NEAR)
+
+    pair, flow, state = line_call(False, exchange(sent), None)
+    pair, flow = lax.optimization_barrier((exchange(pair), flow))
+    volt, sent = volt_call(True, [pair], volt_init)
+    sent, flow = lax.optimization_barrier((sent, exchange(flow)))
     arrived = exchange(sent)
-    disp1, mism1, part, total = dispatch_call(False, received, ())
-    for step in range(1, NEAR):
-        if step & (step - 1) == 0:
-            part = near_sum(part, "grid", ngrid, step, 2)
-    part = near_sum(part, "grid", ngrid, NEAR, NEAR)
-    arrived, part = lax.optimization_barrier((arrived, part))
-    totals = doubling_sum(total, "scen", nscen)
-    regional = near_sum(part, "grid", ngrid, NEAR * NEAR, ngrid // (NEAR * NEAR))
-    out, dual = line_call(True, arrived, state)
-    received = exchange(out)
-    dispatch, part, total, price = dispatch_call(True, received, (disp1, mism1, regional, totals))
-    near = [[i * NEAR + j for j in range(NEAR)] for i in range(ngrid // NEAR)]
-    far = [[i * NEAR + j for i in range(ngrid // NEAR)] for j in range(NEAR)]
-    part = lax.all_to_all(part, "grid", 0, 0, axis_index_groups=near, tiled=True)
-    total = near_sum(total, "scen", nscen, 1, 2)
-    part, total = lax.optimization_barrier((part, total))
-    part = jnp.sum(part.reshape(NEAR, REGIONS, LANES), axis=0)
-    part = jnp.broadcast_to(part[None], (ngrid // NEAR, REGIONS, LANES))
-    parts = lax.all_to_all(part, "grid", 0, 0, axis_index_groups=far, tiled=True)
-    commit = doubling_sum(total, "scen", nscen, 2)[0] / (scen * nscen)
-    (volt,) = volt_call(False, received, volt)
+    disp1, mism1, part, total = dispatch_call(False, flow, ())
+    arrived, part, totals = lax.optimization_barrier(
+        (arrived, fine_sum(part), doubling_sum(total, "scen", nscen))
+    )
+    mag, ang, flow, dual = line_call(True, arrived, state)
+    flow, regional, mag = lax.optimization_barrier((exchange(flow), coarse_sum(part), mag))
+    dispatch, part, total, price = dispatch_call(True, flow, (disp1, mism1, regional, totals))
+    mag, part, ang = lax.optimization_barrier((exchange(mag), fine_sum(part), ang))
+    ang = exchange(ang)
+    commit = doubling_sum(total, "scen", nscen)[0] / (scen * nscen)
+    regional = coarse_sum(part)
+    (volt,) = volt_call(False, [mag, ang], volt)
     price = pl.pallas_call(
         functools.partial(close_kernel, buses_all),
         out_shape=bus_shape,
@@ -554,7 +560,7 @@
         out_specs=vmem(),
         compiler_params=pltpu.CompilerParams(vmem_limit_bytes=GRANT),
         name="close",
-    )(bus_param, parts.reshape(ngrid // NEAR * REGIONS, LANES), price)
+    )(bus_param, regional, price)
     return (volt, dual, dispatch, price, commit)
 
 

time: 369 us -> 393 us (1.065)
  waiting for transfers between devices: 223 us -> 146 us
  blocking collectives: 33.2 us -> 93.4 us
  starting transfers between devices: 82 us -> 125 us
    all_to_all x1 -> x2, blocking collectives: 33.2 us -> 93.4 us  [exchange(): return lax.all_to_all(x, 'grid', split_axis=0, concat_axis=0, tiled=True)]
    all_to_all x4 -> x6, waiting for transfers between devices: 139 us -> 94.1 us  [exchange(): return lax.all_to_all(x, 'grid', split_axis=0, concat_axis=0, tiled=True)]
    ppermute x14 -> x22, starting transfers between devices: 51.5 us -> 86.6 us  [near_sum(): lax.ppermute(x, axis, [(i, i ^ k * step) for i in range(size)])]
    ppermute x14 -> x22, waiting for transfers between devices: 81.5 us -> 51.9 us  [near_sum(): lax.ppermute(x, axis, [(i, i ^ k * step) for i in range(size)])]
    all_to_all x4 -> x6, starting transfers between devices: 22.7 us -> 38.3 us  [exchange(): return lax.all_to_all(x, 'grid', split_axis=0, concat_axis=0, tiled=True)]
    all_to_all x2 -> x0, starting transfers between devices: 7.76 us -> none  [the longest x1 4.25 us: on_device(): lax.all_to_all(part, 'grid', 0, 0, axis_index_groups=near, tiled=True)]
  transfers between devices with their start and end apart: 20 -> 28, of which waited for: 15 -> 15; matrix products, arithmetic and copies ran while one was open for 0% -> 0% of each run, Pallas kernels for 1% -> 2%
where the time goes in v7:
time: 393 us; the launch traced here: 390 us
  waiting for transfers between devices  146 us (37%)
  starting transfers between devices  125 us (32%)
  blocking collectives  93.4 us (24%)
  Pallas kernels  21.5 us (5%)
    all_to_all x6, waiting for transfers between devices, exchange(): return lax.all_to_all(x, 'grid', split_axis=0, concat_axis=0, tiled=True)  94.1 us
    all_to_all x2, blocking collectives, exchange(): return lax.all_to_all(x, 'grid', split_axis=0, concat_axis=0, tiled=True)  93.4 us
    ppermute x22, starting transfers between devices, near_sum(): lax.ppermute(x, axis, [(i, i ^ k * step) for i in range(size)])  86.6 us
    ppermute x22, waiting for transfers between devices, near_sum(): lax.ppermute(x, axis, [(i, i ^ k * step) for i in range(size)])  51.9 us
    all_to_all x6, starting transfers between devices, exchange(): return lax.all_to_all(x, 'grid', split_axis=0, concat_axis=0, tiled=True)  38.3 us
    pallas_call x2, Pallas kernels, line_call(): pl.pallas_call(functools.partial(line_kernel, second), out_shape=outs + [...  9.49 us
  transfers between devices with their start and end apart: 28, of which 15 were waited for; matrix products, arithmetic and copies ran while one was open for 0% of the time, Pallas kernels for 2%

profile of v7, /device:TPU:6, one launch (start us, length us, event | category | flops | bytes accessed | tf_op | source)
XLA Modules:
  0.0 390.0 jit_solution(15832187577343265732)
XLA Ops:
  2.4 33.2 %all_to_all.46 = s32[64,1,128]{2,1,0:T(1,128)S(1)} all-to-all(s32[64,1,128]{2,1,0:T(1,128)S(1)} %bitcast.30), channel_id=1, replica_groups=mesh['grid'=64,'scen'=8] {'grid'}, dimensions={0} | all-to-all | bytes 65536 | tf_op jit(solution)/shard_map/all_to_all | solution.py:420
  35.6 3.3 first_send.1
  38.9 4.8 %all-to-all-start.1 = ((f32[64,32,128]{2,1,0:T(8,128)}), f32[64,32,128]{2,1,0:T(8,128)S(1)}, u32[]{:S(2)}, u32[]{:S(2)}) async-start(f32[64,32,128]{2,1,0:T(8,128)} %first_send.1), calls=%async_computation.1 | async-start | bytes 2097152 | tf_op jit(solution)/shard_map/all_to_all | solution.py:420
  44.6 53.3 %all-to-all-done.1 = f32[64,32,128]{2,1,0:T(8,128)S(1)} async-done(((f32[64,32,128]{2,1,0:T(8,128)}), f32[64,32,128]{2,1,0:T(8,128)S(1)}, u32[]{:S(2)}, u32[]{:S(2)}) %all-to-all-start.1) | async-done | bytes 1048608 | tf_op jit(solution)/shard_map/all_to_all | solution.py:420
  97.9 4.6 %lines1.1 = (f32[2048,128]{1,0:T(8,128)}, f32[1024,128]{1,0:T(8,128)}, f32[4,256,128]{2,1,0:T(8,128)}) custom-call(s32[1]{0:T(128)S(6)} %copy.39.count_ref, s32[1,512]{1,0:T(1,128)S(1)} %get-tuple-element.39.pair_any, s32[1,512]{1,0:T(1,128)S(1)} %get-tuple-element.40.slot_any, f32[2048,128]{1,0:T(8,128)S(1)} %bitcast.26, f32[4,256,128]{2,1,0:T(8,128)S(1)} %copy-done, ...), custom_call_target="tpu_custom_call" | custom-call | tf_op jit(solution)/shard_map/lines1/pallas_call | solution.py:473
  102.5 60.2 %all_to_all.47.refs_2_ = f32[64,32,128]{2,1,0:T(8,128)S(1)} all-to-all(f32[64,32,128]{2,1,0:T(8,128)} %bitcast.33), channel_id=1, replica_groups=mesh['grid'=64,'scen'=8] {'grid'}, dimensions={0} | all-to-all | bytes 2097152 | tf_op jit(solution)/shard_map/all_to_all | solution.py:420
  162.7 6.0 %all-to-all-start.3 = ((f32[64,16,128]{2,1,0:T(8,128)}), f32[64,16,128]{2,1,0:T(8,128)S(1)}, u32[]{:S(2)}, u32[]{:S(2)}) async-start(f32[64,16,128]{2,1,0:T(8,128)} %bitcast.9), calls=%async_computation.3 | async-start | bytes 1048576 | tf_op jit(solution)/shard_map/all_to_all | solution.py:420
  169.7 3.3 volt1.1
  173.0 27.2 %all-to-all-done.3.recv_ref = f32[64,16,128]{2,1,0:T(8,128)S(1)} async-done(((f32[64,16,128]{2,1,0:T(8,128)}), f32[64,16,128]{2,1,0:T(8,128)S(1)}, u32[]{:S(2)}, u32[]{:S(2)}) %all-to-all-start.3) | async-done | bytes 524320 | tf_op jit(solution)/shard_map/all_to_all | solution.py:420
  200.2 5.8 %all-to-all-start.4 = ((f32[64,32,128]{2,1,0:T(8,128)}), f32[64,32,128]{2,1,0:T(8,128)S(1)}, u32[]{:S(2)}, u32[]{:S(2)}) async-start(f32[64,32,128]{2,1,0:T(8,128)} %get-tuple-element.46), calls=%async_computation.4 | async-start | bytes 2097152 | tf_op jit(solution)/shard_map/all_to_all | solution.py:420
  206.7 1.9 collective-permute-start.5
  208.7 3.5 collective-permute-start
  212.2 2.7 collective-permute-start.6
  215.0 4.6 %collective-permute-start.1 = (f32[16,128]{1,0:T(8,128)S(1)}, f32[16,128]{1,0:T(8,128)S(1)}, u32[]{:S(2)}, u32[]{:S(2)}) collective-permute-start(f32[16,128]{1,0:T(8,128)S(1)} %add.66), channel_id=1, source_target_pairs={{0,16},{8,24},{16,0},{24,8},{32,48},{40,56},{48,32},{56,40},{64,80... | collective-permute-start | bytes 24584 | tf_op jit(solution)/shard_map/ppermute | solution.py:519
  219.6 3.0 collective-permute-start.7
  222.6 5.2 %collective-permute-start.4 = (f32[16,128]{1,0:T(8,128)S(1)}, f32[16,128]{1,0:T(8,128)S(1)}, u32[]{:S(2)}, u32[]{:S(2)}) collective-permute-start(f32[16,128]{1,0:T(8,128)S(1)} %add.67), channel_id=1, source_target_pairs={{0,96},{8,104},{16,112},{24,120},{32,64},{40,72},{48,80},{56,88},{... | collective-permute-start | bytes 24584 | tf_op jit(solution)/shard_map/ppermute | solution.py:519
  227.8 1.9 collective-permute-start.3
  229.7 3.0 collective-permute-start.2
  232.8 19.1 %collective-permute-done.4 = f32[16,128]{1,0:T(8,128)S(1)} collective-permute-done((f32[16,128]{1,0:T(8,128)S(1)}, f32[16,128]{1,0:T(8,128)S(1)}, u32[]{:S(2)}, u32[]{:S(2)}) %collective-permute-start.4) | collective-permute-done | bytes 8224 | tf_op jit(solution)/shard_map/ppermute | solution.py:519
  251.9 8.5 %all-to-all-done.4 = f32[64,32,128]{2,1,0:T(8,128)S(1)} async-done(((f32[64,32,128]{2,1,0:T(8,128)}), f32[64,32,128]{2,1,0:T(8,128)S(1)}, u32[]{:S(2)}, u32[]{:S(2)}) %all-to-all-start.4) | async-done | bytes 1048608 | tf_op jit(solution)/shard_map/all_to_all | solution.py:420
  260.4 4.9 %lines2.1 = (f32[1024,128]{1,0:T(8,128)}, f32[1024,128]{1,0:T(8,128)}, f32[1024,128]{1,0:T(8,128)}, f32[4,256,128]{2,1,0:T(8,128)}) custom-call(s32[1]{0:T(128)S(6)} %copy.39.count_ref, s32[1,512]{1,0:T(1,128)S(1)} %get-tuple-element.39.pair_any, s32[1,512]{1,0:T(1,128)S(1)} %get-tuple-element.40.slot_any, f32[2048,128]{1,0:T(8,128)S(1)} %bitcast.25, ...), custom_call_target="tpu_custom_call" | custom-call | tf_op jit(solution)/shard_map/lines2/pallas_call | solution.py:473
  265.3 6.1 %all-to-all-start.5 = ((f32[64,16,128]{2,1,0:T(8,128)}), f32[64,16,128]{2,1,0:T(8,128)S(1)}, u32[]{:S(2)}, u32[]{:S(2)}) async-start(f32[64,16,128]{2,1,0:T(8,128)} %bitcast.34), calls=%async_computation.5 | async-start | bytes 1048576 | tf_op jit(solution)/shard_map/all_to_all | solution.py:420
  271.4 7.6 %collective-permute-start.10 = (f32[16,128]{1,0:T(8,128)S(1)}, f32[16,128]{1,0:T(8,128)S(1)}, u32[]{:S(2)}, u32[]{:S(2)}) collective-permute-start(f32[16,128]{1,0:T(8,128)S(1)} %add_add_fusion.3), channel_id=1, source_target_pairs={{0,384},{8,392},{16,400},{24,408},{32,416},{40,424},{48,432},{56,4... | collective-permute-start | bytes 24584 | tf_op jit(solution)/shard_map/ppermute | solution.py:519
  279.0 7.1 %collective-permute-start.9 = (f32[16,128]{1,0:T(8,128)S(1)}, f32[16,128]{1,0:T(8,128)S(1)}, u32[]{:S(2)}, u32[]{:S(2)}) collective-permute-start(f32[16,128]{1,0:T(8,128)S(1)} %add_add_fusion.3), channel_id=1, source_target_pairs={{0,256},{8,264},{16,272},{24,280},{32,288},{40,296},{48,304},{56,3... | collective-permute-start | bytes 24584 | tf_op jit(solution)/shard_map/ppermute | solution.py:519
  286.1 2.4 collective-permute-start.8
  288.4 7.1 %collective-permute-done.10 = f32[16,128]{1,0:T(8,128)S(1)} collective-permute-done((f32[16,128]{1,0:T(8,128)S(1)}, f32[16,128]{1,0:T(8,128)S(1)}, u32[]{:S(2)}, u32[]{:S(2)}) %collective-permute-start.10) | collective-permute-done | bytes 8224 | tf_op jit(solution)/shard_map/ppermute | solution.py:519
  295.6 8.5 %collective-permute-done.9 = f32[16,128]{1,0:T(8,128)S(1)} collective-permute-done((f32[16,128]{1,0:T(8,128)S(1)}, f32[16,128]{1,0:T(8,128)S(1)}, u32[]{:S(2)}, u32[]{:S(2)}) %collective-permute-start.9) | collective-permute-done | bytes 8224 | tf_op jit(solution)/shard_map/ppermute | solution.py:519
  304.1 6.1 %all-to-all-start.6 = ((f32[64,16,128]{2,1,0:T(8,128)}), f32[64,16,128]{2,1,0:T(8,128)S(1)}, u32[]{:S(2)}, u32[]{:S(2)}) async-start(f32[64,16,128]{2,1,0:T(8,128)} %bitcast.20), calls=%async_computation.6 | async-start | bytes 1048576 | tf_op jit(solution)/shard_map/all_to_all | solution.py:420
  311.5 3.5 collective-permute-start.11
  315.0 2.1 collective-permute-done.11
  317.1 5.0 %collective-permute-start.12 = (f32[16,128]{1,0:T(8,128)S(1)}, f32[16,128]{1,0:T(8,128)S(1)}, u32[]{:S(2)}, u32[]{:S(2)}) collective-permute-start(f32[16,128]{1,0:T(8,128)S(1)} %add.77), channel_id=1, source_target_pairs={{0,16},{8,24},{16,0},{24,8},{32,48},{40,56},{48,32},{56,40},{64,80... | collective-permute-start | bytes 24584 | tf_op jit(solution)/shard_map/ppermute | solution.py:519
  322.1 2.1 collective-permute-done.12
  324.2 5.2 %collective-permute-start.15 = (f32[16,128]{1,0:T(8,128)S(1)}, f32[16,128]{1,0:T(8,128)S(1)}, u32[]{:S(2)}, u32[]{:S(2)}) collective-permute-start(f32[16,128]{1,0:T(8,128)S(1)} %add.78), channel_id=1, source_target_pairs={{0,96},{8,104},{16,112},{24,120},{32,64},{40,72},{48,80},{56,88},{... | collective-permute-start | bytes 24584 | tf_op jit(solution)/shard_map/ppermute | solution.py:519
  329.4 1.9 collective-permute-start.14
  331.3 3.0 collective-permute-start.13
  334.3 1.5 collective-permute-done.14
  336.9 5.1 %all-to-all-done.6.refs_1_ = f32[64,16,128]{2,1,0:T(8,128)S(1)} async-done(((f32[64,16,128]{2,1,0:T(8,128)}), f32[64,16,128]{2,1,0:T(8,128)S(1)}, u32[]{:S(2)}, u32[]{:S(2)}) %all-to-all-start.6) | async-done | bytes 524320 | tf_op jit(solution)/shard_map/all_to_all | solution.py:420
  342.0 9.6 %all-to-all-start.7 = ((f32[64,16,128]{2,1,0:T(8,128)}), f32[64,16,128]{2,1,0:T(8,128)S(1)}, u32[]{:S(2)}, u32[]{:S(2)}) async-start(f32[64,16,128]{2,1,0:T(8,128)} %bitcast.21), calls=%async_computation.7 | async-start | bytes 1048576 | tf_op jit(solution)/shard_map/all_to_all | solution.py:420
  351.6 2.1 collective-permute-start.19
  354.8 2.7 collective-permute-start.20
  357.5 2.8 collective-permute-done.20
  360.3 3.3 collective-permute-start.21
  363.6 7.6 %collective-permute-start.18 = (f32[16,128]{1,0:T(8,128)S(1)}, f32[16,128]{1,0:T(8,128)S(1)}, u32[]{:S(2)}, u32[]{:S(2)}) collective-permute-start(f32[16,128]{1,0:T(8,128)S(1)} %add_add_fusion.1), channel_id=1, source_target_pairs={{0,384},{8,392},{16,400},{24,408},{32,416},{40,424},{48,432},{56,4... | collective-permute-start | bytes 24584 | tf_op jit(solution)/shard_map/ppermute | solution.py:519
  371.2 7.1 %collective-permute-start.17 = (f32[16,128]{1,0:T(8,128)S(1)}, f32[16,128]{1,0:T(8,128)S(1)}, u32[]{:S(2)}, u32[]{:S(2)}) collective-permute-start(f32[16,128]{1,0:T(8,128)S(1)} %add_add_fusion.1), channel_id=1, source_target_pairs={{0,256},{8,264},{16,272},{24,280},{32,288},{40,296},{48,304},{56,3... | collective-permute-start | bytes 24584 | tf_op jit(solution)/shard_map/ppermute | solution.py:519
  378.3 2.4 collective-permute-start.16
  381.3 4.2 %collective-permute-done.17 = f32[16,128]{1,0:T(8,128)S(1)} collective-permute-done((f32[16,128]{1,0:T(8,128)S(1)}, f32[16,128]{1,0:T(8,128)S(1)}, u32[]{:S(2)}, u32[]{:S(2)}) %collective-permute-start.17) | collective-permute-done | bytes 8224 | tf_op jit(solution)/shard_map/ppermute | solution.py:519
  385.5 2.3 collective-permute-done.16
  388.7 1.3 volt2.1
  (70 shorter events, 8.6 us)
Async XLA Ops:
  38.9 4.8 %copy-start.14 = (f32[256]{0:T(256)S(1)}, f32[256]{0:T(256)}, u32[]{:S(2)}) copy-start(f32[256]{0:T(256)} %param.19) | copy-start | bytes 3076
  38.9 59.0 %copy-start = (f32[4,256,128]{2,1,0:T(8,128)S(1)}, f32[4,256,128]{2,1,0:T(8,128)}, u32[]{:S(2)}) copy-start(f32[4,256,128]{2,1,0:T(8,128)} %dual_ref.3) | copy-start | bytes 1572868
  38.9 58.9 %all-to-all-start.1 = ((f32[64,32,128]{2,1,0:T(8,128)}), f32[64,32,128]{2,1,0:T(8,128)S(1)}, u32[]{:S(2)}, u32[]{:S(2)}) async-start(f32[64,32,128]{2,1,0:T(8,128)} %first_send.1), calls=%async_computation.1 | async-start | bytes 2097152 | tf_op jit(solution)/shard_map/all_to_all | solution.py:420
  43.7 0.7 copy-start.13
  162.7 6.0 %copy-start.6 = (s32[256]{0:T(256)S(1)}, s32[256]{0:T(256)}, u32[]{:S(2)}) copy-start(s32[256]{0:T(256)} %param.24) | copy-start | bytes 3076
  162.7 6.1 %copy-start.8 = (f32[256]{0:T(256)S(1)}, f32[256]{0:T(256)}, u32[]{:S(2)}) copy-start(f32[256]{0:T(256)} %param.25) | copy-start | bytes 3076
  162.7 6.1 %copy-start.9 = (f32[256]{0:T(256)S(1)}, f32[256]{0:T(256)}, u32[]{:S(2)}) copy-start(f32[256]{0:T(256)} %param.31) | copy-start | bytes 3076
  162.7 6.1 %copy-start.10 = (f32[256]{0:T(256)S(1)}, f32[256]{0:T(256)}, u32[]{:S(2)}) copy-start(f32[256]{0:T(256)} %param.32) | copy-start | bytes 3076
  162.7 6.1 %copy-start.11 = (f32[256]{0:T(256)S(1)}, f32[256]{0:T(256)}, u32[]{:S(2)}) copy-start(f32[256]{0:T(256)} %param.33) | copy-start | bytes 3076
  162.7 6.1 %copy-start.12 = (f32[256]{0:T(256)S(1)}, f32[256]{0:T(256)}, u32[]{:S(2)}) copy-start(f32[256]{0:T(256)} %param.30) | copy-start | bytes 3076
  162.7 6.9 %copy-start.1 = (f32[2,256,128]{2,1,0:T(8,128)S(1)}, f32[2,256,128]{2,1,0:T(8,128)}, u32[]{:S(2)}) copy-start(f32[2,256,128]{2,1,0:T(8,128)} %refs_3_.1) | copy-start | bytes 786436
  162.7 37.5 %all-to-all-start.3 = ((f32[64,16,128]{2,1,0:T(8,128)}), f32[64,16,128]{2,1,0:T(8,128)S(1)}, u32[]{:S(2)}, u32[]{:S(2)}) async-start(f32[64,16,128]{2,1,0:T(8,128)} %bitcast.9), calls=%async_computation.3 | async-start | bytes 1048576 | tf_op jit(solution)/shard_map/all_to_all | solution.py:420
  168.7 0.7 copy-start.7
  200.2 5.8 %copy-start.2 = (f32[256,128]{1,0:T(8,128)S(1)}, f32[256,128]{1,0:T(8,128)}, u32[]{:S(2)}) copy-start(f32[256,128]{1,0:T(8,128)} %load_ref.3) | copy-start | bytes 393220
  200.2 5.8 %copy-start.3 = (f32[256,128]{1,0:T(8,128)S(1)}, f32[256,128]{1,0:T(8,128)}, u32[]{:S(2)}) copy-start(f32[256,128]{1,0:T(8,128)} %price_ref.3) | copy-start | bytes 393220
  200.2 5.8 %copy-start.4 = (f32[256,128]{1,0:T(8,128)S(1)}, f32[256,128]{1,0:T(8,128)}, u32[]{:S(2)}) copy-start(f32[256,128]{1,0:T(8,128)} %nadual_ref.3) | copy-start | bytes 393220
  200.2 60.2 %all-to-all-start.4 = ((f32[64,32,128]{2,1,0:T(8,128)}), f32[64,32,128]{2,1,0:T(8,128)S(1)}, u32[]{:S(2)}, u32[]{:S(2)}) async-start(f32[64,32,128]{2,1,0:T(8,128)} %get-tuple-element.46), calls=%async_computation.4 | async-start | bytes 2097152 | tf_op jit(solution)/shard_map/all_to_all | solution.py:420
  206.7 5.4 %collective-permute-start.5 = (f32[8,256]{1,0:T(8,128)S(1)}, f32[8,256]{1,0:T(8,128)S(1)}, u32[]{:S(2)}, u32[]{:S(2)}) collective-permute-start(f32[8,256]{1,0:T(8,128)S(1)} %get-tuple-element.49), channel_id=1, source_target_pairs={{0,1},{1,0},{2,3},{3,2},{4,5},{5,4},{6,7},{7,6},{8,9},{9,8},{10,11... | collective-permute-start | bytes 24584 | tf_op jit(solution)/shard_map/ppermute | solution.py:519
  208.7 6.3 %collective-permute-start = (f32[16,128]{1,0:T(8,128)S(1)}, f32[16,128]{1,0:T(8,128)S(1)}, u32[]{:S(2)}, u32[]{:S(2)}) collective-permute-start(f32[16,128]{1,0:T(8,128)S(1)} %get-tuple-element.48), channel_id=1, source_target_pairs={{0,8},{8,0},{16,24},{24,16},{32,40},{40,32},{48,56},{56,48},{64,72... | collective-permute-start | bytes 24584 | tf_op jit(solution)/shard_map/ppermute | solution.py:519
  212.2 7.4 %collective-permute-start.6 = (f32[8,256]{1,0:T(8,128)S(1)}, f32[8,256]{1,0:T(8,128)S(1)}, u32[]{:S(2)}, u32[]{:S(2)}) collective-permute-start(f32[8,256]{1,0:T(8,128)S(1)} %add.71), channel_id=1, source_target_pairs={{0,2},{1,3},{2,0},{3,1},{4,6},{5,7},{6,4},{7,5},{8,10},{9,11},{10,... | collective-permute-start | bytes 24584 | tf_op jit(solution)/shard_map/ppermute | solution.py:519
  215.0 7.6 %collective-permute-start.1 = (f32[16,128]{1,0:T(8,128)S(1)}, f32[16,128]{1,0:T(8,128)S(1)}, u32[]{:S(2)}, u32[]{:S(2)}) collective-permute-start(f32[16,128]{1,0:T(8,128)S(1)} %add.66), channel_id=1, source_target_pairs={{0,16},{8,24},{16,0},{24,8},{32,48},{40,56},{48,32},{56,40},{64,80... | collective-permute-start | bytes 24584 | tf_op jit(solution)/shard_map/ppermute | solution.py:519
  219.6 13.2 %collective-permute-start.7 = (f32[8,256]{1,0:T(8,128)S(1)}, f32[8,256]{1,0:T(8,128)S(1)}, u32[]{:S(2)}, u32[]{:S(2)}) collective-permute-start(f32[8,256]{1,0:T(8,128)S(1)} %add.72), channel_id=1, source_target_pairs={{0,4},{1,5},{2,6},{3,7},{4,0},{5,1},{6,2},{7,3},{8,12},{9,13},{10,... | collective-permute-start | bytes 24584 | tf_op jit(solution)/shard_map/ppermute | solution.py:519
  222.6 29.3 %collective-permute-start.4 = (f32[16,128]{1,0:T(8,128)S(1)}, f32[16,128]{1,0:T(8,128)S(1)}, u32[]{:S(2)}, u32[]{:S(2)}) collective-permute-start(f32[16,128]{1,0:T(8,128)S(1)} %add.67), channel_id=1, source_target_pairs={{0,96},{8,104},{16,112},{24,120},{32,64},{40,72},{48,80},{56,88},{... | collective-permute-start | bytes 24584 | tf_op jit(solution)/shard_map/ppermute | solution.py:519
  227.8 24.1 %collective-permute-start.3 = (f32[16,128]{1,0:T(8,128)S(1)}, f32[16,128]{1,0:T(8,128)S(1)}, u32[]{:S(2)}, u32[]{:S(2)}) collective-permute-start(f32[16,128]{1,0:T(8,128)S(1)} %add.67), channel_id=1, source_target_pairs={{0,64},{8,72},{16,80},{24,88},{32,96},{40,104},{48,112},{56,120},{... | collective-permute-start | bytes 24584 | tf_op jit(solution)/shard_map/ppermute | solution.py:519
  229.7 22.2 %collective-permute-start.2 = (f32[16,128]{1,0:T(8,128)S(1)}, f32[16,128]{1,0:T(8,128)S(1)}, u32[]{:S(2)}, u32[]{:S(2)}) collective-permute-start(f32[16,128]{1,0:T(8,128)S(1)} %add.67), channel_id=1, source_target_pairs={{0,32},{8,40},{16,48},{24,56},{32,0},{40,8},{48,16},{56,24},{64,96... | collective-permute-start | bytes 24584 | tf_op jit(solution)/shard_map/ppermute | solution.py:519
  265.3 38.8 %all-to-all-start.5 = ((f32[64,16,128]{2,1,0:T(8,128)}), f32[64,16,128]{2,1,0:T(8,128)S(1)}, u32[]{:S(2)}, u32[]{:S(2)}) async-start(f32[64,16,128]{2,1,0:T(8,128)} %bitcast.34), calls=%async_computation.5 | async-start | bytes 1048576 | tf_op jit(solution)/shard_map/all_to_all | solution.py:420
  271.4 24.2 %collective-permute-start.10 = (f32[16,128]{1,0:T(8,128)S(1)}, f32[16,128]{1,0:T(8,128)S(1)}, u32[]{:S(2)}, u32[]{:S(2)}) collective-permute-start(f32[16,128]{1,0:T(8,128)S(1)} %add_add_fusion.3), channel_id=1, source_target_pairs={{0,384},{8,392},{16,400},{24,408},{32,416},{40,424},{48,432},{56,4... | collective-permute-start | bytes 24584 | tf_op jit(solution)/shard_map/ppermute | solution.py:519
  279.0 25.1 %collective-permute-start.9 = (f32[16,128]{1,0:T(8,128)S(1)}, f32[16,128]{1,0:T(8,128)S(1)}, u32[]{:S(2)}, u32[]{:S(2)}) collective-permute-start(f32[16,128]{1,0:T(8,128)S(1)} %add_add_fusion.3), channel_id=1, source_target_pairs={{0,256},{8,264},{16,272},{24,280},{32,288},{40,296},{48,304},{56,3... | collective-permute-start | bytes 24584 | tf_op jit(solution)/shard_map/ppermute | solution.py:519
  286.1 18.0 %collective-permute-start.8 = (f32[16,128]{1,0:T(8,128)S(1)}, f32[16,128]{1,0:T(8,128)S(1)}, u32[]{:S(2)}, u32[]{:S(2)}) collective-permute-start(f32[16,128]{1,0:T(8,128)S(1)} %add_add_fusion.3), channel_id=1, source_target_pairs={{0,128},{8,136},{16,144},{24,152},{32,160},{40,168},{48,176},{56,1... | collective-permute-start | bytes 24584 | tf_op jit(solution)/shard_map/ppermute | solution.py:519
  304.1 37.9 %all-to-all-start.6 = ((f32[64,16,128]{2,1,0:T(8,128)}), f32[64,16,128]{2,1,0:T(8,128)S(1)}, u32[]{:S(2)}, u32[]{:S(2)}) async-start(f32[64,16,128]{2,1,0:T(8,128)} %bitcast.20), calls=%async_computation.6 | async-start | bytes 1048576 | tf_op jit(solution)/shard_map/all_to_all | solution.py:420
  311.5 5.5 %collective-permute-start.11 = (f32[16,128]{1,0:T(8,128)S(1)}, f32[16,128]{1,0:T(8,128)S(1)}, u32[]{:S(2)}, u32[]{:S(2)}) collective-permute-start(f32[16,128]{1,0:T(8,128)S(1)} %get-tuple-element.61), channel_id=1, source_target_pairs={{0,8},{8,0},{16,24},{24,16},{32,40},{40,32},{48,56},{56,48},{64,72... | collective-permute-start | bytes 24584 | tf_op jit(solution)/shard_map/ppermute | solution.py:519
  317.1 7.1 %collective-permute-start.12 = (f32[16,128]{1,0:T(8,128)S(1)}, f32[16,128]{1,0:T(8,128)S(1)}, u32[]{:S(2)}, u32[]{:S(2)}) collective-permute-start(f32[16,128]{1,0:T(8,128)S(1)} %add.77), channel_id=1, source_target_pairs={{0,16},{8,24},{16,0},{24,8},{32,48},{40,56},{48,32},{56,40},{64,80... | collective-permute-start | bytes 24584 | tf_op jit(solution)/shard_map/ppermute | solution.py:519
  324.2 10.1 %collective-permute-start.15 = (f32[16,128]{1,0:T(8,128)S(1)}, f32[16,128]{1,0:T(8,128)S(1)}, u32[]{:S(2)}, u32[]{:S(2)}) collective-permute-start(f32[16,128]{1,0:T(8,128)S(1)} %add.78), channel_id=1, source_target_pairs={{0,96},{8,104},{16,112},{24,120},{32,64},{40,72},{48,80},{56,88},{... | collective-permute-start | bytes 24584 | tf_op jit(solution)/shard_map/ppermute | solution.py:519
  329.4 6.4 %collective-permute-start.14 = (f32[16,128]{1,0:T(8,128)S(1)}, f32[16,128]{1,0:T(8,128)S(1)}, u32[]{:S(2)}, u32[]{:S(2)}) collective-permute-start(f32[16,128]{1,0:T(8,128)S(1)} %add.78), channel_id=1, source_target_pairs={{0,64},{8,72},{16,80},{24,88},{32,96},{40,104},{48,112},{56,120},{... | collective-permute-start | bytes 24584 | tf_op jit(solution)/shard_map/ppermute | solution.py:519
  331.3 5.5 %collective-permute-start.13 = (f32[16,128]{1,0:T(8,128)S(1)}, f32[16,128]{1,0:T(8,128)S(1)}, u32[]{:S(2)}, u32[]{:S(2)}) collective-permute-start(f32[16,128]{1,0:T(8,128)S(1)} %add.78), channel_id=1, source_target_pairs={{0,32},{8,40},{16,48},{24,56},{32,0},{40,8},{48,16},{56,24},{64,96... | collective-permute-start | bytes 24584 | tf_op jit(solution)/shard_map/ppermute | solution.py:519
  342.0 46.7 %all-to-all-start.7 = ((f32[64,16,128]{2,1,0:T(8,128)}), f32[64,16,128]{2,1,0:T(8,128)S(1)}, u32[]{:S(2)}, u32[]{:S(2)}) async-start(f32[64,16,128]{2,1,0:T(8,128)} %bitcast.21), calls=%async_computation.7 | async-start | bytes 1048576 | tf_op jit(solution)/shard_map/all_to_all | solution.py:420
  351.6 37.1 %copy-start.5 = (f32[2,256,128]{2,1,0:T(8,128)S(1)}, f32[2,256,128]{2,1,0:T(8,128)}, u32[]{:S(2)}) copy-start(f32[2,256,128]{2,1,0:T(8,128)} %get-tuple-element.65.refs_3_) | copy-start | bytes 786436
  351.6 3.2 collective-permute-start.19
  354.8 5.5 %collective-permute-start.20 = (f32[8,256]{1,0:T(8,128)S(1)}, f32[8,256]{1,0:T(8,128)S(1)}, u32[]{:S(2)}, u32[]{:S(2)}) collective-permute-start(f32[8,256]{1,0:T(8,128)S(1)} %add.85), channel_id=1, source_target_pairs={{0,2},{1,3},{2,0},{3,1},{4,6},{5,7},{6,4},{7,5},{8,10},{9,11},{10,... | collective-permute-start | bytes 24584 | tf_op jit(solution)/shard_map/ppermute | solution.py:519
  360.3 20.4 %collective-permute-start.21 = (f32[8,256]{1,0:T(8,128)S(1)}, f32[8,256]{1,0:T(8,128)S(1)}, u32[]{:S(2)}, u32[]{:S(2)}) collective-permute-start(f32[8,256]{1,0:T(8,128)S(1)} %add.86), channel_id=1, source_target_pairs={{0,4},{1,5},{2,6},{3,7},{4,0},{5,1},{6,2},{7,3},{8,12},{9,13},{10,... | collective-permute-start | bytes 24584 | tf_op jit(solution)/shard_map/ppermute | solution.py:519
  363.6 17.6 %collective-permute-start.18 = (f32[16,128]{1,0:T(8,128)S(1)}, f32[16,128]{1,0:T(8,128)S(1)}, u32[]{:S(2)}, u32[]{:S(2)}) collective-permute-start(f32[16,128]{1,0:T(8,128)S(1)} %add_add_fusion.1), channel_id=1, source_target_pairs={{0,384},{8,392},{16,400},{24,408},{32,416},{40,424},{48,432},{56,4... | collective-permute-start | bytes 24584 | tf_op jit(solution)/shard_map/ppermute | solution.py:519
  371.2 14.3 %collective-permute-start.17 = (f32[16,128]{1,0:T(8,128)S(1)}, f32[16,128]{1,0:T(8,128)S(1)}, u32[]{:S(2)}, u32[]{:S(2)}) collective-permute-start(f32[16,128]{1,0:T(8,128)S(1)} %add_add_fusion.1), channel_id=1, source_target_pairs={{0,256},{8,264},{16,272},{24,280},{32,288},{40,296},{48,304},{56,3... | collective-permute-start | bytes 24584 | tf_op jit(solution)/shard_map/ppermute | solution.py:519
  378.3 9.5 %collective-permute-start.16 = (f32[16,128]{1,0:T(8,128)S(1)}, f32[16,128]{1,0:T(8,128)S(1)}, u32[]{:S(2)}, u32[]{:S(2)}) collective-permute-start(f32[16,128]{1,0:T(8,128)S(1)} %add_add_fusion.1), channel_id=1, source_target_pairs={{0,128},{8,136},{16,144},{24,152},{32,160},{40,168},{48,176},{56,1... | collective-permute-start | bytes 24584 | tf_op jit(solution)/shard_map/ppermute | solution.py:519

commit v8 on v6

--- a/solution.py
+++ b/solution.py
@@ -14,6 +14,7 @@
 REGION_GAIN = 10.0
 BLOCK = 16
 GROUP = 4
+SPARE = 8
 PARTS = 4
 NEAR = 4
 GRANT = 16 * 2**20
@@ -80,7 +81,7 @@
     return lax.dot_general(a, b, (((1,), (1,)), ((), ())), preferred_element_type=F32)
 
 
-def plan_kernel(count_ref, owner_hbm, bus_hbm, near_ref, term_ref, request_ref, owner_ref, bus_ref, sem):
+def plan_kernel(buses, count_ref, owner_hbm, bus_hbm, near_ref, term_ref, request_ref, owner_ref, bus_ref, sem):
     fetch = copies_of([(owner_hbm, owner_ref), (bus_hbm, bus_ref)], sem)
     start_all(fetch)
     wait_all(fetch)
@@ -89,7 +90,7 @@
     owner = owner_ref[...]
     end_id = lax.broadcasted_iota(jnp.int32, (1, ends), 1)
     live = lax.rem(end_id, ends // 2) < count_ref[0]
-    code = jnp.where(live, bus_ref[...] + 1, 0).astype(F32)
+    code = jnp.where(live, bus_ref[...] - buses, 0).astype(F32)
     hits = lax.broadcasted_iota(jnp.int32, (owners, ends), 0) == owner
     hits = hits.astype(F32)
     before = lax.broadcasted_iota(jnp.int32, (ends, ends), 0) < lax.broadcasted_iota(
@@ -101,11 +102,10 @@
     term_ref[...] = owner * (3 * CAP) + rank
     ranks = lax.broadcasted_iota(jnp.int32, (LANES, ends), 0) == rank
     table = dot_lanes((hits * code).astype(BF16), ranks.astype(BF16))
-    request_ref[...] = table.astype(jnp.int32)
+    request_ref[...] = table.astype(jnp.int32) + buses
 
 
 def send_rows(asked_ref, volt_ref, out_hbm, row_ref, sem):
-    buses = volt_ref.shape[1]
     groups = row_ref.shape[0] // GROUP
 
     def ship(group):
@@ -116,7 +116,7 @@
         for i in range(GROUP):
             o = group * GROUP + i
             for r in range(CAP):
-                bus = (asked_ref[o, r] - 1) & (buses - 1)
+                bus = asked_ref[o, r]
                 for c in range(2):
                     row_ref[o, c * CAP + r : c * CAP + r + 1, :] = volt_ref[c, pl.ds(bus, 1), :]
         ship(group).start()
@@ -130,11 +130,17 @@
     lax.fori_loop(0, groups, done, 0)
 
 
+def clear_spare(volt_ref, buses):
+    volt_ref[:, buses:, :] = jnp.zeros((2, SPARE, LANES), F32)
+
+
 def first_send_kernel(asked_any, volt_hbm, out_hbm, asked_ref, volt_ref, row_ref, in_sem, sem):
+    buses = volt_hbm.shape[1]
     fetch = copies_of(
-        [(asked_any, asked_ref)] + [(volt_hbm.at[c], volt_ref.at[c]) for c in range(2)], in_sem
+        [(asked_any, asked_ref)] + [(volt_hbm.at[c], volt_ref.at[c, 0:buses]) for c in range(2)], in_sem
     )
     start_all(fetch)
+    clear_spare(volt_ref, buses)
     wait_all(fetch)
     send_rows(asked_ref, volt_ref, out_hbm, row_ref, sem)
 
@@ -305,7 +311,7 @@
 
 def bus_hits(row_ref, buses):
     slots = row_ref.shape[1]
-    ids = lax.broadcasted_iota(jnp.int32, (buses, slots), 0) + 1
+    ids = lax.broadcasted_iota(jnp.int32, (buses, slots), 0)
     return (ids == row_ref[...]).astype(BF16)
 
 
@@ -328,11 +334,13 @@
     param = param_ref[...]
     weight = column(param, 0)
     inverse = 1.0 / (degree + weight)
-    volt_out[0] = (pair[:, :LANES] + weight * column(param, 1)) * inverse
-    volt_out[1] = (pair[:, LANES:] + weight * volt_ref[1]) * inverse
+    buses = volt_ref.shape[1]
+    volt_out[0, 0:buses, :] = (pair[:, :LANES] + weight * column(param, 1)) * inverse
+    volt_out[1, 0:buses, :] = (pair[:, LANES:] + weight * volt_ref[1]) * inverse
     if send:
-        keep = pltpu.make_async_copy(volt_out, volt_hbm, volt_sem)
+        keep = pltpu.make_async_copy(volt_out.at[:, 0:buses], volt_hbm, volt_sem)
         keep.start()
+        clear_spare(volt_out, buses)
         index.wait()
         send_rows(asked_ref, volt_out, send_hbm, rows_ref, sem)
         keep.wait()
@@ -417,7 +425,7 @@
         return lax.all_to_all(x, "grid", split_axis=0, concat_axis=0, tiled=True)
 
     *starts, request = pl.pallas_call(
-        plan_kernel,
+        functools.partial(plan_kernel, buses),
         out_shape=[shape((1, ends), jnp.int32)] * 2 + [shape((ngrid, LANES), jnp.int32)],
         in_specs=[smem(), hbm(), hbm()],
         out_specs=[vmem()] * 3,
@@ -444,7 +452,7 @@
         out_shape=send_hbm,
         in_specs=[anywhere(), hbm()],
         out_specs=hbm(),
-        scratch_shapes=[SMEM(request.shape, jnp.int32), VMEM((2, buses, LANES), F32),
+        scratch_shapes=[SMEM(request.shape, jnp.int32), VMEM((2, buses + SPARE, LANES), F32),
                         VMEM(send_shape, F32), pltpu.SemaphoreType.DMA((3,)),
                         pltpu.SemaphoreType.DMA((ngrid // GROUP,))],
         compiler_params=pltpu.CompilerParams(vmem_limit_bytes=GRANT),
@@ -484,7 +492,8 @@
             out_shape=outs,
             in_specs=[anywhere()] + [vmem()] * 4,
             out_specs=[hbm()] * 2 if send else [vmem()],
-            scratch_shapes=[SMEM(asked.shape, jnp.int32), VMEM(volt_shape, F32),
+            scratch_shapes=[SMEM(asked.shape, jnp.int32),
+                            VMEM((2, buses + SPARE, LANES), F32),
                             VMEM(send_shape, F32), pltpu.SemaphoreType.DMA,
                             pltpu.SemaphoreType.DMA,
                             pltpu.SemaphoreType.DMA((ngrid // GROUP,))] if send else [],

time: 369 us -> 368 us (level)
  no operation moved by 1% of the time
where the time goes in v8:
time: 368 us; the launch traced here: 367 us
  waiting for transfers between devices  223 us (61%)
  starting transfers between devices  82 us (22%)
  blocking collectives  33.2 us (9%)
  Pallas kernels  21.2 us (6%)
  local copies, waits for them, and re-layouts  5.19 us (1%)
    all_to_all x4, waiting for transfers between devices, exchange(): return lax.all_to_all(x, 'grid', split_axis=0, concat_axis=0, tiled=True)  139 us
    ppermute x14, waiting for transfers between devices, near_sum(): lax.ppermute(x, axis, [(i, i ^ k * step) for i in range(size)])  81.5 us
    ppermute x14, starting transfers between devices, near_sum(): lax.ppermute(x, axis, [(i, i ^ k * step) for i in range(size)])  51.5 us
    all_to_all x1, blocking collectives, exchange(): return lax.all_to_all(x, 'grid', split_axis=0, concat_axis=0, tiled=True)  33.2 us
    all_to_all x4, starting transfers between devices, exchange(): return lax.all_to_all(x, 'grid', split_axis=0, concat_axis=0, tiled=True)  22.7 us
    pallas_call x2, Pallas kernels, line_call(): pl.pallas_call(functools.partial(line_kernel, second), out_shape=outs, in...  9.6 us
  transfers between devices with their start and end apart: 20, of which 15 were waited for; matrix products, arithmetic and copies ran while one was open for 0% of the time, Pallas kernels for 1%

profile of v8, /device:TPU:6, one launch (start us, length us, event | category | flops | bytes accessed | tf_op | source)
XLA Modules:
  0.0 367.2 jit_solution(2593856481330639614)
XLA Ops:
  1.3 1.1 plan.1
  2.4 33.2 %all_to_all.48 = s32[64,1,128]{2,1,0:T(1,128)S(1)} all-to-all(s32[64,1,128]{2,1,0:T(1,128)S(1)} %bitcast.33), channel_id=1, replica_groups=mesh['grid'=64,'scen'=8] {'grid'}, dimensions={0} | all-to-all | bytes 65536 | tf_op jit(solution)/shard_map/all_to_all | solution.py:425
  35.6 3.0 first_send.1
  38.6 4.7 %all-to-all-start.1 = ((f32[64,32,128]{2,1,0:T(8,128)}), f32[64,32,128]{2,1,0:T(8,128)S(1)}, u32[]{:S(2)}, u32[]{:S(2)}) async-start(f32[64,32,128]{2,1,0:T(8,128)} %first_send.1), calls=%async_computation.1 | async-start | bytes 2097152 | tf_op jit(solution)/shard_map/all_to_all | solution.py:425
  43.5 54.0 %all-to-all-done.1 = f32[64,32,128]{2,1,0:T(8,128)S(1)} async-done(((f32[64,32,128]{2,1,0:T(8,128)}), f32[64,32,128]{2,1,0:T(8,128)S(1)}, u32[]{:S(2)}, u32[]{:S(2)}) %all-to-all-start.1) | async-done | bytes 1048608 | tf_op jit(solution)/shard_map/all_to_all | solution.py:425
  97.5 4.6 %lines1.1 = (f32[3072,128]{1,0:T(8,128)}, f32[4,256,128]{2,1,0:T(8,128)}) custom-call(s32[1]{0:T(128)S(6)} %copy.39.count_ref, s32[1,512]{1,0:T(1,128)S(1)} %get-tuple-element.27.near_any, s32[1,512]{1,0:T(1,128)S(1)} %get-tuple-element.28.term_any, f32[2048,128]{1,0:T(8,128)S(1)} %bitcast.27, f32[4,256,128]{2,1,0:T(8,128)S(1)} %copy-done, ...), custom_call_target="tpu_custom_call" | custom-call | tf_op jit(solution)/shard_map/lines1/pallas_call | solution.py:476
  102.2 6.0 %all-to-all-start.2 = ((f32[64,48,128]{2,1,0:T(8,128)}), f32[64,48,128]{2,1,0:T(8,128)S(1)}, u32[]{:S(2)}, u32[]{:S(2)}) async-start(f32[64,48,128]{2,1,0:T(8,128)} %bitcast.37), calls=%async_computation.2 | async-start | bytes 3145728 | tf_op jit(solution)/shard_map/all_to_all | solution.py:425
  108.5 76.5 %all-to-all-done.2.recv_ref = f32[64,48,128]{2,1,0:T(8,128)S(1)} async-done(((f32[64,48,128]{2,1,0:T(8,128)}), f32[64,48,128]{2,1,0:T(8,128)S(1)}, u32[]{:S(2)}, u32[]{:S(2)}) %all-to-all-start.2) | async-done | bytes 1572896 | tf_op jit(solution)/shard_map/all_to_all | solution.py:425
  185.0 3.0 volt1.1
  188.0 5.8 %all-to-all-start.3 = ((f32[64,32,128]{2,1,0:T(8,128)}), f32[64,32,128]{2,1,0:T(8,128)S(1)}, u32[]{:S(2)}, u32[]{:S(2)}) async-start(f32[64,32,128]{2,1,0:T(8,128)} %get-tuple-element.30), calls=%async_computation.3 | async-start | bytes 2097152 | tf_op jit(solution)/shard_map/all_to_all | solution.py:425
  193.9 0.9 copy-done.2
  194.8 0.9 copy-done.4
  195.7 0.9 copy-done.6
  196.6 0.7 dispatch1.1
  197.3 0.7 copy-done.9
  198.7 3.5 collective-permute-start
  202.1 2.1 collective-permute-done
  204.3 4.9 %collective-permute-start.1 = (f32[16,128]{1,0:T(8,128)S(1)}, f32[16,128]{1,0:T(8,128)S(1)}, u32[]{:S(2)}, u32[]{:S(2)}) collective-permute-start(f32[16,128]{1,0:T(8,128)S(1)} %add.42), channel_id=1, source_target_pairs={{0,16},{8,24},{16,0},{24,8},{32,48},{40,56},{48,32},{56,40},{64,80... | collective-permute-start | bytes 24584 | tf_op jit(solution)/shard_map/ppermute | solution.py:523
  209.2 2.2 collective-permute-done.1
  211.4 5.2 %collective-permute-start.4 = (f32[16,128]{1,0:T(8,128)S(1)}, f32[16,128]{1,0:T(8,128)S(1)}, u32[]{:S(2)}, u32[]{:S(2)}) collective-permute-start(f32[16,128]{1,0:T(8,128)S(1)} %add.43), channel_id=1, source_target_pairs={{0,96},{8,104},{16,112},{24,120},{32,64},{40,72},{48,80},{56,88},{... | collective-permute-start | bytes 24584 | tf_op jit(solution)/shard_map/ppermute | solution.py:523
  216.6 1.9 collective-permute-start.3
  218.5 3.0 collective-permute-start.2
  221.5 18.4 %collective-permute-done.4 = f32[16,128]{1,0:T(8,128)S(1)} collective-permute-done((f32[16,128]{1,0:T(8,128)S(1)}, f32[16,128]{1,0:T(8,128)S(1)}, u32[]{:S(2)}, u32[]{:S(2)}) %collective-permute-start.4) | collective-permute-done | bytes 8224 | tf_op jit(solution)/shard_map/ppermute | solution.py:523
  239.9 8.5 %all-to-all-done.3 = f32[64,32,128]{2,1,0:T(8,128)S(1)} async-done(((f32[64,32,128]{2,1,0:T(8,128)}), f32[64,32,128]{2,1,0:T(8,128)S(1)}, u32[]{:S(2)}, u32[]{:S(2)}) %all-to-all-start.3) | async-done | bytes 1048608 | tf_op jit(solution)/shard_map/all_to_all | solution.py:425
  248.4 5.0 %lines2.1 = (f32[3072,128]{1,0:T(8,128)}, f32[4,256,128]{2,1,0:T(8,128)}) custom-call(s32[1]{0:T(128)S(6)} %copy.39.count_ref, s32[1,512]{1,0:T(1,128)S(1)} %get-tuple-element.27.near_any, s32[1,512]{1,0:T(1,128)S(1)} %get-tuple-element.28.term_any, f32[2048,128]{1,0:T(8,128)S(1)} %bitcast.26, f32[4,256,128]{2,1,0:T(8,128)S(1)} %copy-done, ...), custom_call_target="tpu_custom_call" | custom-call | tf_op jit(solution)/shard_map/lines2/pallas_call | solution.py:476
  253.4 6.2 %all-to-all-start.4 = ((f32[64,48,128]{2,1,0:T(8,128)}), f32[64,48,128]{2,1,0:T(8,128)S(1)}, u32[]{:S(2)}, u32[]{:S(2)}) async-start(f32[64,48,128]{2,1,0:T(8,128)} %bitcast.36), calls=%async_computation.4 | async-start | bytes 3145728 | tf_op jit(solution)/shard_map/all_to_all | solution.py:425
  259.6 2.1 collective-permute-start.8
  261.7 1.1 collective-permute-done.8
  262.8 2.7 collective-permute-start.9
  265.6 2.8 collective-permute-done.9
  268.4 3.3 collective-permute-start.10
  271.7 7.6 %collective-permute-start.7 = (f32[16,128]{1,0:T(8,128)S(1)}, f32[16,128]{1,0:T(8,128)S(1)}, u32[]{:S(2)}, u32[]{:S(2)}) collective-permute-start(f32[16,128]{1,0:T(8,128)S(1)} %add_add_fusion.1), channel_id=1, source_target_pairs={{0,384},{8,392},{16,400},{24,408},{32,416},{40,424},{48,432},{56,4... | collective-permute-start | bytes 24584 | tf_op jit(solution)/shard_map/ppermute | solution.py:523
  279.3 7.1 %collective-permute-start.6 = (f32[16,128]{1,0:T(8,128)S(1)}, f32[16,128]{1,0:T(8,128)S(1)}, u32[]{:S(2)}, u32[]{:S(2)}) collective-permute-start(f32[16,128]{1,0:T(8,128)S(1)} %add_add_fusion.1), channel_id=1, source_target_pairs={{0,256},{8,264},{16,272},{24,280},{32,288},{40,296},{48,304},{56,3... | collective-permute-start | bytes 24584 | tf_op jit(solution)/shard_map/ppermute | solution.py:523
  286.4 2.4 collective-permute-start.5
  288.8 39.4 %collective-permute-done.7 = f32[16,128]{1,0:T(8,128)S(1)} collective-permute-done((f32[16,128]{1,0:T(8,128)S(1)}, f32[16,128]{1,0:T(8,128)S(1)}, u32[]{:S(2)}, u32[]{:S(2)}) %collective-permute-start.7) | collective-permute-done | bytes 8224 | tf_op jit(solution)/shard_map/ppermute | solution.py:523
  328.2 9.1 %collective-permute-done.6 = f32[16,128]{1,0:T(8,128)S(1)} collective-permute-done((f32[16,128]{1,0:T(8,128)S(1)}, f32[16,128]{1,0:T(8,128)S(1)}, u32[]{:S(2)}, u32[]{:S(2)}) %collective-permute-start.6) | collective-permute-done | bytes 8224 | tf_op jit(solution)/shard_map/ppermute | solution.py:523
  337.3 1.4 dispatch2.1
  338.8 4.3 %all-to-all-start.5 = ((f32[4,16,128]{2,1,0:T(8,128)}), f32[4,16,128]{2,1,0:T(8,128)S(1)}, u32[]{:S(2)}, u32[]{:S(2)}) async-start(f32[4,16,128]{2,1,0:T(8,128)} %bitcast.19), calls=%async_computation.5 | async-start | bytes 65536 | tf_op jit(solution)/shard_map/all_to_all | solution.py:551
  343.0 1.9 collective-permute-start.11
  345.0 1.1 collective-permute-done.11
  346.1 2.4 all-to-all-done.5
  349.2 3.5 all-to-all-start.6
  352.7 2.7 collective-permute-start.12
  355.4 2.8 collective-permute-done.12
  358.2 3.3 collective-permute-start.13
  361.6 1.4 volt2.1
  362.9 2.4 collective-permute-done.13
  366.2 0.9 close.1
  (65 shorter events, 2.8 us)
Async XLA Ops:
  35.6 7.7 %copy-start.20 = (f32[256]{0:T(256)S(1)}, f32[256]{0:T(256)}, u32[]{:S(2)}) copy-start(f32[256]{0:T(256)} %param.20) | copy-start | bytes 3076
  35.6 7.7 %copy-start.21 = (f32[256]{0:T(256)S(1)}, f32[256]{0:T(256)}, u32[]{:S(2)}) copy-start(f32[256]{0:T(256)} %param.19) | copy-start | bytes 3076
  35.6 61.9 %copy-start = (f32[4,256,128]{2,1,0:T(8,128)S(1)}, f32[4,256,128]{2,1,0:T(8,128)}, u32[]{:S(2)}) copy-start(f32[4,256,128]{2,1,0:T(8,128)} %dual_ref.3) | copy-start | bytes 1572868
  38.6 58.8 %all-to-all-start.1 = ((f32[64,32,128]{2,1,0:T(8,128)}), f32[64,32,128]{2,1,0:T(8,128)S(1)}, u32[]{:S(2)}, u32[]{:S(2)}) async-start(f32[64,32,128]{2,1,0:T(8,128)} %first_send.1), calls=%async_computation.1 | async-start | bytes 2097152 | tf_op jit(solution)/shard_map/all_to_all | solution.py:425
  102.1 6.1 %copy-start.13 = (s32[256]{0:T(256)S(1)}, s32[256]{0:T(256)}, u32[]{:S(2)}) copy-start(s32[256]{0:T(256)} %param.24) | copy-start | bytes 3076
  102.1 6.1 %copy-start.14 = (f32[256]{0:T(256)S(1)}, f32[256]{0:T(256)}, u32[]{:S(2)}) copy-start(f32[256]{0:T(256)} %param.26) | copy-start | bytes 3076
  102.1 6.1 %copy-start.15 = (f32[256]{0:T(256)S(1)}, f32[256]{0:T(256)}, u32[]{:S(2)}) copy-start(f32[256]{0:T(256)} %param.25) | copy-start | bytes 3076
  102.1 6.1 %copy-start.16 = (f32[256]{0:T(256)S(1)}, f32[256]{0:T(256)}, u32[]{:S(2)}) copy-start(f32[256]{0:T(256)} %param.31) | copy-start | bytes 3076
  102.1 6.1 %copy-start.17 = (f32[256]{0:T(256)S(1)}, f32[256]{0:T(256)}, u32[]{:S(2)}) copy-start(f32[256]{0:T(256)} %param.32) | copy-start | bytes 3076
  102.1 6.1 %copy-start.18 = (f32[256]{0:T(256)S(1)}, f32[256]{0:T(256)}, u32[]{:S(2)}) copy-start(f32[256]{0:T(256)} %param.33) | copy-start | bytes 3076
  102.1 6.1 %copy-start.19 = (f32[256]{0:T(256)S(1)}, f32[256]{0:T(256)}, u32[]{:S(2)}) copy-start(f32[256]{0:T(256)} %param.30) | copy-start | bytes 3076
  102.1 82.9 %copy-start.1 = (f32[2,256,128]{2,1,0:T(8,128)S(1)}, f32[2,256,128]{2,1,0:T(8,128)}, u32[]{:S(2)}) copy-start(f32[2,256,128]{2,1,0:T(8,128)} %volt_ref.1) | copy-start | bytes 786436
  102.2 82.8 %all-to-all-start.2 = ((f32[64,48,128]{2,1,0:T(8,128)}), f32[64,48,128]{2,1,0:T(8,128)S(1)}, u32[]{:S(2)}, u32[]{:S(2)}) async-start(f32[64,48,128]{2,1,0:T(8,128)} %bitcast.37), calls=%async_computation.2 | async-start | bytes 3145728 | tf_op jit(solution)/shard_map/all_to_all | solution.py:425
  188.0 60.3 %all-to-all-start.3 = ((f32[64,32,128]{2,1,0:T(8,128)}), f32[64,32,128]{2,1,0:T(8,128)S(1)}, u32[]{:S(2)}, u32[]{:S(2)}) async-start(f32[64,32,128]{2,1,0:T(8,128)} %get-tuple-element.30), calls=%async_computation.3 | async-start | bytes 2097152 | tf_op jit(solution)/shard_map/all_to_all | solution.py:425
  193.9 0.9 copy-start.2
  194.8 0.9 copy-start.4
  195.7 0.9 copy-start.6
  197.3 0.7 copy-start.9
  198.0 0.7 copy-start.11
  198.7 5.6 %collective-permute-start = (f32[16,128]{1,0:T(8,128)S(1)}, f32[16,128]{1,0:T(8,128)S(1)}, u32[]{:S(2)}, u32[]{:S(2)}) collective-permute-start(f32[16,128]{1,0:T(8,128)S(1)} %get-tuple-element.31), channel_id=1, source_target_pairs={{0,8},{8,0},{16,24},{24,16},{32,40},{40,32},{48,56},{56,48},{64,72... | collective-permute-start | bytes 24584 | tf_op jit(solution)/shard_map/ppermute | solution.py:523
  204.3 7.1 %collective-permute-start.1 = (f32[16,128]{1,0:T(8,128)S(1)}, f32[16,128]{1,0:T(8,128)S(1)}, u32[]{:S(2)}, u32[]{:S(2)}) collective-permute-start(f32[16,128]{1,0:T(8,128)S(1)} %add.42), channel_id=1, source_target_pairs={{0,16},{8,24},{16,0},{24,8},{32,48},{40,56},{48,32},{56,40},{64,80... | collective-permute-start | bytes 24584 | tf_op jit(solution)/shard_map/ppermute | solution.py:523
  211.4 28.5 %collective-permute-start.4 = (f32[16,128]{1,0:T(8,128)S(1)}, f32[16,128]{1,0:T(8,128)S(1)}, u32[]{:S(2)}, u32[]{:S(2)}) collective-permute-start(f32[16,128]{1,0:T(8,128)S(1)} %add.43), channel_id=1, source_target_pairs={{0,96},{8,104},{16,112},{24,120},{32,64},{40,72},{48,80},{56,88},{... | collective-permute-start | bytes 24584 | tf_op jit(solution)/shard_map/ppermute | solution.py:523
  216.6 23.3 %collective-permute-start.3 = (f32[16,128]{1,0:T(8,128)S(1)}, f32[16,128]{1,0:T(8,128)S(1)}, u32[]{:S(2)}, u32[]{:S(2)}) collective-permute-start(f32[16,128]{1,0:T(8,128)S(1)} %add.43), channel_id=1, source_target_pairs={{0,64},{8,72},{16,80},{24,88},{32,96},{40,104},{48,112},{56,120},{... | collective-permute-start | bytes 24584 | tf_op jit(solution)/shard_map/ppermute | solution.py:523
  218.5 21.3 %collective-permute-start.2 = (f32[16,128]{1,0:T(8,128)S(1)}, f32[16,128]{1,0:T(8,128)S(1)}, u32[]{:S(2)}, u32[]{:S(2)}) collective-permute-start(f32[16,128]{1,0:T(8,128)S(1)} %add.43), channel_id=1, source_target_pairs={{0,32},{8,40},{16,48},{24,56},{32,0},{40,8},{48,16},{56,24},{64,96... | collective-permute-start | bytes 24584 | tf_op jit(solution)/shard_map/ppermute | solution.py:523
  253.4 83.9 %copy-start.3 = (f32[256,128]{1,0:T(8,128)S(1)}, f32[256,128]{1,0:T(8,128)}, u32[]{:S(2)}) copy-start(f32[256,128]{1,0:T(8,128)} %load_ref.3) | copy-start | bytes 393220
  253.4 83.9 %copy-start.5 = (f32[256,128]{1,0:T(8,128)S(1)}, f32[256,128]{1,0:T(8,128)}, u32[]{:S(2)}) copy-start(f32[256,128]{1,0:T(8,128)} %price_ref.3) | copy-start | bytes 393220
  253.4 83.9 %copy-start.7 = (f32[256,128]{1,0:T(8,128)S(1)}, f32[256,128]{1,0:T(8,128)}, u32[]{:S(2)}) copy-start(f32[256,128]{1,0:T(8,128)} %nadual_ref.3) | copy-start | bytes 393220
  253.4 83.9 %copy-start.10 = (f32[256,128]{1,0:T(8,128)S(1)}, f32[256,128]{1,0:T(8,128)}, u32[]{:S(2)}) copy-start(f32[256,128]{1,0:T(8,128)} %copy-done.9) | copy-start | bytes 393220
  253.4 83.9 %copy-start.12 = (f32[256,128]{1,0:T(8,128)S(1)}, f32[256,128]{1,0:T(8,128)}, u32[]{:S(2)}) copy-start(f32[256,128]{1,0:T(8,128)} %copy-done.11) | copy-start | bytes 393220
  253.4 83.9 %all-to-all-start.4 = ((f32[64,48,128]{2,1,0:T(8,128)}), f32[64,48,128]{2,1,0:T(8,128)S(1)}, u32[]{:S(2)}, u32[]{:S(2)}) async-start(f32[64,48,128]{2,1,0:T(8,128)} %bitcast.36), calls=%async_computation.4 | async-start | bytes 3145728 | tf_op jit(solution)/shard_map/all_to_all | solution.py:425
  259.6 101.9 %copy-start.8 = (f32[2,256,128]{2,1,0:T(8,128)S(1)}, f32[2,256,128]{2,1,0:T(8,128)}, u32[]{:S(2)}) copy-start(f32[2,256,128]{2,1,0:T(8,128)} %get-tuple-element.35.volt_ref) | copy-start | bytes 786436
  259.6 3.2 collective-permute-start.8
  262.8 5.5 %collective-permute-start.9 = (f32[8,256]{1,0:T(8,128)S(1)}, f32[8,256]{1,0:T(8,128)S(1)}, u32[]{:S(2)}, u32[]{:S(2)}) collective-permute-start(f32[8,256]{1,0:T(8,128)S(1)} %add.50), channel_id=1, source_target_pairs={{0,2},{1,3},{2,0},{3,1},{4,6},{5,7},{6,4},{7,5},{8,10},{9,11},{10,... | collective-permute-start | bytes 24584 | tf_op jit(solution)/shard_map/ppermute | solution.py:523
  268.4 20.4 %collective-permute-start.10 = (f32[8,256]{1,0:T(8,128)S(1)}, f32[8,256]{1,0:T(8,128)S(1)}, u32[]{:S(2)}, u32[]{:S(2)}) collective-permute-start(f32[8,256]{1,0:T(8,128)S(1)} %add.51), channel_id=1, source_target_pairs={{0,4},{1,5},{2,6},{3,7},{4,0},{5,1},{6,2},{7,3},{8,12},{9,13},{10,... | collective-permute-start | bytes 24584 | tf_op jit(solution)/shard_map/ppermute | solution.py:523
  271.7 56.5 %collective-permute-start.7 = (f32[16,128]{1,0:T(8,128)S(1)}, f32[16,128]{1,0:T(8,128)S(1)}, u32[]{:S(2)}, u32[]{:S(2)}) collective-permute-start(f32[16,128]{1,0:T(8,128)S(1)} %add_add_fusion.1), channel_id=1, source_target_pairs={{0,384},{8,392},{16,400},{24,408},{32,416},{40,424},{48,432},{56,4... | collective-permute-start | bytes 24584 | tf_op jit(solution)/shard_map/ppermute | solution.py:523
  279.3 58.0 %collective-permute-start.6 = (f32[16,128]{1,0:T(8,128)S(1)}, f32[16,128]{1,0:T(8,128)S(1)}, u32[]{:S(2)}, u32[]{:S(2)}) collective-permute-start(f32[16,128]{1,0:T(8,128)S(1)} %add_add_fusion.1), channel_id=1, source_target_pairs={{0,256},{8,264},{16,272},{24,280},{32,288},{40,296},{48,304},{56,3... | collective-permute-start | bytes 24584 | tf_op jit(solution)/shard_map/ppermute | solution.py:523
  286.4 50.9 %collective-permute-start.5 = (f32[16,128]{1,0:T(8,128)S(1)}, f32[16,128]{1,0:T(8,128)S(1)}, u32[]{:S(2)}, u32[]{:S(2)}) collective-permute-start(f32[16,128]{1,0:T(8,128)S(1)} %add_add_fusion.1), channel_id=1, source_target_pairs={{0,128},{8,136},{16,144},{24,152},{32,160},{40,168},{48,176},{56,1... | collective-permute-start | bytes 24584 | tf_op jit(solution)/shard_map/ppermute | solution.py:523
  338.8 9.7 %all-to-all-start.5 = ((f32[4,16,128]{2,1,0:T(8,128)}), f32[4,16,128]{2,1,0:T(8,128)S(1)}, u32[]{:S(2)}, u32[]{:S(2)}) async-start(f32[4,16,128]{2,1,0:T(8,128)} %bitcast.19), calls=%async_computation.5 | async-start | bytes 65536 | tf_op jit(solution)/shard_map/all_to_all | solution.py:551
  343.0 3.1 collective-permute-start.11
  349.2 17.1 %all-to-all-start.6 = ((f32[16,16,128]{2,1,0:T(8,128)}), f32[16,16,128]{2,1,0:T(8,128)S(1)}, u32[]{:S(2)}, u32[]{:S(2)}) async-start(f32[16,16,128]{2,1,0:T(8,128)} %broadcast_in_dim.2), calls=%async_computation.6 | async-start | bytes 262144 | tf_op jit(solution)/shard_map/all_to_all | solution.py:556
  352.7 5.5 %collective-permute-start.12 = (f32[8,256]{1,0:T(8,128)S(1)}, f32[8,256]{1,0:T(8,128)S(1)}, u32[]{:S(2)}, u32[]{:S(2)}) collective-permute-start(f32[8,256]{1,0:T(8,128)S(1)} %add.53), channel_id=1, source_target_pairs={{0,2},{1,3},{2,0},{3,1},{4,6},{5,7},{6,4},{7,5},{8,10},{9,11},{10,... | collective-permute-start | bytes 24584 | tf_op jit(solution)/shard_map/ppermute | solution.py:523
  358.2 7.0 %collective-permute-start.13 = (f32[8,256]{1,0:T(8,128)S(1)}, f32[8,256]{1,0:T(8,128)S(1)}, u32[]{:S(2)}, u32[]{:S(2)}) collective-permute-start(f32[8,256]{1,0:T(8,128)S(1)} %add.54), channel_id=1, source_target_pairs={{0,4},{1,5},{2,6},{3,7},{4,0},{5,1},{6,2},{7,3},{8,12},{9,13},{10,... | collective-permute-start | bytes 24584 | tf_op jit(solution)/shard_map/ppermute | solution.py:523

commit v9 on v8

--- a/solution.py
+++ b/solution.py
@@ -540,8 +540,8 @@
         if step & (step - 1) == 0:
             part = near_sum(part, "grid", ngrid, step, 2)
     part = near_sum(part, "grid", ngrid, NEAR, NEAR)
-    arrived, part = lax.optimization_barrier((arrived, part))
     totals = doubling_sum(total, "scen", nscen)
+    arrived, part, totals = lax.optimization_barrier((arrived, part, totals))
     regional = near_sum(part, "grid", ngrid, NEAR * NEAR, ngrid // (NEAR * NEAR))
     out, dual = line_call(True, arrived, state)
     received = exchange(out)

time: 368 us -> 368 us (level)
  transfers between devices with their start and end apart: 20 -> 20, of which waited for: 15 -> 11; matrix products, arithmetic and copies ran while one was open for 0% -> 0% of each run, Pallas kernels for 1% -> 1%
where the time goes in v9:
time: 368 us; the launch traced here: 367 us
  waiting for transfers between devices  224 us (61%)
  starting transfers between devices  81.4 us (22%)
  blocking collectives  33.2 us (9%)
  Pallas kernels  21.2 us (6%)
  local copies, waits for them, and re-layouts  5.19 us (1%)
    all_to_all x4, waiting for transfers between devices, exchange(): return lax.all_to_all(x, 'grid', split_axis=0, concat_axis=0, tiled=True)  139 us
    ppermute x14, waiting for transfers between devices, near_sum(): lax.ppermute(x, axis, [(i, i ^ k * step) for i in range(size)])  82 us
    ppermute x14, starting transfers between devices, near_sum(): lax.ppermute(x, axis, [(i, i ^ k * step) for i in range(size)])  50.9 us
    all_to_all x1, blocking collectives, exchange(): return lax.all_to_all(x, 'grid', split_axis=0, concat_axis=0, tiled=True)  33.2 us
    all_to_all x4, starting transfers between devices, exchange(): return lax.all_to_all(x, 'grid', split_axis=0, concat_axis=0, tiled=True)  22.7 us
    pallas_call x2, Pallas kernels, line_call(): pl.pallas_call(functools.partial(line_kernel, second), out_shape=outs, in...  9.6 us
  transfers between devices with their start and end apart: 20, of which 11 were waited for; matrix products, arithmetic and copies ran while one was open for 0% of the time, Pallas kernels for 1%

profile of v9, /device:TPU:6, one launch (start us, length us, event | category | flops | bytes accessed | tf_op | source)
XLA Modules:
  0.0 367.2 jit_solution(4752558017124416098)
XLA Ops:
  1.3 1.1 plan.1
  2.4 33.2 %all_to_all.48 = s32[64,1,128]{2,1,0:T(1,128)S(1)} all-to-all(s32[64,1,128]{2,1,0:T(1,128)S(1)} %bitcast.33), channel_id=1, replica_groups=mesh['grid'=64,'scen'=8] {'grid'}, dimensions={0} | all-to-all | bytes 65536 | tf_op jit(solution)/shard_map/all_to_all | solution.py:425
  35.6 3.0 first_send.1
  38.6 4.7 %all-to-all-start.1 = ((f32[64,32,128]{2,1,0:T(8,128)}), f32[64,32,128]{2,1,0:T(8,128)S(1)}, u32[]{:S(2)}, u32[]{:S(2)}) async-start(f32[64,32,128]{2,1,0:T(8,128)} %first_send.1), calls=%async_computation.1 | async-start | bytes 2097152 | tf_op jit(solution)/shard_map/all_to_all | solution.py:425
  43.5 54.0 %all-to-all-done.1 = f32[64,32,128]{2,1,0:T(8,128)S(1)} async-done(((f32[64,32,128]{2,1,0:T(8,128)}), f32[64,32,128]{2,1,0:T(8,128)S(1)}, u32[]{:S(2)}, u32[]{:S(2)}) %all-to-all-start.1) | async-done | bytes 1048608 | tf_op jit(solution)/shard_map/all_to_all | solution.py:425
  97.5 4.6 %lines1.1 = (f32[3072,128]{1,0:T(8,128)}, f32[4,256,128]{2,1,0:T(8,128)}) custom-call(s32[1]{0:T(128)S(6)} %copy.39.count_ref, s32[1,512]{1,0:T(1,128)S(1)} %get-tuple-element.28.near_any, s32[1,512]{1,0:T(1,128)S(1)} %get-tuple-element.29.term_any, f32[2048,128]{1,0:T(8,128)S(1)} %bitcast.27, f32[4,256,128]{2,1,0:T(8,128)S(1)} %copy-done, ...), custom_call_target="tpu_custom_call" | custom-call | tf_op jit(solution)/shard_map/lines1/pallas_call | solution.py:476
  102.2 6.0 %all-to-all-start.2 = ((f32[64,48,128]{2,1,0:T(8,128)}), f32[64,48,128]{2,1,0:T(8,128)S(1)}, u32[]{:S(2)}, u32[]{:S(2)}) async-start(f32[64,48,128]{2,1,0:T(8,128)} %bitcast.37), calls=%async_computation.2 | async-start | bytes 3145728 | tf_op jit(solution)/shard_map/all_to_all | solution.py:425
  108.5 76.5 %all-to-all-done.2.recv_ref = f32[64,48,128]{2,1,0:T(8,128)S(1)} async-done(((f32[64,48,128]{2,1,0:T(8,128)}), f32[64,48,128]{2,1,0:T(8,128)S(1)}, u32[]{:S(2)}, u32[]{:S(2)}) %all-to-all-start.2) | async-done | bytes 1572896 | tf_op jit(solution)/shard_map/all_to_all | solution.py:425
  185.0 3.0 volt1.1
  188.0 5.8 %all-to-all-start.3 = ((f32[64,32,128]{2,1,0:T(8,128)}), f32[64,32,128]{2,1,0:T(8,128)S(1)}, u32[]{:S(2)}, u32[]{:S(2)}) async-start(f32[64,32,128]{2,1,0:T(8,128)} %get-tuple-element.31), calls=%async_computation.3 | async-start | bytes 2097152 | tf_op jit(solution)/shard_map/all_to_all | solution.py:425
  193.9 0.9 copy-done.2
  194.8 0.9 copy-done.4
  195.7 0.9 copy-done.6
  196.6 0.7 dispatch1.1
  197.3 0.7 copy-done.9
  198.0 0.7 copy-done.11
  198.6 1.9 collective-permute-start.5
  200.6 3.5 collective-permute-start
  204.1 2.7 collective-permute-start.6
  206.8 4.6 %collective-permute-start.1 = (f32[16,128]{1,0:T(8,128)S(1)}, f32[16,128]{1,0:T(8,128)S(1)}, u32[]{:S(2)}, u32[]{:S(2)}) collective-permute-start(f32[16,128]{1,0:T(8,128)S(1)} %add.42), channel_id=1, source_target_pairs={{0,16},{8,24},{16,0},{24,8},{32,48},{40,56},{48,32},{56,40},{64,80... | collective-permute-start | bytes 24584 | tf_op jit(solution)/shard_map/ppermute | solution.py:523
  211.5 3.0 collective-permute-start.7
  214.5 5.2 %collective-permute-start.4 = (f32[16,128]{1,0:T(8,128)S(1)}, f32[16,128]{1,0:T(8,128)S(1)}, u32[]{:S(2)}, u32[]{:S(2)}) collective-permute-start(f32[16,128]{1,0:T(8,128)S(1)} %add.43), channel_id=1, source_target_pairs={{0,96},{8,104},{16,112},{24,120},{32,64},{40,72},{48,80},{56,88},{... | collective-permute-start | bytes 24584 | tf_op jit(solution)/shard_map/ppermute | solution.py:523
  219.7 1.9 collective-permute-start.3
  221.6 3.0 collective-permute-start.2
  224.7 15.2 %collective-permute-done.4 = f32[16,128]{1,0:T(8,128)S(1)} collective-permute-done((f32[16,128]{1,0:T(8,128)S(1)}, f32[16,128]{1,0:T(8,128)S(1)}, u32[]{:S(2)}, u32[]{:S(2)}) %collective-permute-start.4) | collective-permute-done | bytes 8224 | tf_op jit(solution)/shard_map/ppermute | solution.py:523
  239.9 8.5 %all-to-all-done.3 = f32[64,32,128]{2,1,0:T(8,128)S(1)} async-done(((f32[64,32,128]{2,1,0:T(8,128)}), f32[64,32,128]{2,1,0:T(8,128)S(1)}, u32[]{:S(2)}, u32[]{:S(2)}) %all-to-all-start.3) | async-done | bytes 1048608 | tf_op jit(solution)/shard_map/all_to_all | solution.py:425
  248.4 5.0 %lines2.1 = (f32[3072,128]{1,0:T(8,128)}, f32[4,256,128]{2,1,0:T(8,128)}) custom-call(s32[1]{0:T(128)S(6)} %copy.39.count_ref, s32[1,512]{1,0:T(1,128)S(1)} %get-tuple-element.28.near_any, s32[1,512]{1,0:T(1,128)S(1)} %get-tuple-element.29.term_any, f32[2048,128]{1,0:T(8,128)S(1)} %bitcast.26, f32[4,256,128]{2,1,0:T(8,128)S(1)} %copy-done, ...), custom_call_target="tpu_custom_call" | custom-call | tf_op jit(solution)/shard_map/lines2/pallas_call | solution.py:476
  253.4 6.2 %all-to-all-start.4 = ((f32[64,48,128]{2,1,0:T(8,128)}), f32[64,48,128]{2,1,0:T(8,128)S(1)}, u32[]{:S(2)}, u32[]{:S(2)}) async-start(f32[64,48,128]{2,1,0:T(8,128)} %bitcast.36), calls=%async_computation.4 | async-start | bytes 3145728 | tf_op jit(solution)/shard_map/all_to_all | solution.py:425
  259.6 7.7 %collective-permute-start.10 = (f32[16,128]{1,0:T(8,128)S(1)}, f32[16,128]{1,0:T(8,128)S(1)}, u32[]{:S(2)}, u32[]{:S(2)}) collective-permute-start(f32[16,128]{1,0:T(8,128)S(1)} %add_add_fusion.1), channel_id=1, source_target_pairs={{0,384},{8,392},{16,400},{24,408},{32,416},{40,424},{48,432},{56,4... | collective-permute-start | bytes 24584 | tf_op jit(solution)/shard_map/ppermute | solution.py:523
  267.4 7.1 %collective-permute-start.9 = (f32[16,128]{1,0:T(8,128)S(1)}, f32[16,128]{1,0:T(8,128)S(1)}, u32[]{:S(2)}, u32[]{:S(2)}) collective-permute-start(f32[16,128]{1,0:T(8,128)S(1)} %add_add_fusion.1), channel_id=1, source_target_pairs={{0,256},{8,264},{16,272},{24,280},{32,288},{40,296},{48,304},{56,3... | collective-permute-start | bytes 24584 | tf_op jit(solution)/shard_map/ppermute | solution.py:523
  274.5 2.4 collective-permute-start.8
  276.8 51.3 %collective-permute-done.10 = f32[16,128]{1,0:T(8,128)S(1)} collective-permute-done((f32[16,128]{1,0:T(8,128)S(1)}, f32[16,128]{1,0:T(8,128)S(1)}, u32[]{:S(2)}, u32[]{:S(2)}) %collective-permute-start.10) | collective-permute-done | bytes 8224 | tf_op jit(solution)/shard_map/ppermute | solution.py:523
  328.2 9.1 %collective-permute-done.9 = f32[16,128]{1,0:T(8,128)S(1)} collective-permute-done((f32[16,128]{1,0:T(8,128)S(1)}, f32[16,128]{1,0:T(8,128)S(1)}, u32[]{:S(2)}, u32[]{:S(2)}) %collective-permute-start.9) | collective-permute-done | bytes 8224 | tf_op jit(solution)/shard_map/ppermute | solution.py:523
  337.3 1.5 dispatch2.1
  338.8 4.2 %all-to-all-start.5 = ((f32[4,16,128]{2,1,0:T(8,128)}), f32[4,16,128]{2,1,0:T(8,128)S(1)}, u32[]{:S(2)}, u32[]{:S(2)}) async-start(f32[4,16,128]{2,1,0:T(8,128)} %bitcast.19), calls=%async_computation.5 | async-start | bytes 65536 | tf_op jit(solution)/shard_map/all_to_all | solution.py:551
  343.1 1.9 collective-permute-start.11
  345.0 1.1 collective-permute-done.11
  346.1 2.4 all-to-all-done.5
  348.5 0.7 broadcast_in_dim.2
  349.2 3.5 all-to-all-start.6
  352.7 2.7 collective-permute-start.12
  355.4 2.8 collective-permute-done.12
  358.2 3.3 collective-permute-start.13
  361.6 1.3 volt2.1
  362.9 2.4 collective-permute-done.13
  365.3 0.6 fusion
  365.9 0.4 all-to-all-done.6
  366.3 0.9 close.1
  (65 shorter events, 0.6 us)
Async XLA Ops:
  35.6 7.7 %copy-start.20 = (f32[256]{0:T(256)S(1)}, f32[256]{0:T(256)}, u32[]{:S(2)}) copy-start(f32[256]{0:T(256)} %param.20) | copy-start | bytes 3076
  35.6 7.7 %copy-start.21 = (f32[256]{0:T(256)S(1)}, f32[256]{0:T(256)}, u32[]{:S(2)}) copy-start(f32[256]{0:T(256)} %param.19) | copy-start | bytes 3076
  35.6 61.9 %copy-start = (f32[4,256,128]{2,1,0:T(8,128)S(1)}, f32[4,256,128]{2,1,0:T(8,128)}, u32[]{:S(2)}) copy-start(f32[4,256,128]{2,1,0:T(8,128)} %dual_ref.3) | copy-start | bytes 1572868
  38.6 58.8 %all-to-all-start.1 = ((f32[64,32,128]{2,1,0:T(8,128)}), f32[64,32,128]{2,1,0:T(8,128)S(1)}, u32[]{:S(2)}, u32[]{:S(2)}) async-start(f32[64,32,128]{2,1,0:T(8,128)} %first_send.1), calls=%async_computation.1 | async-start | bytes 2097152 | tf_op jit(solution)/shard_map/all_to_all | solution.py:425
  102.1 6.1 %copy-start.13 = (s32[256]{0:T(256)S(1)}, s32[256]{0:T(256)}, u32[]{:S(2)}) copy-start(s32[256]{0:T(256)} %param.24) | copy-start | bytes 3076
  102.1 6.1 %copy-start.14 = (f32[256]{0:T(256)S(1)}, f32[256]{0:T(256)}, u32[]{:S(2)}) copy-start(f32[256]{0:T(256)} %param.26) | copy-start | bytes 3076
  102.1 6.1 %copy-start.15 = (f32[256]{0:T(256)S(1)}, f32[256]{0:T(256)}, u32[]{:S(2)}) copy-start(f32[256]{0:T(256)} %param.25) | copy-start | bytes 3076
  102.1 6.1 %copy-start.16 = (f32[256]{0:T(256)S(1)}, f32[256]{0:T(256)}, u32[]{:S(2)}) copy-start(f32[256]{0:T(256)} %param.31) | copy-start | bytes 3076
  102.1 6.1 %copy-start.17 = (f32[256]{0:T(256)S(1)}, f32[256]{0:T(256)}, u32[]{:S(2)}) copy-start(f32[256]{0:T(256)} %param.32) | copy-start | bytes 3076
  102.1 6.1 %copy-start.18 = (f32[256]{0:T(256)S(1)}, f32[256]{0:T(256)}, u32[]{:S(2)}) copy-start(f32[256]{0:T(256)} %param.33) | copy-start | bytes 3076
  102.1 6.1 %copy-start.19 = (f32[256]{0:T(256)S(1)}, f32[256]{0:T(256)}, u32[]{:S(2)}) copy-start(f32[256]{0:T(256)} %param.30) | copy-start | bytes 3076
  102.1 82.9 %copy-start.1 = (f32[2,256,128]{2,1,0:T(8,128)S(1)}, f32[2,256,128]{2,1,0:T(8,128)}, u32[]{:S(2)}) copy-start(f32[2,256,128]{2,1,0:T(8,128)} %volt_ref.1) | copy-start | bytes 786436
  102.2 82.8 %all-to-all-start.2 = ((f32[64,48,128]{2,1,0:T(8,128)}), f32[64,48,128]{2,1,0:T(8,128)S(1)}, u32[]{:S(2)}, u32[]{:S(2)}) async-start(f32[64,48,128]{2,1,0:T(8,128)} %bitcast.37), calls=%async_computation.2 | async-start | bytes 3145728 | tf_op jit(solution)/shard_map/all_to_all | solution.py:425
  188.0 60.3 %all-to-all-start.3 = ((f32[64,32,128]{2,1,0:T(8,128)}), f32[64,32,128]{2,1,0:T(8,128)S(1)}, u32[]{:S(2)}, u32[]{:S(2)}) async-start(f32[64,32,128]{2,1,0:T(8,128)} %get-tuple-element.31), calls=%async_computation.3 | async-start | bytes 2097152 | tf_op jit(solution)/shard_map/all_to_all | solution.py:425
  193.9 0.9 copy-start.2
  194.8 0.9 copy-start.4
  195.7 0.9 copy-start.6
  197.3 0.7 copy-start.9
  198.0 0.7 copy-start.11
  198.6 5.4 %collective-permute-start.5 = (f32[8,256]{1,0:T(8,128)S(1)}, f32[8,256]{1,0:T(8,128)S(1)}, u32[]{:S(2)}, u32[]{:S(2)}) collective-permute-start(f32[8,256]{1,0:T(8,128)S(1)} %get-tuple-element.33), channel_id=1, source_target_pairs={{0,1},{1,0},{2,3},{3,2},{4,5},{5,4},{6,7},{7,6},{8,9},{9,8},{10,11... | collective-permute-start | bytes 24584 | tf_op jit(solution)/shard_map/ppermute | solution.py:523
  200.6 6.3 %collective-permute-start = (f32[16,128]{1,0:T(8,128)S(1)}, f32[16,128]{1,0:T(8,128)S(1)}, u32[]{:S(2)}, u32[]{:S(2)}) collective-permute-start(f32[16,128]{1,0:T(8,128)S(1)} %get-tuple-element.32), channel_id=1, source_target_pairs={{0,8},{8,0},{16,24},{24,16},{32,40},{40,32},{48,56},{56,48},{64,72... | collective-permute-start | bytes 24584 | tf_op jit(solution)/shard_map/ppermute | solution.py:523
  204.1 7.4 %collective-permute-start.6 = (f32[8,256]{1,0:T(8,128)S(1)}, f32[8,256]{1,0:T(8,128)S(1)}, u32[]{:S(2)}, u32[]{:S(2)}) collective-permute-start(f32[8,256]{1,0:T(8,128)S(1)} %add.47), channel_id=1, source_target_pairs={{0,2},{1,3},{2,0},{3,1},{4,6},{5,7},{6,4},{7,5},{8,10},{9,11},{10,... | collective-permute-start | bytes 24584 | tf_op jit(solution)/shard_map/ppermute | solution.py:523
  206.8 7.6 %collective-permute-start.1 = (f32[16,128]{1,0:T(8,128)S(1)}, f32[16,128]{1,0:T(8,128)S(1)}, u32[]{:S(2)}, u32[]{:S(2)}) collective-permute-start(f32[16,128]{1,0:T(8,128)S(1)} %add.42), channel_id=1, source_target_pairs={{0,16},{8,24},{16,0},{24,8},{32,48},{40,56},{48,32},{56,40},{64,80... | collective-permute-start | bytes 24584 | tf_op jit(solution)/shard_map/ppermute | solution.py:523
  211.5 13.2 %collective-permute-start.7 = (f32[8,256]{1,0:T(8,128)S(1)}, f32[8,256]{1,0:T(8,128)S(1)}, u32[]{:S(2)}, u32[]{:S(2)}) collective-permute-start(f32[8,256]{1,0:T(8,128)S(1)} %add.48), channel_id=1, source_target_pairs={{0,4},{1,5},{2,6},{3,7},{4,0},{5,1},{6,2},{7,3},{8,12},{9,13},{10,... | collective-permute-start | bytes 24584 | tf_op jit(solution)/shard_map/ppermute | solution.py:523
  214.5 25.4 %collective-permute-start.4 = (f32[16,128]{1,0:T(8,128)S(1)}, f32[16,128]{1,0:T(8,128)S(1)}, u32[]{:S(2)}, u32[]{:S(2)}) collective-permute-start(f32[16,128]{1,0:T(8,128)S(1)} %add.43), channel_id=1, source_target_pairs={{0,96},{8,104},{16,112},{24,120},{32,64},{40,72},{48,80},{56,88},{... | collective-permute-start | bytes 24584 | tf_op jit(solution)/shard_map/ppermute | solution.py:523
  219.7 20.2 %collective-permute-start.3 = (f32[16,128]{1,0:T(8,128)S(1)}, f32[16,128]{1,0:T(8,128)S(1)}, u32[]{:S(2)}, u32[]{:S(2)}) collective-permute-start(f32[16,128]{1,0:T(8,128)S(1)} %add.43), channel_id=1, source_target_pairs={{0,64},{8,72},{16,80},{24,88},{32,96},{40,104},{48,112},{56,120},{... | collective-permute-start | bytes 24584 | tf_op jit(solution)/shard_map/ppermute | solution.py:523
  221.6 18.3 %collective-permute-start.2 = (f32[16,128]{1,0:T(8,128)S(1)}, f32[16,128]{1,0:T(8,128)S(1)}, u32[]{:S(2)}, u32[]{:S(2)}) collective-permute-start(f32[16,128]{1,0:T(8,128)S(1)} %add.43), channel_id=1, source_target_pairs={{0,32},{8,40},{16,48},{24,56},{32,0},{40,8},{48,16},{56,24},{64,96... | collective-permute-start | bytes 24584 | tf_op jit(solution)/shard_map/ppermute | solution.py:523
  253.4 83.9 %copy-start.3 = (f32[256,128]{1,0:T(8,128)S(1)}, f32[256,128]{1,0:T(8,128)}, u32[]{:S(2)}) copy-start(f32[256,128]{1,0:T(8,128)} %load_ref.3) | copy-start | bytes 393220
  253.4 83.9 %copy-start.5 = (f32[256,128]{1,0:T(8,128)S(1)}, f32[256,128]{1,0:T(8,128)}, u32[]{:S(2)}) copy-start(f32[256,128]{1,0:T(8,128)} %price_ref.3) | copy-start | bytes 393220
  253.4 83.9 %copy-start.7 = (f32[256,128]{1,0:T(8,128)S(1)}, f32[256,128]{1,0:T(8,128)}, u32[]{:S(2)}) copy-start(f32[256,128]{1,0:T(8,128)} %nadual_ref.3) | copy-start | bytes 393220
  253.4 83.9 %copy-start.10 = (f32[256,128]{1,0:T(8,128)S(1)}, f32[256,128]{1,0:T(8,128)}, u32[]{:S(2)}) copy-start(f32[256,128]{1,0:T(8,128)} %copy-done.9) | copy-start | bytes 393220
  253.4 83.9 %copy-start.12 = (f32[256,128]{1,0:T(8,128)S(1)}, f32[256,128]{1,0:T(8,128)}, u32[]{:S(2)}) copy-start(f32[256,128]{1,0:T(8,128)} %copy-done.11) | copy-start | bytes 393220
  253.4 83.9 %all-to-all-start.4 = ((f32[64,48,128]{2,1,0:T(8,128)}), f32[64,48,128]{2,1,0:T(8,128)S(1)}, u32[]{:S(2)}, u32[]{:S(2)}) async-start(f32[64,48,128]{2,1,0:T(8,128)} %bitcast.36), calls=%async_computation.4 | async-start | bytes 3145728 | tf_op jit(solution)/shard_map/all_to_all | solution.py:425
  259.6 101.9 %copy-start.8 = (f32[2,256,128]{2,1,0:T(8,128)S(1)}, f32[2,256,128]{2,1,0:T(8,128)}, u32[]{:S(2)}) copy-start(f32[2,256,128]{2,1,0:T(8,128)} %get-tuple-element.37.volt_ref) | copy-start | bytes 786436
  259.6 68.5 %collective-permute-start.10 = (f32[16,128]{1,0:T(8,128)S(1)}, f32[16,128]{1,0:T(8,128)S(1)}, u32[]{:S(2)}, u32[]{:S(2)}) collective-permute-start(f32[16,128]{1,0:T(8,128)S(1)} %add_add_fusion.1), channel_id=1, source_target_pairs={{0,384},{8,392},{16,400},{24,408},{32,416},{40,424},{48,432},{56,4... | collective-permute-start | bytes 24584 | tf_op jit(solution)/shard_map/ppermute | solution.py:523
  267.4 69.9 %collective-permute-start.9 = (f32[16,128]{1,0:T(8,128)S(1)}, f32[16,128]{1,0:T(8,128)S(1)}, u32[]{:S(2)}, u32[]{:S(2)}) collective-permute-start(f32[16,128]{1,0:T(8,128)S(1)} %add_add_fusion.1), channel_id=1, source_target_pairs={{0,256},{8,264},{16,272},{24,280},{32,288},{40,296},{48,304},{56,3... | collective-permute-start | bytes 24584 | tf_op jit(solution)/shard_map/ppermute | solution.py:523
  274.5 62.8 %collective-permute-start.8 = (f32[16,128]{1,0:T(8,128)S(1)}, f32[16,128]{1,0:T(8,128)S(1)}, u32[]{:S(2)}, u32[]{:S(2)}) collective-permute-start(f32[16,128]{1,0:T(8,128)S(1)} %add_add_fusion.1), channel_id=1, source_target_pairs={{0,128},{8,136},{16,144},{24,152},{32,160},{40,168},{48,176},{56,1... | collective-permute-start | bytes 24584 | tf_op jit(solution)/shard_map/ppermute | solution.py:523
  338.8 9.7 %all-to-all-start.5 = ((f32[4,16,128]{2,1,0:T(8,128)}), f32[4,16,128]{2,1,0:T(8,128)S(1)}, u32[]{:S(2)}, u32[]{:S(2)}) async-start(f32[4,16,128]{2,1,0:T(8,128)} %bitcast.19), calls=%async_computation.5 | async-start | bytes 65536 | tf_op jit(solution)/shard_map/all_to_all | solution.py:551
  343.1 3.1 collective-permute-start.11
  349.2 17.1 %all-to-all-start.6 = ((f32[16,16,128]{2,1,0:T(8,128)}), f32[16,16,128]{2,1,0:T(8,128)S(1)}, u32[]{:S(2)}, u32[]{:S(2)}) async-start(f32[16,16,128]{2,1,0:T(8,128)} %broadcast_in_dim.2), calls=%async_computation.6 | async-start | bytes 262144 | tf_op jit(solution)/shard_map/all_to_all | solution.py:556
  352.7 5.5 %collective-permute-start.12 = (f32[8,256]{1,0:T(8,128)S(1)}, f32[8,256]{1,0:T(8,128)S(1)}, u32[]{:S(2)}, u32[]{:S(2)}) collective-permute-start(f32[8,256]{1,0:T(8,128)S(1)} %add.53), channel_id=1, source_target_pairs={{0,2},{1,3},{2,0},{3,1},{4,6},{5,7},{6,4},{7,5},{8,10},{9,11},{10,... | collective-permute-start | bytes 24584 | tf_op jit(solution)/shard_map/ppermute | solution.py:523
  358.2 7.0 %collective-permute-start.13 = (f32[8,256]{1,0:T(8,128)S(1)}, f32[8,256]{1,0:T(8,128)S(1)}, u32[]{:S(2)}, u32[]{:S(2)}) collective-permute-start(f32[8,256]{1,0:T(8,128)S(1)} %add.54), channel_id=1, source_target_pairs={{0,4},{1,5},{2,6},{3,7},{4,0},{5,1},{6,2},{7,3},{8,12},{9,13},{10,... | collective-permute-start | bytes 24584 | tf_op jit(solution)/shard_map/ppermute | solution.py:523

commit v10 on v9

--- a/solution.py
+++ b/solution.py
@@ -539,10 +539,10 @@
     for step in range(1, NEAR):
         if step & (step - 1) == 0:
             part = near_sum(part, "grid", ngrid, step, 2)
-    part = near_sum(part, "grid", ngrid, NEAR, NEAR)
+    part = near_sum(part, "grid", ngrid, NEAR * NEAR, ngrid // (NEAR * NEAR))
     totals = doubling_sum(total, "scen", nscen)
     arrived, part, totals = lax.optimization_barrier((arrived, part, totals))
-    regional = near_sum(part, "grid", ngrid, NEAR * NEAR, ngrid // (NEAR * NEAR))
+    regional = near_sum(part, "grid", ngrid, NEAR, NEAR)
     out, dual = line_call(True, arrived, state)
     received = exchange(out)
     dispatch, part, total, price = dispatch_call(True, received, (disp1, mism1, regional, totals))

time: 368 us -> 368 us (level)
  no operation moved by 1% of the time
where the time goes in v10:
time: 368 us; the launch traced here: 367 us
  waiting for transfers between devices  223 us (61%)
  starting transfers between devices  81.9 us (22%)
  blocking collectives  33.2 us (9%)
  Pallas kernels  21.2 us (6%)
  local copies, waits for them, and re-layouts  5.19 us (1%)
    all_to_all x4, waiting for transfers between devices, exchange(): return lax.all_to_all(x, 'grid', split_axis=0, concat_axis=0, tiled=True)  139 us
    ppermute x14, waiting for transfers between devices, near_sum(): lax.ppermute(x, axis, [(i, i ^ k * step) for i in range(size)])  81.1 us
    ppermute x14, starting transfers between devices, near_sum(): lax.ppermute(x, axis, [(i, i ^ k * step) for i in range(size)])  50.9 us
    all_to_all x1, blocking collectives, exchange(): return lax.all_to_all(x, 'grid', split_axis=0, concat_axis=0, tiled=True)  33.2 us
    all_to_all x4, starting transfers between devices, exchange(): return lax.all_to_all(x, 'grid', split_axis=0, concat_axis=0, tiled=True)  23.2 us
    pallas_call x2, Pallas kernels, line_call(): pl.pallas_call(functools.partial(line_kernel, second), out_shape=outs, in...  9.6 us
  transfers between devices with their start and end apart: 20, of which 11 were waited for; matrix products, arithmetic and copies ran while one was open for 0% of the time, Pallas kernels for 1%

profile of v10, /device:TPU:6, one launch (start us, length us, event | category | flops | bytes accessed | tf_op | source)
XLA Modules:
  0.0 367.2 jit_solution(2913974094128693484)
XLA Ops:
  1.3 1.1 plan.1
  2.4 33.2 %all_to_all.48 = s32[64,1,128]{2,1,0:T(1,128)S(1)} all-to-all(s32[64,1,128]{2,1,0:T(1,128)S(1)} %bitcast.33), channel_id=1, replica_groups=mesh['grid'=64,'scen'=8] {'grid'}, dimensions={0} | all-to-all | bytes 65536 | tf_op jit(solution)/shard_map/all_to_all | solution.py:425
  35.6 3.0 first_send.1
  38.6 4.7 %all-to-all-start.1 = ((f32[64,32,128]{2,1,0:T(8,128)}), f32[64,32,128]{2,1,0:T(8,128)S(1)}, u32[]{:S(2)}, u32[]{:S(2)}) async-start(f32[64,32,128]{2,1,0:T(8,128)} %first_send.1), calls=%async_computation.1 | async-start | bytes 2097152 | tf_op jit(solution)/shard_map/all_to_all | solution.py:425
  43.5 54.0 %all-to-all-done.1 = f32[64,32,128]{2,1,0:T(8,128)S(1)} async-done(((f32[64,32,128]{2,1,0:T(8,128)}), f32[64,32,128]{2,1,0:T(8,128)S(1)}, u32[]{:S(2)}, u32[]{:S(2)}) %all-to-all-start.1) | async-done | bytes 1048608 | tf_op jit(solution)/shard_map/all_to_all | solution.py:425
  97.5 4.6 %lines1.1 = (f32[3072,128]{1,0:T(8,128)}, f32[4,256,128]{2,1,0:T(8,128)}) custom-call(s32[1]{0:T(128)S(6)} %copy.39.count_ref, s32[1,512]{1,0:T(1,128)S(1)} %get-tuple-element.28.near_any, s32[1,512]{1,0:T(1,128)S(1)} %get-tuple-element.29.term_any, f32[2048,128]{1,0:T(8,128)S(1)} %bitcast.27, f32[4,256,128]{2,1,0:T(8,128)S(1)} %copy-done, ...), custom_call_target="tpu_custom_call" | custom-call | tf_op jit(solution)/shard_map/lines1/pallas_call | solution.py:476
  102.2 6.0 %all-to-all-start.2 = ((f32[64,48,128]{2,1,0:T(8,128)}), f32[64,48,128]{2,1,0:T(8,128)S(1)}, u32[]{:S(2)}, u32[]{:S(2)}) async-start(f32[64,48,128]{2,1,0:T(8,128)} %bitcast.37), calls=%async_computation.2 | async-start | bytes 3145728 | tf_op jit(solution)/shard_map/all_to_all | solution.py:425
  108.5 76.5 %all-to-all-done.2.recv_ref = f32[64,48,128]{2,1,0:T(8,128)S(1)} async-done(((f32[64,48,128]{2,1,0:T(8,128)}), f32[64,48,128]{2,1,0:T(8,128)S(1)}, u32[]{:S(2)}, u32[]{:S(2)}) %all-to-all-start.2) | async-done | bytes 1572896 | tf_op jit(solution)/shard_map/all_to_all | solution.py:425
  185.0 3.0 volt1.1
  188.0 5.8 %all-to-all-start.3 = ((f32[64,32,128]{2,1,0:T(8,128)}), f32[64,32,128]{2,1,0:T(8,128)S(1)}, u32[]{:S(2)}, u32[]{:S(2)}) async-start(f32[64,32,128]{2,1,0:T(8,128)} %get-tuple-element.31), calls=%async_computation.3 | async-start | bytes 2097152 | tf_op jit(solution)/shard_map/all_to_all | solution.py:425
  193.9 0.9 copy-done.2
  194.8 0.9 copy-done.4
  195.7 0.9 copy-done.6
  196.6 0.7 dispatch1.1
  197.3 0.7 copy-done.9
  198.0 0.7 copy-done.11
  198.6 1.9 collective-permute-start.5
  200.6 3.5 collective-permute-start
  204.1 2.7 collective-permute-start.6
  206.8 4.6 %collective-permute-start.1 = (f32[16,128]{1,0:T(8,128)S(1)}, f32[16,128]{1,0:T(8,128)S(1)}, u32[]{:S(2)}, u32[]{:S(2)}) collective-permute-start(f32[16,128]{1,0:T(8,128)S(1)} %add.42), channel_id=1, source_target_pairs={{0,16},{8,24},{16,0},{24,8},{32,48},{40,56},{48,32},{56,40},{64,80... | collective-permute-start | bytes 24584 | tf_op jit(solution)/shard_map/ppermute | solution.py:523
  211.5 3.0 collective-permute-start.7
  214.5 7.5 %collective-permute-start.4 = (f32[16,128]{1,0:T(8,128)S(1)}, f32[16,128]{1,0:T(8,128)S(1)}, u32[]{:S(2)}, u32[]{:S(2)}) collective-permute-start(f32[16,128]{1,0:T(8,128)S(1)} %add.43), channel_id=1, source_target_pairs={{0,384},{8,392},{16,400},{24,408},{32,416},{40,424},{48,432},{56,4... | collective-permute-start | bytes 24584 | tf_op jit(solution)/shard_map/ppermute | solution.py:523
  222.0 7.1 %collective-permute-start.3 = (f32[16,128]{1,0:T(8,128)S(1)}, f32[16,128]{1,0:T(8,128)S(1)}, u32[]{:S(2)}, u32[]{:S(2)}) collective-permute-start(f32[16,128]{1,0:T(8,128)S(1)} %add.43), channel_id=1, source_target_pairs={{0,256},{8,264},{16,272},{24,280},{32,288},{40,296},{48,304},{56,3... | collective-permute-start | bytes 24584 | tf_op jit(solution)/shard_map/ppermute | solution.py:523
  229.1 2.5 collective-permute-start.2
  231.6 7.9 %collective-permute-done.4 = f32[16,128]{1,0:T(8,128)S(1)} collective-permute-done((f32[16,128]{1,0:T(8,128)S(1)}, f32[16,128]{1,0:T(8,128)S(1)}, u32[]{:S(2)}, u32[]{:S(2)}) %collective-permute-start.4) | collective-permute-done | bytes 8224 | tf_op jit(solution)/shard_map/ppermute | solution.py:523
  239.5 9.2 %collective-permute-done.3 = f32[16,128]{1,0:T(8,128)S(1)} collective-permute-done((f32[16,128]{1,0:T(8,128)S(1)}, f32[16,128]{1,0:T(8,128)S(1)}, u32[]{:S(2)}, u32[]{:S(2)}) %collective-permute-start.3) | collective-permute-done | bytes 8224 | tf_op jit(solution)/shard_map/ppermute | solution.py:523
  248.7 5.0 %lines2.1 = (f32[3072,128]{1,0:T(8,128)}, f32[4,256,128]{2,1,0:T(8,128)}) custom-call(s32[1]{0:T(128)S(6)} %copy.39.count_ref, s32[1,512]{1,0:T(1,128)S(1)} %get-tuple-element.28.near_any, s32[1,512]{1,0:T(1,128)S(1)} %get-tuple-element.29.term_any, f32[2048,128]{1,0:T(8,128)S(1)} %bitcast.26, f32[4,256,128]{2,1,0:T(8,128)S(1)} %copy-done, ...), custom_call_target="tpu_custom_call" | custom-call | tf_op jit(solution)/shard_map/lines2/pallas_call | solution.py:476
  253.8 6.7 %all-to-all-start.4 = ((f32[64,48,128]{2,1,0:T(8,128)}), f32[64,48,128]{2,1,0:T(8,128)S(1)}, u32[]{:S(2)}, u32[]{:S(2)}) async-start(f32[64,48,128]{2,1,0:T(8,128)} %bitcast.36), calls=%async_computation.4 | async-start | bytes 3145728 | tf_op jit(solution)/shard_map/all_to_all | solution.py:425
  260.5 5.4 %collective-permute-start.10 = (f32[16,128]{1,0:T(8,128)S(1)}, f32[16,128]{1,0:T(8,128)S(1)}, u32[]{:S(2)}, u32[]{:S(2)}) collective-permute-start(f32[16,128]{1,0:T(8,128)S(1)} %add_add_fusion.1), channel_id=1, source_target_pairs={{0,96},{8,104},{16,112},{24,120},{32,64},{40,72},{48,80},{56,88},{... | collective-permute-start | bytes 24584 | tf_op jit(solution)/shard_map/ppermute | solution.py:523
  265.9 1.9 collective-permute-start.9
  267.8 2.9 collective-permute-start.8
  270.7 57.7 %collective-permute-done.10 = f32[16,128]{1,0:T(8,128)S(1)} collective-permute-done((f32[16,128]{1,0:T(8,128)S(1)}, f32[16,128]{1,0:T(8,128)S(1)}, u32[]{:S(2)}, u32[]{:S(2)}) %collective-permute-start.10) | collective-permute-done | bytes 8224 | tf_op jit(solution)/shard_map/ppermute | solution.py:523
  328.4 8.9 %all-to-all-done.4.recv_ref = f32[64,48,128]{2,1,0:T(8,128)S(1)} async-done(((f32[64,48,128]{2,1,0:T(8,128)}), f32[64,48,128]{2,1,0:T(8,128)S(1)}, u32[]{:S(2)}, u32[]{:S(2)}) %all-to-all-start.4) | async-done | bytes 1572896 | tf_op jit(solution)/shard_map/all_to_all | solution.py:425
  337.4 1.5 dispatch2.1
  338.8 4.2 %all-to-all-start.5 = ((f32[4,16,128]{2,1,0:T(8,128)}), f32[4,16,128]{2,1,0:T(8,128)S(1)}, u32[]{:S(2)}, u32[]{:S(2)}) async-start(f32[4,16,128]{2,1,0:T(8,128)} %bitcast.19), calls=%async_computation.5 | async-start | bytes 65536 | tf_op jit(solution)/shard_map/all_to_all | solution.py:551
  343.1 1.9 collective-permute-start.11
  345.0 1.1 collective-permute-done.11
  346.1 2.4 all-to-all-done.5
  348.5 0.7 broadcast_in_dim.2
  349.2 3.5 all-to-all-start.6
  352.7 2.7 collective-permute-start.12
  355.4 2.8 collective-permute-done.12
  358.3 3.3 collective-permute-start.13
  361.6 1.4 volt2.1
  362.9 2.4 collective-permute-done.13
  365.3 0.6 fusion
  365.9 0.4 all-to-all-done.6
  366.3 0.9 close.1
  (65 shorter events, 0.6 us)
Async XLA Ops:
  35.6 7.7 %copy-start.20 = (f32[256]{0:T(256)S(1)}, f32[256]{0:T(256)}, u32[]{:S(2)}) copy-start(f32[256]{0:T(256)} %param.20) | copy-start | bytes 3076
  35.6 7.7 %copy-start.21 = (f32[256]{0:T(256)S(1)}, f32[256]{0:T(256)}, u32[]{:S(2)}) copy-start(f32[256]{0:T(256)} %param.19) | copy-start | bytes 3076
  35.6 61.9 %copy-start = (f32[4,256,128]{2,1,0:T(8,128)S(1)}, f32[4,256,128]{2,1,0:T(8,128)}, u32[]{:S(2)}) copy-start(f32[4,256,128]{2,1,0:T(8,128)} %dual_ref.3) | copy-start | bytes 1572868
  38.6 58.8 %all-to-all-start.1 = ((f32[64,32,128]{2,1,0:T(8,128)}), f32[64,32,128]{2,1,0:T(8,128)S(1)}, u32[]{:S(2)}, u32[]{:S(2)}) async-start(f32[64,32,128]{2,1,0:T(8,128)} %first_send.1), calls=%async_computation.1 | async-start | bytes 2097152 | tf_op jit(solution)/shard_map/all_to_all | solution.py:425
  102.1 6.1 %copy-start.13 = (s32[256]{0:T(256)S(1)}, s32[256]{0:T(256)}, u32[]{:S(2)}) copy-start(s32[256]{0:T(256)} %param.24) | copy-start | bytes 3076
  102.1 6.1 %copy-start.14 = (f32[256]{0:T(256)S(1)}, f32[256]{0:T(256)}, u32[]{:S(2)}) copy-start(f32[256]{0:T(256)} %param.26) | copy-start | bytes 3076
  102.1 6.1 %copy-start.15 = (f32[256]{0:T(256)S(1)}, f32[256]{0:T(256)}, u32[]{:S(2)}) copy-start(f32[256]{0:T(256)} %param.25) | copy-start | bytes 3076
  102.1 6.1 %copy-start.16 = (f32[256]{0:T(256)S(1)}, f32[256]{0:T(256)}, u32[]{:S(2)}) copy-start(f32[256]{0:T(256)} %param.31) | copy-start | bytes 3076
  102.1 6.1 %copy-start.17 = (f32[256]{0:T(256)S(1)}, f32[256]{0:T(256)}, u32[]{:S(2)}) copy-start(f32[256]{0:T(256)} %param.32) | copy-start | bytes 3076
  102.1 6.1 %copy-start.18 = (f32[256]{0:T(256)S(1)}, f32[256]{0:T(256)}, u32[]{:S(2)}) copy-start(f32[256]{0:T(256)} %param.33) | copy-start | bytes 3076
  102.1 6.1 %copy-start.19 = (f32[256]{0:T(256)S(1)}, f32[256]{0:T(256)}, u32[]{:S(2)}) copy-start(f32[256]{0:T(256)} %param.30) | copy-start | bytes 3076
  102.1 82.9 %copy-start.1 = (f32[2,256,128]{2,1,0:T(8,128)S(1)}, f32[2,256,128]{2,1,0:T(8,128)}, u32[]{:S(2)}) copy-start(f32[2,256,128]{2,1,0:T(8,128)} %volt_ref.1) | copy-start | bytes 786436
  102.2 82.8 %all-to-all-start.2 = ((f32[64,48,128]{2,1,0:T(8,128)}), f32[64,48,128]{2,1,0:T(8,128)S(1)}, u32[]{:S(2)}, u32[]{:S(2)}) async-start(f32[64,48,128]{2,1,0:T(8,128)} %bitcast.37), calls=%async_computation.2 | async-start | bytes 3145728 | tf_op jit(solution)/shard_map/all_to_all | solution.py:425
  188.0 60.7 %all-to-all-start.3 = ((f32[64,32,128]{2,1,0:T(8,128)}), f32[64,32,128]{2,1,0:T(8,128)S(1)}, u32[]{:S(2)}, u32[]{:S(2)}) async-start(f32[64,32,128]{2,1,0:T(8,128)} %get-tuple-element.31), calls=%async_computation.3 | async-start | bytes 2097152 | tf_op jit(solution)/shard_map/all_to_all | solution.py:425
  193.9 0.9 copy-start.2
  194.8 0.9 copy-start.4
  195.7 0.9 copy-start.6
  197.3 0.7 copy-start.9
  198.0 0.7 copy-start.11
  198.6 5.4 %collective-permute-start.5 = (f32[8,256]{1,0:T(8,128)S(1)}, f32[8,256]{1,0:T(8,128)S(1)}, u32[]{:S(2)}, u32[]{:S(2)}) collective-permute-start(f32[8,256]{1,0:T(8,128)S(1)} %get-tuple-element.33), channel_id=1, source_target_pairs={{0,1},{1,0},{2,3},{3,2},{4,5},{5,4},{6,7},{7,6},{8,9},{9,8},{10,11... | collective-permute-start | bytes 24584 | tf_op jit(solution)/shard_map/ppermute | solution.py:523
  200.6 6.3 %collective-permute-start = (f32[16,128]{1,0:T(8,128)S(1)}, f32[16,128]{1,0:T(8,128)S(1)}, u32[]{:S(2)}, u32[]{:S(2)}) collective-permute-start(f32[16,128]{1,0:T(8,128)S(1)} %get-tuple-element.32), channel_id=1, source_target_pairs={{0,8},{8,0},{16,24},{24,16},{32,40},{40,32},{48,56},{56,48},{64,72... | collective-permute-start | bytes 24584 | tf_op jit(solution)/shard_map/ppermute | solution.py:523
  204.1 7.4 %collective-permute-start.6 = (f32[8,256]{1,0:T(8,128)S(1)}, f32[8,256]{1,0:T(8,128)S(1)}, u32[]{:S(2)}, u32[]{:S(2)}) collective-permute-start(f32[8,256]{1,0:T(8,128)S(1)} %add.47), channel_id=1, source_target_pairs={{0,2},{1,3},{2,0},{3,1},{4,6},{5,7},{6,4},{7,5},{8,10},{9,11},{10,... | collective-permute-start | bytes 24584 | tf_op jit(solution)/shard_map/ppermute | solution.py:523
  206.8 7.6 %collective-permute-start.1 = (f32[16,128]{1,0:T(8,128)S(1)}, f32[16,128]{1,0:T(8,128)S(1)}, u32[]{:S(2)}, u32[]{:S(2)}) collective-permute-start(f32[16,128]{1,0:T(8,128)S(1)} %add.42), channel_id=1, source_target_pairs={{0,16},{8,24},{16,0},{24,8},{32,48},{40,56},{48,32},{56,40},{64,80... | collective-permute-start | bytes 24584 | tf_op jit(solution)/shard_map/ppermute | solution.py:523
  211.5 20.1 %collective-permute-start.7 = (f32[8,256]{1,0:T(8,128)S(1)}, f32[8,256]{1,0:T(8,128)S(1)}, u32[]{:S(2)}, u32[]{:S(2)}) collective-permute-start(f32[8,256]{1,0:T(8,128)S(1)} %add.48), channel_id=1, source_target_pairs={{0,4},{1,5},{2,6},{3,7},{4,0},{5,1},{6,2},{7,3},{8,12},{9,13},{10,... | collective-permute-start | bytes 24584 | tf_op jit(solution)/shard_map/ppermute | solution.py:523
  214.5 25.0 %collective-permute-start.4 = (f32[16,128]{1,0:T(8,128)S(1)}, f32[16,128]{1,0:T(8,128)S(1)}, u32[]{:S(2)}, u32[]{:S(2)}) collective-permute-start(f32[16,128]{1,0:T(8,128)S(1)} %add.43), channel_id=1, source_target_pairs={{0,384},{8,392},{16,400},{24,408},{32,416},{40,424},{48,432},{56,4... | collective-permute-start | bytes 24584 | tf_op jit(solution)/shard_map/ppermute | solution.py:523
  222.0 26.7 %collective-permute-start.3 = (f32[16,128]{1,0:T(8,128)S(1)}, f32[16,128]{1,0:T(8,128)S(1)}, u32[]{:S(2)}, u32[]{:S(2)}) collective-permute-start(f32[16,128]{1,0:T(8,128)S(1)} %add.43), channel_id=1, source_target_pairs={{0,256},{8,264},{16,272},{24,280},{32,288},{40,296},{48,304},{56,3... | collective-permute-start | bytes 24584 | tf_op jit(solution)/shard_map/ppermute | solution.py:523
  229.1 19.6 %collective-permute-start.2 = (f32[16,128]{1,0:T(8,128)S(1)}, f32[16,128]{1,0:T(8,128)S(1)}, u32[]{:S(2)}, u32[]{:S(2)}) collective-permute-start(f32[16,128]{1,0:T(8,128)S(1)} %add.43), channel_id=1, source_target_pairs={{0,128},{8,136},{16,144},{24,152},{32,160},{40,168},{48,176},{56,1... | collective-permute-start | bytes 24584 | tf_op jit(solution)/shard_map/ppermute | solution.py:523
  253.7 83.6 %copy-start.3 = (f32[256,128]{1,0:T(8,128)S(1)}, f32[256,128]{1,0:T(8,128)}, u32[]{:S(2)}) copy-start(f32[256,128]{1,0:T(8,128)} %load_ref.3) | copy-start | bytes 393220
  253.7 83.6 %copy-start.5 = (f32[256,128]{1,0:T(8,128)S(1)}, f32[256,128]{1,0:T(8,128)}, u32[]{:S(2)}) copy-start(f32[256,128]{1,0:T(8,128)} %price_ref.3) | copy-start | bytes 393220
  253.7 83.6 %copy-start.7 = (f32[256,128]{1,0:T(8,128)S(1)}, f32[256,128]{1,0:T(8,128)}, u32[]{:S(2)}) copy-start(f32[256,128]{1,0:T(8,128)} %nadual_ref.3) | copy-start | bytes 393220
  253.8 83.6 %copy-start.10 = (f32[256,128]{1,0:T(8,128)S(1)}, f32[256,128]{1,0:T(8,128)}, u32[]{:S(2)}) copy-start(f32[256,128]{1,0:T(8,128)} %copy-done.9) | copy-start | bytes 393220
  253.8 83.6 %copy-start.12 = (f32[256,128]{1,0:T(8,128)S(1)}, f32[256,128]{1,0:T(8,128)}, u32[]{:S(2)}) copy-start(f32[256,128]{1,0:T(8,128)} %copy-done.11) | copy-start | bytes 393220
  253.8 83.6 %all-to-all-start.4 = ((f32[64,48,128]{2,1,0:T(8,128)}), f32[64,48,128]{2,1,0:T(8,128)S(1)}, u32[]{:S(2)}, u32[]{:S(2)}) async-start(f32[64,48,128]{2,1,0:T(8,128)} %bitcast.36), calls=%async_computation.4 | async-start | bytes 3145728 | tf_op jit(solution)/shard_map/all_to_all | solution.py:425
  260.5 101.1 %copy-start.8 = (f32[2,256,128]{2,1,0:T(8,128)S(1)}, f32[2,256,128]{2,1,0:T(8,128)}, u32[]{:S(2)}) copy-start(f32[2,256,128]{2,1,0:T(8,128)} %get-tuple-element.37.volt_ref) | copy-start | bytes 786436
  260.5 68.0 %collective-permute-start.10 = (f32[16,128]{1,0:T(8,128)S(1)}, f32[16,128]{1,0:T(8,128)S(1)}, u32[]{:S(2)}, u32[]{:S(2)}) collective-permute-start(f32[16,128]{1,0:T(8,128)S(1)} %add_add_fusion.1), channel_id=1, source_target_pairs={{0,96},{8,104},{16,112},{24,120},{32,64},{40,72},{48,80},{56,88},{... | collective-permute-start | bytes 24584 | tf_op jit(solution)/shard_map/ppermute | solution.py:523
  265.9 62.5 %collective-permute-start.9 = (f32[16,128]{1,0:T(8,128)S(1)}, f32[16,128]{1,0:T(8,128)S(1)}, u32[]{:S(2)}, u32[]{:S(2)}) collective-permute-start(f32[16,128]{1,0:T(8,128)S(1)} %add_add_fusion.1), channel_id=1, source_target_pairs={{0,64},{8,72},{16,80},{24,88},{32,96},{40,104},{48,112},{56,120},{... | collective-permute-start | bytes 24584 | tf_op jit(solution)/shard_map/ppermute | solution.py:523
  267.8 60.6 %collective-permute-start.8 = (f32[16,128]{1,0:T(8,128)S(1)}, f32[16,128]{1,0:T(8,128)S(1)}, u32[]{:S(2)}, u32[]{:S(2)}) collective-permute-start(f32[16,128]{1,0:T(8,128)S(1)} %add_add_fusion.1), channel_id=1, source_target_pairs={{0,32},{8,40},{16,48},{24,56},{32,0},{40,8},{48,16},{56,24},{64,96... | collective-permute-start | bytes 24584 | tf_op jit(solution)/shard_map/ppermute | solution.py:523
  338.8 9.7 %all-to-all-start.5 = ((f32[4,16,128]{2,1,0:T(8,128)}), f32[4,16,128]{2,1,0:T(8,128)S(1)}, u32[]{:S(2)}, u32[]{:S(2)}) async-start(f32[4,16,128]{2,1,0:T(8,128)} %bitcast.19), calls=%async_computation.5 | async-start | bytes 65536 | tf_op jit(solution)/shard_map/all_to_all | solution.py:551
  343.1 3.1 collective-permute-start.11
  349.2 17.1 %all-to-all-start.6 = ((f32[16,16,128]{2,1,0:T(8,128)}), f32[16,16,128]{2,1,0:T(8,128)S(1)}, u32[]{:S(2)}, u32[]{:S(2)}) async-start(f32[16,16,128]{2,1,0:T(8,128)} %broadcast_in_dim.2), calls=%async_computation.6 | async-start | bytes 262144 | tf_op jit(solution)/shard_map/all_to_all | solution.py:556
  352.7 5.5 %collective-permute-start.12 = (f32[8,256]{1,0:T(8,128)S(1)}, f32[8,256]{1,0:T(8,128)S(1)}, u32[]{:S(2)}, u32[]{:S(2)}) collective-permute-start(f32[8,256]{1,0:T(8,128)S(1)} %add.53), channel_id=1, source_target_pairs={{0,2},{1,3},{2,0},{3,1},{4,6},{5,7},{6,4},{7,5},{8,10},{9,11},{10,... | collective-permute-start | bytes 24584 | tf_op jit(solution)/shard_map/ppermute | solution.py:523
  358.3 7.0 %collective-permute-start.13 = (f32[8,256]{1,0:T(8,128)S(1)}, f32[8,256]{1,0:T(8,128)S(1)}, u32[]{:S(2)}, u32[]{:S(2)}) collective-permute-start(f32[8,256]{1,0:T(8,128)S(1)} %add.54), channel_id=1, source_target_pairs={{0,4},{1,5},{2,6},{3,7},{4,0},{5,1},{6,2},{7,3},{8,12},{9,13},{10,... | collective-permute-start | bytes 24584 | tf_op jit(solution)/shard_map/ppermute | solution.py:523
